TPU v7x, 32 devices: a whole 2x2x4 slice. The times are simulated.
32 devices in a mesh: grp: 2 (over x), dp: 8 (over z, y), tp: 2 (over core).
Axes of the slice: x: 2, y: 2, z: 4, core: 2. Of those that a mesh axis runs over, the one named last changes fastest.
Arguments:
- frames: bfloat16 [2, 16, 128, 1280], P('grp', ('dp', 'tp')), may hold values from -12 to 12
- counts: int32 [16], P('dp'), may hold values from 0 to 1, as said below
- w_qkv: bfloat16 [2, 1280, 3840], P('grp'), may hold values from -0.18727069 to 0.18727069
- ln_gain: bfloat16 [2, 1280], P('grp'), may hold values from 0.5 to 1.5
- w_proj: bfloat16 [2, 5120, 8192], P('grp', 'dp', 'tp'), may hold values from -1.5931984 to 1.5931984
- rms_gain: bfloat16 [2, 8192], P('grp', 'tp'), may hold values from 0.5 to 1.5
- cotangent: bfloat16 [2, 512, 8192], P('grp', 'dp', 'tp'), may hold values from -6 to 6
Outputs:
- frame_grad: bfloat16 [2, 16, 128, 1280], P('grp', ('dp', 'tp'))
Inputs may be any that keep to these rules, and one draw needn't show every extreme that they name: `counts`: some encoder device has all 1 frames live.
All inputs are finite; a program needn't handle non-finite values.
Results may differ from a plain program's by a relative error of at most 0.025.
Values may be sent and summed in bfloat16 or wider, within the bound.
No kernel may reach another device: no remote copies, remote signals or barrier semaphores. Data moves between devices by JAX's collectives and lax.ppermute only.
A program may use at most 128 MiB of HBM per device.

v0:
```python
import jax
import jax.numpy as jnp
from jax import lax
from jax.sharding import PartitionSpec as P

HEADS = 16
HDIM = 80
D = 8192


def passed_along(block, axis, distance):
    devices = range(lax.axis_size(axis))
    route = [(i - distance, i) for i in devices if i - distance in devices]
    return lax.ppermute(block, axis, route)


def encoder_forward(frames, w_qkv, ln_gain):
    frame_count = frames.shape[0]
    length = frames.shape[1]
    vis_width = frames.shape[2]
    mixed_qkv = jnp.einsum("fpe,ec->fpc", frames, w_qkv, preferred_element_type=jnp.float32).astype(
        jnp.bfloat16
    )
    split_heads = mixed_qkv.reshape(frame_count, length, 3, HEADS, HDIM)
    scores = jnp.einsum(
        "fqhd,fkhd->fhqk",
        split_heads[:, :, 0],
        split_heads[:, :, 1],
        preferred_element_type=jnp.float32,
    ) * HDIM ** (-0.5)
    attn_probs = jax.nn.softmax(scores, axis=-1)
    weights = attn_probs.astype(jnp.bfloat16)
    attended = jnp.einsum(
        "fhqk,fkhd->fqhd", weights, split_heads[:, :, 2], preferred_element_type=jnp.float32
    )
    summed = frames.astype(jnp.float32) + attended.reshape(frame_count, length, vis_width)
    centred = summed - jnp.mean(summed, axis=-1, keepdims=True)
    inverse = lax.rsqrt(jnp.mean(centred * centred, axis=-1, keepdims=True) + 1e-06)
    normal_part = centred * inverse
    embedded = (normal_part * ln_gain.astype(jnp.float32)).astype(jnp.bfloat16)
    return (
        embedded.reshape(frame_count * length // 4, 4 * vis_width),
        mixed_qkv,
        attn_probs,
        normal_part,
        inverse,
    )


def encoder_backward(w_qkv, ln_gain, mixed_qkv, attn_probs, normal_part, inverse, grad_embed):
    frame_count = normal_part.shape[0]
    length = normal_part.shape[1]
    vis_width = normal_part.shape[2]
    split_heads = mixed_qkv.reshape(frame_count, length, 3, HEADS, HDIM)
    query_heads = split_heads[:, :, 0]
    key_heads = split_heads[:, :, 1]
    value_heads = split_heads[:, :, 2]
    weights = attn_probs.astype(jnp.bfloat16)
    grad_norm = grad_embed.reshape(frame_count, length, vis_width).astype(
        jnp.float32
    ) * ln_gain.astype(jnp.float32)
    grad_summed = inverse * (
        grad_norm
        - jnp.mean(grad_norm, axis=-1, keepdims=True)
        - normal_part * jnp.mean(grad_norm * normal_part, axis=-1, keepdims=True)
    )
    grad_heads = grad_summed.astype(jnp.bfloat16).reshape(frame_count, length, HEADS, HDIM)
    grad_weights = jnp.einsum(
        "fqhd,fkhd->fhqk", grad_heads, value_heads, preferred_element_type=jnp.float32
    )
    grad_values = jnp.einsum(
        "fhqk,fqhd->fkhd", weights, grad_heads, preferred_element_type=jnp.float32
    ).astype(jnp.bfloat16)
    grad_scores = (
        attn_probs
        * (grad_weights - jnp.sum(grad_weights * attn_probs, axis=-1, keepdims=True))
        * HDIM ** (-0.5)
    ).astype(jnp.bfloat16)
    grad_query = jnp.einsum(
        "fhqk,fkhd->fqhd", grad_scores, key_heads, preferred_element_type=jnp.float32
    ).astype(jnp.bfloat16)
    grad_keys = jnp.einsum(
        "fhqk,fqhd->fkhd", grad_scores, query_heads, preferred_element_type=jnp.float32
    ).astype(jnp.bfloat16)
    grad_mixed = jnp.stack([grad_query, grad_keys, grad_values], axis=2).reshape(
        frame_count, length, 3 * vis_width
    )
    through = jnp.einsum("fpc,ec->fpe", grad_mixed, w_qkv, preferred_element_type=jnp.float32)
    return (grad_summed + through).astype(jnp.bfloat16)


def per_device(frames, counts, w_qkv, ln_gain, w_proj, rms_gain, cotangent):
    is_encoder = lax.axis_index("grp") == 0
    local_frames = frames[0]
    weight_mix = w_qkv[0]
    gain_ln = ln_gain[0]
    frame_count = local_frames.shape[0]
    length = local_frames.shape[1]
    vis_width = local_frames.shape[2]
    merged_width = 4 * vis_width
    tokens_frame = length // 4
    tokens_here = frame_count * tokens_frame

    def run_encoder():
        return encoder_forward(local_frames, weight_mix, gain_ln)

    def skip_encoder():
        return (
            jnp.zeros((tokens_here, merged_width), jnp.bfloat16),
            jnp.zeros((frame_count, length, 3 * vis_width), jnp.bfloat16),
            jnp.zeros((frame_count, HEADS, length, length), jnp.float32),
            jnp.zeros((frame_count, length, vis_width), jnp.float32),
            jnp.zeros((frame_count, length, 1), jnp.float32),
        )

    embedded, mixed_qkv, attn_probs, normal_part, inverse = lax.cond(
        is_encoder, run_encoder, skip_encoder
    )
    arrived = passed_along(embedded, "grp", 1)
    pooled = lax.all_gather(arrived, "tp", axis=0, tiled=True)
    full_proj = lax.all_gather(w_proj[0], "dp", axis=0, tiled=True)
    row_count = pooled.shape[0]
    col_count = full_proj.shape[1]
    activations = lax.cond(
        is_encoder,
        lambda: jnp.zeros((row_count, col_count), jnp.float32),
        lambda: jnp.dot(pooled, full_proj, preferred_element_type=jnp.float32),
    )
    tp_count = lax.axis_size("tp")
    position = lax.broadcasted_iota(jnp.int32, (row_count,), 0)
    source = position // tokens_here
    slot_index = position // tokens_frame % frame_count
    owner_hits = source[:, None] == lax.broadcasted_iota(jnp.int32, (1, tp_count), 1)
    live_limit = jnp.sum(jnp.where(owner_hits, counts[None, :], 0), axis=1)
    live_mask = (slot_index < live_limit).astype(jnp.float32)
    scaled = (
        rms_gain[0].astype(jnp.float32)[None, :]
        * cotangent[0].astype(jnp.float32)
        * live_mask[:, None]
    )
    squares = jnp.sum(activations * activations, axis=1)
    products = jnp.sum(activations * scaled, axis=1)
    total_sq, total_prod = lax.psum((squares, products), "tp")
    inverse_rms = lax.rsqrt(total_sq / D + 1e-06)[:, None]
    product = (total_prod / D)[:, None]
    grad_acts = (inverse_rms * scaled - activations * inverse_rms**3 * product).astype(jnp.bfloat16)
    term_rows = lax.cond(
        is_encoder,
        lambda: jnp.zeros((row_count, merged_width), jnp.bfloat16),
        lambda: lax.dot_general(
            grad_acts, full_proj, (((1,), (1,)), ((), ())), preferred_element_type=jnp.float32
        ).astype(jnp.bfloat16),
    )
    rounded_terms = lax.optimization_barrier(term_rows)
    summed_rows = lax.psum_scatter(
        rounded_terms.astype(jnp.float32).astype(jnp.bfloat16),
        "tp",
        scatter_dimension=0,
        tiled=True,
    )
    returned = passed_along(summed_rows, "grp", -1)
    grad_frames = lax.cond(
        is_encoder,
        lambda: encoder_backward(
            weight_mix, gain_ln, mixed_qkv, attn_probs, normal_part, inverse, returned
        ),
        lambda: jnp.zeros(local_frames.shape, jnp.bfloat16),
    )
    return grad_frames[None]


def solution(mesh):
    placed = (
        P("grp", ("dp", "tp"), None, None),
        P("dp"),
        P("grp", None, None),
        P("grp", None),
        P("grp", "dp", "tp"),
        P("grp", "tp"),
        P("grp", "dp", "tp"),
    )
    return jax.shard_map(
        per_device,
        mesh=mesh,
        in_specs=placed,
        out_specs=P("grp", ("dp", "tp"), None, None),
        check_vma=False,
    )
```

profile of v0, /device:TPU:0, one launch (start us, length us, event | category | flops | bytes accessed | tf_op | source)
XLA Modules:
  0.0 887.2 jit_solution(567608343134886291)
XLA Ops:
  6.5 0.7 all-gather.3.cloned.1.call-update
  7.3 0.7 reduce.10
  8.0 19.9 %conditional.4 = (bf16[32,5120]{1,0:T(8,128)(2,1)}, bf16[1,128,3840]{2,1,0:T(8,128)(2,1)}, f32[1,16,128,128]{2,3,1,0:T(8,128)S(1)}, f32[1,128,1280]{2,1,0:T(8,128)S(1)}, f32[1,128,1]{1,2,0:T(1,128)S(1)}) conditional(s32[]{:T(128)} %convert_element_type.147, () %tuple.34, (bf16[1,1,128,1280]{3,2,1,0:T(8,128)(2,1)}, bf16[1280,3840]{1,0:T(8,128)(2,1)}, ...), branch_computations={%region_0.0_spmd, %region_1.0_spmd} | conditional | flops 1389332864 | bytes 39174724 | solution.py:116
  8.1 6.4 convolution_convert_fusion
  14.5 1.6 copy.33
  16.1 1.5 fusion.32
  17.6 1.4 convolution_multiply_fusion
  19.1 2.2 add_reduce_fusion
  22.3 1.0 sub.63
  23.4 0.5 copy.35
  23.9 0.6 reshape.363
  24.7 1.9 multiply_convert_fusion
  26.6 1.3 fusion.6
  28.0 1.3 collective-permute-start
  29.4 8.0 collective-permute-done
  37.4 2.3 all_gather.6
  39.7 767.0 %all-gather.3.cloned.1.call-done = bf16[1,5120,4096]{2,1,0:T(8,128)(2,1)} async-done(((bf16[1,640,4096]{2,1,0:T(8,128)(2,1)}), bf16[1,5120,4096]{2,1,0:T(8,128)(2,1)}) %all-gather.3.cloned.1.call-update) | async-done | bytes 41943056 | tf_op jit(solution)/shard_map/all_gather | solution.py:121
  806.7 1.4 multiply_reduce_fusion.3
  808.1 2.5 all-reduce
  810.6 1.4 fusion.29
  812.2 0.8 copy-done.2
  813.1 43.7 %reduce-scatter.2.cloned.1.call-done = bf16[32,5120]{1,0:T(8,128)(2,1)} async-done(((bf16[64,5120]{1,0:T(8,128)(2,1)}), bf16[32,5120]{1,0:T(8,128)(2,1)}) %reduce-scatter.2.cloned.1.call-update) | async-done | bytes 327696 | tf_op jit(solution)/shard_map/reduce_scatter | solution.py:155
  856.8 1.3 collective-permute-start.1
  858.1 10.6 %collective-permute-done.1 = bf16[32,5120]{1,0:T(8,128)(2,1)S(1)} collective-permute-done((bf16[32,5120]{1,0:T(8,128)(2,1)}, bf16[32,5120]{1,0:T(8,128)(2,1)S(1)}, u32[]{:S(2)}, u32[]{:S(2)}) %collective-permute-start.1) | collective-permute-done | bytes 327712 | tf_op jit(solution)/shard_map/ppermute | solution.py:14
  868.6 11.7 %conditional.7 = (bf16[1,1,128,1280]{3,2,1,0:T(8,128)(2,1)}) conditional(s32[]{:T(128)} %convert_element_type.147, () %tuple.33, (f32[1,128,1]{1,2,0:T(1,128)S(1)}, bf16[32,5120]{1,0:T(8,128)(2,1)S(1)}, bf16[1280]{0:T(1024)(128)(2,1)S(1)}, f32[1,128,1280]{2,1,0:T(8,128)S(1)}, bf16[1,128,3840]{2,1,0:T(8,128)(2,1)}, ...), branch_computations={%region_16.17_spmd, %region_17.21_spmd} | conditional | flops 1432157440 | bytes 69775912 | solution.py:162
  869.2 0.9 copy.38
  870.1 1.6 copy.42
  871.7 1.5 fusion.19
  873.4 0.3 fusion.16
  873.8 0.5 fusion.14
  874.3 1.8 fusion.15
  876.2 4.1 fusion.13
  (40 shorter events, 2.9 us)
Async XLA Ops:
  6.5 800.1 %all-gather.3.cloned.1.call-start = ((), (), s32[]{:S(2)}) async-start(), calls=%async_computation.2 | async-start | bytes 47185920 | tf_op jit(solution)/shard_map/all_gather | solution.py:121
  7.3 849.5 %reduce-scatter.2.cloned.1.call-start = ((), (), s32[]{:S(2)}) async-start(), calls=%async_computation.1 | async-start | bytes 983040 | tf_op jit(solution)/shard_map/reduce_scatter | solution.py:155
  8.0 21.2 %copy-start.3 = (bf16[1,4096]{1,0:T(2,128)(2,1)S(1)}, bf16[1,4096]{1,0:T(2,128)(2,1)}, u32[]{:S(2)}) copy-start(bf16[1,4096]{1,0:T(2,128)(2,1)} %param.20) | copy-start | bytes 24580
  8.0 21.3 %copy-start.4 = (s32[2]{0:T(128)S(1)}, s32[2]{0:T(128)}, u32[]{:S(2)}) copy-start(s32[2]{0:T(128)} %param.16) | copy-start | bytes 28
  8.1 10.9 %copy-start.1 = (bf16[1,1,128,1280]{3,2,1,0:T(8,128)(2,1)S(1)}, bf16[1,1,128,1280]{3,2,1,0:T(8,128)(2,1)}, u32[]{:S(2)}) copy-start(bf16[1,1,128,1280]{3,2,1,0:T(8,128)(2,1)} %get-tuple-element.69) | copy-start | bytes 983044 | tf_op jit(solution)/shard_map/cond
  28.0 9.5 %collective-permute-start = (bf16[32,5120]{1,0:T(8,128)(2,1)}, bf16[32,5120]{1,0:T(8,128)(2,1)S(1)}, u32[]{:S(2)}, u32[]{:S(2)}) collective-permute-start(bf16[32,5120]{1,0:T(8,128)(2,1)} %get-tuple-element.64), channel_id=1, source_target_pairs={{0,16},{1,17},{2,18},{3,19},{4,20},{5,21},{6,22},{7,23},{8,24},{9,... | collective-permute-start | bytes 983048 | tf_op jit(solution)/shard_map/ppermute | solution.py:14
  812.2 0.8 copy-start.2
  856.8 11.9 %collective-permute-start.1 = (bf16[32,5120]{1,0:T(8,128)(2,1)}, bf16[32,5120]{1,0:T(8,128)(2,1)S(1)}, u32[]{:S(2)}, u32[]{:S(2)}) collective-permute-start(bf16[32,5120]{1,0:T(8,128)(2,1)} %reduce-scatter.2.cloned.1.call-done), channel_id=1, source_target_pairs={{16,0},{17,1},{18,2},{19,3},{20,4},{21,5},{22,6},{23,7},{24,8},{25... | collective-permute-start | bytes 983048 | tf_op jit(solution)/shard_map/ppermute | solution.py:14
  871.7 4.5 copy-start
Sparse Core Ops, SparseCore 0:
  8.9 797.7 all-gather.2
  813.2 43.5 reduce-scatter.1
where the time goes:
time: 888 us; the launch traced here: 887 us
  waiting for transfers between devices  830 us (93%)
  matrix products  19.7 us (2%)
  between operations  13.5 us (2%)
    all_gather x1, waiting for transfers between devices, per_device(): full_proj = lax.all_gather(w_proj[0], 'dp', axis=0, tiled=True)  767 us
    reduce_scatter x1, waiting for transfers between devices, per_device(): lax.psum_scatter(rounded_terms.astype(jnp.float32).astype(jnp.bfloat16),...  43.7 us
    ppermute x2, waiting for transfers between devices, passed_along(): return lax.ppermute(block, axis, route)  18.6 us
  transfers between devices with their start and end apart: 4, of which 4 were waited for; matrix products, arithmetic and copies ran while one was open for 2% of the time, Pallas kernels for 0%

commit v1 on v0

--- a/solution.py
+++ b/solution.py
@@ -89,82 +89,155 @@
     return (grad_summed + through).astype(jnp.bfloat16)
 
 
+def rotated(blocks, shift):
+    count = blocks.shape[0]
+    step = 1
+    while step < count:
+        turned = jnp.concatenate([blocks[step:], blocks[:step]], axis=0)
+        blocks = jnp.where((shift // step) % 2 == 1, turned, blocks)
+        step *= 2
+    return blocks
+
+
+def flipped(pairs, odd):
+    return jnp.where(odd == 1, pairs[:, ::-1], pairs)
+
+
+def sent_round(block, distance):
+    count = lax.axis_size("dp")
+    return lax.ppermute(block, "dp", [(i, (i + 2 * distance) % count) for i in range(count)])
+
+
+def sent_across(block):
+    return lax.ppermute(block, "dp", [(i, i ^ 1) for i in range(lax.axis_size("dp"))])
+
+
 def per_device(frames, counts, w_qkv, ln_gain, w_proj, rms_gain, cotangent):
+    f32, bf16 = jnp.float32, jnp.bfloat16
     is_encoder = lax.axis_index("grp") == 0
+    dp_count, tp_count = lax.axis_size("dp"), lax.axis_size("tp")
+    pair_count = dp_count // 2
+    dp_index, tp_index = lax.axis_index("dp"), lax.axis_index("tp")
+    pair, odd = dp_index // 2, dp_index % 2
+
     local_frames = frames[0]
     weight_mix = w_qkv[0]
     gain_ln = ln_gain[0]
-    frame_count = local_frames.shape[0]
-    length = local_frames.shape[1]
-    vis_width = local_frames.shape[2]
+    frame_count, length, vis_width = local_frames.shape
     merged_width = 4 * vis_width
     tokens_frame = length // 4
     tokens_here = frame_count * tokens_frame
+    rows = tokens_here * tp_count
+    depth = w_proj.shape[1]
+    half = w_proj.shape[2] // 2
+    first = half * 11 // 16 // 128 * 128
+    second = half - first
+
+    w_mine = w_proj[0]
+    got_first = passed_along(w_mine[:, :first], "grp", -1)
+    got_second = passed_along(w_mine[:, first:half], "grp", -1)
+    got_cot = passed_along(cotangent[0][:, :half], "grp", -1)
+    got_gain = passed_along(rms_gain[:, :half], "grp", -1)
+    w_first = jnp.where(is_encoder, got_first, w_mine[:, half : half + first])
+    w_second = jnp.where(is_encoder, got_second, w_mine[:, half + first :])
+    cot = jnp.where(is_encoder, got_cot, cotangent[0][:, half:])
+    gain_rms = jnp.where(is_encoder, got_gain, rms_gain[:, half:])[0]
 
     def run_encoder():
         return encoder_forward(local_frames, weight_mix, gain_ln)
 
     def skip_encoder():
         return (
-            jnp.zeros((tokens_here, merged_width), jnp.bfloat16),
-            jnp.zeros((frame_count, length, 3 * vis_width), jnp.bfloat16),
-            jnp.zeros((frame_count, HEADS, length, length), jnp.float32),
-            jnp.zeros((frame_count, length, vis_width), jnp.float32),
-            jnp.zeros((frame_count, length, 1), jnp.float32),
+            jnp.zeros((tokens_here, merged_width), bf16),
+            jnp.zeros((frame_count, length, 3 * vis_width), bf16),
+            jnp.zeros((frame_count, HEADS, length, length), f32),
+            jnp.zeros((frame_count, length, vis_width), f32),
+            jnp.zeros((frame_count, length, 1), f32),
         )
 
     embedded, mixed_qkv, attn_probs, normal_part, inverse = lax.cond(
         is_encoder, run_encoder, skip_encoder
     )
-    arrived = passed_along(embedded, "grp", 1)
-    pooled = lax.all_gather(arrived, "tp", axis=0, tiled=True)
-    full_proj = lax.all_gather(w_proj[0], "dp", axis=0, tiled=True)
-    row_count = pooled.shape[0]
-    col_count = full_proj.shape[1]
-    activations = lax.cond(
-        is_encoder,
-        lambda: jnp.zeros((row_count, col_count), jnp.float32),
-        lambda: jnp.dot(pooled, full_proj, preferred_element_type=jnp.float32),
-    )
-    tp_count = lax.axis_size("tp")
-    position = lax.broadcasted_iota(jnp.int32, (row_count,), 0)
+
+    pieces = embedded.reshape(tokens_here, dp_count, depth).transpose(1, 0, 2)
+    swapped = lax.all_to_all(pieces, "dp", 0, 0)
+    arrived = passed_along(swapped, "grp", 1)
+    features = jnp.where(is_encoder, swapped, arrived)
+    features = lax.all_gather(features, "tp", axis=1)
+    features = features.reshape(pair_count, 2, rows, depth)
+    features = flipped(rotated(features, pair), odd)
+
+    def product(block, weight):
+        return jnp.einsum("...rk,kc->...rc", block, weight, preferred_element_type=f32)
+
+    away = product(features[:, 1], w_first).astype(bf16)
+    away = sent_across(away)
+    home = product(features[:, 0], w_first) + away.astype(f32)
+    home_sent = home.astype(bf16)
+    parts = [sent_round(home_sent[s], s) for s in range(1, pair_count)]
+    acts_first = home[0]
+    around = [
+        sent_round(product(features[s], w_second).astype(bf16), s) for s in range(1, pair_count)
+    ]
+    both = product(features[0], w_second)
+    for block in around:
+        both = both + block.astype(f32)
+    other = sent_across(both[1].astype(bf16))
+    acts_second = both[0] + other.astype(f32)
+    for block in parts:
+        acts_first = acts_first + block.astype(f32)
+
+    position = lax.broadcasted_iota(jnp.int32, (rows,), 0)
     source = position // tokens_here
     slot_index = position // tokens_frame % frame_count
     owner_hits = source[:, None] == lax.broadcasted_iota(jnp.int32, (1, tp_count), 1)
     live_limit = jnp.sum(jnp.where(owner_hits, counts[None, :], 0), axis=1)
-    live_mask = (slot_index < live_limit).astype(jnp.float32)
-    scaled = (
-        rms_gain[0].astype(jnp.float32)[None, :]
-        * cotangent[0].astype(jnp.float32)
-        * live_mask[:, None]
-    )
-    squares = jnp.sum(activations * activations, axis=1)
-    products = jnp.sum(activations * scaled, axis=1)
-    total_sq, total_prod = lax.psum((squares, products), "tp")
+    live_mask = (slot_index < live_limit).astype(f32)
+    scaled = gain_rms.astype(f32)[None, :] * cot.astype(f32) * live_mask[:, None]
+    scaled_first, scaled_second = scaled[:, :first], scaled[:, first:]
+    squares = jnp.sum(acts_first * acts_first, axis=1) + jnp.sum(acts_second * acts_second, axis=1)
+    products = jnp.sum(acts_first * scaled_first, axis=1) + jnp.sum(
+        acts_second * scaled_second, axis=1
+    )
+    total_sq, total_prod = lax.psum((squares, products), ("grp", "tp"))
     inverse_rms = lax.rsqrt(total_sq / D + 1e-06)[:, None]
-    product = (total_prod / D)[:, None]
-    grad_acts = (inverse_rms * scaled - activations * inverse_rms**3 * product).astype(jnp.bfloat16)
-    term_rows = lax.cond(
-        is_encoder,
-        lambda: jnp.zeros((row_count, merged_width), jnp.bfloat16),
-        lambda: lax.dot_general(
-            grad_acts, full_proj, (((1,), (1,)), ((), ())), preferred_element_type=jnp.float32
-        ).astype(jnp.bfloat16),
-    )
-    rounded_terms = lax.optimization_barrier(term_rows)
-    summed_rows = lax.psum_scatter(
-        rounded_terms.astype(jnp.float32).astype(jnp.bfloat16),
-        "tp",
-        scatter_dimension=0,
-        tiled=True,
-    )
-    returned = passed_along(summed_rows, "grp", -1)
+    fall = inverse_rms**3 * (total_prod / D)[:, None]
+    grad_first = (inverse_rms * scaled_first - acts_first * fall).astype(bf16)
+    grad_second = (inverse_rms * scaled_second - acts_second * fall).astype(bf16)
+
+    row_first = [grad_first] + [None] * (pair_count - 1)
+    for s in range(1, pair_count):
+        row_first[pair_count - s] = sent_round(grad_first, s)
+    row_first = jnp.stack(row_first)
+    all_first = jnp.stack([row_first, sent_across(row_first)], axis=1)
+    duo = jnp.stack([grad_second, sent_across(grad_second)])
+    all_second = [duo] + [None] * (pair_count - 1)
+    for s in range(1, pair_count):
+        all_second[pair_count - s] = sent_round(duo, s)
+    all_second = jnp.stack(all_second)
+
+    def back(block, weight):
+        return jnp.einsum("pjrc,kc->pjrk", block, weight, preferred_element_type=f32)
+
+    terms = back(all_first, w_first) + back(all_second, w_second)
+    terms = rotated(flipped(terms, odd), (pair_count - pair) % pair_count)
+    terms = terms.reshape(dp_count, tp_count, tokens_here, depth).transpose(1, 0, 2, 3)
+    terms = rotated(terms, tp_index)
+    total = terms[0]
+    for s in range(1, tp_count):
+        route = [(i, (i + s) % tp_count) for i in range(tp_count)]
+        total = total + lax.ppermute(terms[s].astype(bf16), "tp", route).astype(f32)
+    returned = passed_along(total.astype(bf16), "grp", -1)
+    whole = (total + returned.astype(f32)).astype(bf16)
+    whole = lax.all_to_all(whole, "dp", 0, 0)
+    grad_embed = whole.transpose(1, 0, 2).reshape(tokens_here, merged_width)
+
     grad_frames = lax.cond(
         is_encoder,
         lambda: encoder_backward(
-            weight_mix, gain_ln, mixed_qkv, attn_probs, normal_part, inverse, returned
+            weight_mix, gain_ln, mixed_qkv, attn_probs, normal_part, inverse, grad_embed
         ),
-        lambda: jnp.zeros(local_frames.shape, jnp.bfloat16),
+        lambda: jnp.zeros(local_frames.shape, bf16),
     )
     return grad_frames[None]
 

time: 888 us -> 241 us (0.27)
  waiting for transfers between devices: 830 us -> 107 us
  starting transfers between devices: 2.63 us -> 53 us
  local copies, waits for them, and re-layouts: 8.35 us -> 23.2 us
  between operations: 13.5 us -> 0.52 us
  other arithmetic: 7.89 us -> 18.7 us
  matrix products: 19.7 us -> 29.8 us
    all_gather x1 -> x0, waiting for transfers between devices: 767 us -> none  [per_device(): full_proj = lax.all_gather(w_proj[0], 'dp', axis=0, tiled=True)]
    ppermute x0 -> x17, waiting for transfers between devices: none -> 59.6 us  [the longest x12 30.4 us: sent_round(): lax.ppermute(block, 'dp', [(i, (i + 2 * distance) % count) for i in range...]
    reduce_scatter x1 -> x0, waiting for transfers between devices: 43.7 us -> none  [per_device(): lax.psum_scatter(rounded_terms.astype(jnp.float32).astype(jnp.bfloat16),...]
    ppermute x0 -> x17, starting transfers between devices: none -> 27.3 us  [the longest x12 21.8 us: sent_round(): lax.ppermute(block, 'dp', [(i, (i + 2 * distance) % count) for i in range...]
    ppermute x2 -> x6, waiting for transfers between devices: 18.6 us -> 35.4 us  [passed_along(): return lax.ppermute(block, axis, route)]
    all_to_all x0 -> x2, starting transfers between devices: none -> 13.9 us  [the longest x1 7.28 us: per_device(): swapped = lax.all_to_all(pieces, 'dp', 0, 0)]
    all_to_all x0 -> x2, waiting for transfers between devices: none -> 11.6 us  [the longest x1 9.75 us: per_device(): whole = lax.all_to_all(whole, 'dp', 0, 0)]
    ppermute x2 -> x6, starting transfers between devices: 2.59 us -> 11.8 us  [passed_along(): return lax.ppermute(block, axis, route)]
  transfers between devices with their start and end apart: 4 -> 25, of which waited for: 4 -> 15; matrix products, arithmetic and copies ran while one was open for 2% -> 15% of each run, Pallas kernels for 0% -> 0%
where the time goes in v1:
time: 241 us; the launch traced here: 240 us
  waiting for transfers between devices  107 us (44%)
  starting transfers between devices  53 us (22%)
  matrix products  29.8 us (12%)
  local copies, waits for them, and re-layouts  23.2 us (10%)
  other arithmetic  18.7 us (8%)
  blocking collectives  8.04 us (3%)
    ppermute x6, waiting for transfers between devices, passed_along(): return lax.ppermute(block, axis, route)  35.4 us
    ppermute x12, waiting for transfers between devices, sent_round(): lax.ppermute(block, 'dp', [(i, (i + 2 * distance) % count) for i in range...  30.4 us
    ppermute x4, waiting for transfers between devices, sent_across(): lax.ppermute(block, 'dp', [(i, i ^ 1) for i in range(lax.axis_size('dp'))])  27.6 us
    ppermute x12, starting transfers between devices, sent_round(): lax.ppermute(block, 'dp', [(i, (i + 2 * distance) % count) for i in range...  21.8 us
    ppermute x6, starting transfers between devices, passed_along(): return lax.ppermute(block, axis, route)  11.8 us
    all_to_all x1, waiting for transfers between devices, per_device(): whole = lax.all_to_all(whole, 'dp', 0, 0)  9.75 us
    dot_general x1, matrix products, encoder_backward(): jnp.einsum('fpc,ec->fpe', grad_mixed, w_qkv, preferred_element_type=jnp.f...  7.81 us
    all_to_all x1, starting transfers between devices, per_device(): swapped = lax.all_to_all(pieces, 'dp', 0, 0)  7.28 us
  transfers between devices with their start and end apart: 25, of which 15 were waited for; matrix products, arithmetic and copies ran while one was open for 15% of the time, Pallas kernels for 0%

profile of v1, /device:TPU:0, one launch (start us, length us, event | category | flops | bytes accessed | tf_op | source)
XLA Modules:
  0.0 240.2 jit_solution(540457605125330367)
XLA Ops:
  0.0 2.1 slice.185
  3.5 21.0 %conditional.2 = (bf16[32,5120]{1,0:T(8,128)(2,1)S(1)}, bf16[1,128,3840]{2,1,0:T(8,128)(2,1)S(1)}, f32[1,16,128,128]{2,3,1,0:T(8,128)S(1)}, f32[1,128,1280]{2,1,0:T(8,128)S(1)}, f32[1,128,1]{1,2,0:T(1,128)S(1)}) conditional(s32[]{:T(128)} %convert_element_type.202, () %tuple.22, (bf16[1,1,128,1280]{3,2,1,0:T(8,128)(2,1)S(1)}, ...), branch_computations={%region_0.1_spmd, %region_1.6_spmd} | conditional | flops 1389332864 | bytes 60408556 | solution.py:158
  4.5 5.3 %convolution_convert_fusion = bf16[128,3840]{1,0:T(8,128)(2,1)S(1)} fusion(bf16[1280,3840]{1,0:T(8,128)(2,1)} %get-tuple-element.31, bf16[1,1,128,1280]{3,2,1,0:T(8,128)(2,1)S(1)} %get-tuple-element.51), kind=kOutput, calls=%fused_computation.1 | convolution fusion | flops 1258782720 | bytes 11141120 | tf_op jit(solution)/shard_map/cond/branch_1_fun/fpe,ec->fpc/dot_general | solution.py:21
  13.3 2.0 add_reduce_fusion
  25.2 7.3 %all-to-all-start = ((bf16[8,32,640]{2,1,0:T(8,128)(2,1)}), bf16[8,32,640]{2,1,0:T(8,128)(2,1)}, u32[]{:S(2)}, u32[]{:S(2)}) async-start(bf16[8,32,640]{2,1,0:T(8,128)(2,1)} %bitcast.238), calls=%async_computation | async-start | bytes 655360 | tf_op jit(solution)/shard_map/all_to_all | solution.py:163
  36.8 2.9 %slice.177 = bf16[640,1408]{1,0:T(8,128)(2,1)} slice(bf16[640,4096]{1,0:T(8,128)(2,1)} %bitcast.246), slice={[0:640], [0:1408]} | slice | bytes 3604480 | tf_op jit(solution)/shard_map/slice | solution.py:137
  42.9 5.4 %collective-permute-start = (bf16[8,32,640]{2,1,0:T(8,128)(2,1)}, bf16[8,32,640]{2,1,0:T(8,128)(2,1)}, u32[]{:S(2)}, u32[]{:S(2)}) collective-permute-start(bf16[8,32,640]{2,1,0:T(8,128)(2,1)} %all-to-all-done), channel_id=1, source_target_pairs={{0,16},{1,17},{2,18},{3,19},{4,20},{5,21},{6,22},{7,23},{8,24},{9,... | collective-permute-start | bytes 983048 | tf_op jit(solution)/shard_map/ppermute | solution.py:14
  49.8 4.5 %collective-permute-done = bf16[8,32,640]{2,1,0:T(8,128)(2,1)} collective-permute-done((bf16[8,32,640]{2,1,0:T(8,128)(2,1)}, bf16[8,32,640]{2,1,0:T(8,128)(2,1)}, u32[]{:S(2)}, u32[]{:S(2)}) %collective-permute-start) | collective-permute-done | bytes 327712 | tf_op jit(solution)/shard_map/ppermute | solution.py:14
  55.3 2.3 all-gather
  58.4 3.6 %collective-permute-start.9 = (bf16[2,64,640]{2,1,0:T(8,128)(2,1)S(1)}, bf16[2,64,640]{2,1,0:T(8,128)(2,1)S(1)}, u32[]{:S(2)}, u32[]{:S(2)}) collective-permute-start(bf16[2,64,640]{2,1,0:T(8,128)(2,1)S(1)} %convolution_convert_fusion.5), channel_id=1, source_target_pairs={{0,12},{2,14},{4,0},{6,2},{8,4},{10,6},{12,8},{14,10},{1,13},{3,15... | collective-permute-start | bytes 491528 | tf_op jit(solution)/shard_map/ppermute | solution.py:108
  62.7 20.6 %collective-permute-done.1 = bf16[640,1408]{1,0:T(8,128)(2,1)} collective-permute-done((bf16[640,1408]{1,0:T(8,128)(2,1)}, bf16[640,1408]{1,0:T(8,128)(2,1)}, u32[]{:S(2)}, u32[]{:S(2)}) %collective-permute-start.1) | collective-permute-done | bytes 1802272 | tf_op jit(solution)/shard_map/ppermute | solution.py:14
  85.1 2.2 slice_select_fusion
  92.6 12.5 %collective-permute-done.2 = bf16[4,64,1408]{2,1,0:T(8,128)(2,1)S(1)} collective-permute-done((bf16[4,64,1408]{2,1,0:T(8,128)(2,1)S(1)}, bf16[4,64,1408]{2,1,0:T(8,128)(2,1)S(1)}, u32[]{:S(2)}, u32[]{:S(2)}) %collective-permute-start.2) | collective-permute-done | bytes 720928 | tf_op jit(solution)/shard_map/ppermute | solution.py:112
  105.9 2.4 %collective-permute-start.5 = (bf16[64,1408]{1,0:T(8,128)(2,1)S(1)}, bf16[64,1408]{1,0:T(8,128)(2,1)S(1)}, u32[]{:S(2)}, u32[]{:S(2)}) collective-permute-start(bf16[64,1408]{1,0:T(8,128)(2,1)S(1)} %get-tuple-element.101), channel_id=1, source_target_pairs={{0,12},{2,14},{4,0},{6,2},{8,4},{10,6},{12,8},{14,10},{1,13},{3,15... | collective-permute-start | bytes 540680 | tf_op jit(solution)/shard_map/ppermute | solution.py:108
  111.6 2.7 %collective-permute-done.5 = bf16[64,1408]{1,0:T(8,128)(2,1)S(1)} collective-permute-done((bf16[64,1408]{1,0:T(8,128)(2,1)S(1)}, bf16[64,1408]{1,0:T(8,128)(2,1)S(1)}, u32[]{:S(2)}, u32[]{:S(2)}) %collective-permute-start.5) | collective-permute-done | bytes 180256 | tf_op jit(solution)/shard_map/ppermute | solution.py:108
  114.3 7.4 %collective-permute-done.4 = bf16[64,1408]{1,0:T(8,128)(2,1)S(1)} collective-permute-done((bf16[64,1408]{1,0:T(8,128)(2,1)S(1)}, bf16[64,1408]{1,0:T(8,128)(2,1)S(1)}, u32[]{:S(2)}, u32[]{:S(2)}) %collective-permute-start.4) | collective-permute-done | bytes 180256 | tf_op jit(solution)/shard_map/ppermute | solution.py:108
  122.7 5.8 %all-reduce = (f32[64]{0:T(128)S(1)}, f32[64]{0:T(128)S(1)}) all-reduce(f32[64]{0:T(128)S(1)} %add.142, f32[64]{0:T(128)S(1)} %add.139), channel_id=1, replica_groups=mesh['grp'=2,'dp'=8,'tp'=2] {'grp','tp'}, use_global_device_ids=true, to_apply=%region_12.13 | all-reduce | flops 128 | bytes 1024 | tf_op jit(solution)/shard_map/psum | solution.py:202
  132.1 2.8 %collective-permute-start.13 = (bf16[64,1408]{1,0:T(8,128)(2,1)S(1)}, bf16[64,1408]{1,0:T(8,128)(2,1)S(1)}, u32[]{:S(2)}, u32[]{:S(2)}) collective-permute-start(bf16[64,1408]{1,0:T(8,128)(2,1)S(1)} %subtract_convert_fusion), channel_id=1, source_target_pairs={{0,12},{2,14},{4,0},{6,2},{8,4},{10,6},{12,8},{14,10},{1,13},{3,15... | collective-permute-start | bytes 540680 | tf_op jit(solution)/shard_map/ppermute | solution.py:108
  134.9 4.2 %collective-permute-done.15 = bf16[64,1408]{1,0:T(8,128)(2,1)S(1)} collective-permute-done((bf16[64,1408]{1,0:T(8,128)(2,1)S(1)}, bf16[64,1408]{1,0:T(8,128)(2,1)S(1)}, u32[]{:S(2)}, u32[]{:S(2)}) %collective-permute-start.15) | collective-permute-done | bytes 180256 | tf_op jit(solution)/shard_map/ppermute | solution.py:108
  139.1 6.6 %collective-permute-done.14 = bf16[64,1408]{1,0:T(8,128)(2,1)S(1)} collective-permute-done((bf16[64,1408]{1,0:T(8,128)(2,1)S(1)}, bf16[64,1408]{1,0:T(8,128)(2,1)S(1)}, u32[]{:S(2)}, u32[]{:S(2)}) %collective-permute-start.14) | collective-permute-done | bytes 180256 | tf_op jit(solution)/shard_map/ppermute | solution.py:108
  150.1 15.1 %collective-permute-done.17 = bf16[64,640]{1,0:T(8,128)(2,1)S(1)} collective-permute-done((bf16[64,640]{1,0:T(8,128)(2,1)S(1)}, bf16[64,640]{1,0:T(8,128)(2,1)S(1)}, u32[]{:S(2)}, u32[]{:S(2)}) %collective-permute-start.17) | collective-permute-done | bytes 81952 | tf_op jit(solution)/shard_map/ppermute | solution.py:112
  165.9 4.4 %collective-permute-start.20 = (bf16[2,64,640]{2,1,0:T(8,128)(2,1)}, bf16[2,64,640]{2,1,0:T(8,128)(2,1)}, u32[]{:S(2)}, u32[]{:S(2)}) collective-permute-start(bf16[2,64,640]{2,1,0:T(8,128)(2,1)} %get-tuple-element.106), channel_id=1, source_target_pairs={{0,4},{2,6},{4,8},{6,10},{8,12},{10,14},{12,0},{14,2},{1,5},{3,7},... | collective-permute-start | bytes 491528 | tf_op jit(solution)/shard_map/ppermute | solution.py:108
  172.7 4.5 %collective-permute-done.20 = bf16[2,64,640]{2,1,0:T(8,128)(2,1)} collective-permute-done((bf16[2,64,640]{2,1,0:T(8,128)(2,1)}, bf16[2,64,640]{2,1,0:T(8,128)(2,1)}, u32[]{:S(2)}, u32[]{:S(2)}) %collective-permute-start.20) | collective-permute-done | bytes 163872 | tf_op jit(solution)/shard_map/ppermute | solution.py:108
  177.2 4.3 %collective-permute-done.19 = bf16[2,64,640]{2,1,0:T(8,128)(2,1)} collective-permute-done((bf16[2,64,640]{2,1,0:T(8,128)(2,1)}, bf16[2,64,640]{2,1,0:T(8,128)(2,1)}, u32[]{:S(2)}, u32[]{:S(2)}) %collective-permute-start.19) | collective-permute-done | bytes 163872 | tf_op jit(solution)/shard_map/ppermute | solution.py:108
  181.5 2.1 fusion.39
  183.6 2.5 %fusion.32 = f32[4,2,64,640]{3,2,0,1:T(8,128)S(1)} fusion(f32[4,2,64,640]{3,2,0,1:T(8,128)S(1)} %fusion.39, bf16[640,1408]{1,0:T(8,128)(2,1)S(1)} %copy-done.1, bf16[4,1,64,1408]{3,2,0,1:T(8,128)(2,1)} %bitcast.65, bf16[4,1,64,1408]{3,2,0,1:T(8,128)(2,1)S(1)} %copy-done.15), kind=kOutput, calls=%fused_computation.65 | convolution fusion | flops 923795456 | bytes 5865472 | tf_op jit(solution)/shard_map/pjrc,kc->pjrk/dot_general | solution.py:220
  190.2 10.3 %collective-permute-done.22 = bf16[8,32,640]{2,1,0:T(8,128)(2,1)S(1)} collective-permute-done((bf16[8,32,640]{2,1,0:T(8,128)(2,1)S(1)}, bf16[8,32,640]{2,1,0:T(8,128)(2,1)S(1)}, u32[]{:S(2)}, u32[]{:S(2)}) %collective-permute-start.22) | collective-permute-done | bytes 327712 | tf_op jit(solution)/shard_map/ppermute | solution.py:14
  201.4 6.6 %all-to-all-start.1 = ((bf16[8,32,640]{2,1,0:T(8,128)(2,1)}), bf16[8,32,640]{2,1,0:T(8,128)(2,1)S(1)}, u32[]{:S(2)}, u32[]{:S(2)}) async-start(bf16[8,32,640]{2,1,0:T(8,128)(2,1)} %add_convert_fusion), calls=%async_computation.1 | async-start | bytes 655360 | tf_op jit(solution)/shard_map/all_to_all | solution.py:232
  208.1 9.7 %all-to-all-done.1 = bf16[8,32,640]{2,1,0:T(8,128)(2,1)S(1)} async-done(((bf16[8,32,640]{2,1,0:T(8,128)(2,1)}), bf16[8,32,640]{2,1,0:T(8,128)(2,1)S(1)}, u32[]{:S(2)}, u32[]{:S(2)}) %all-to-all-start.1) | async-done | bytes 327712 | tf_op jit(solution)/shard_map/all_to_all | solution.py:232
  217.8 22.4 %conditional.3 = (bf16[1,1,128,1280]{3,2,1,0:T(8,128)(2,1)}) conditional(s32[]{:T(128)} %convert_element_type.202, () %tuple.21, (f32[1,128,1]{1,2,0:T(1,128)S(1)}, bf16[32,8,640]{2,0,1:T(8,128)(2,1)S(1)}, bf16[1280]{0:T(1024)(128)(2,1)S(1)}, f32[1,128,1280]{2,1,0:T(8,128)S(1)}, bf16[1,128,3840]{2,1,0:T(8,128)(2,1)S(1)}, ...), branch_computations={%region_13.14_spmd, %region_14.19_spmd} | conditional | flops 1432648960 | bytes 38745184 | solution.py:235
  225.1 2.2 fusion.15
  232.4 7.8 %fusion.13 = bf16[1,1,128,1280]{3,2,1,0:T(8,128)(2,1)} fusion(bf16[128,3840]{0,1:T(8,128)(2,1)S(1)} %bitcast.252, bf16[1280,3840]{1,0:T(8,128)(2,1)} %get-tuple-element.39, f32[1,128,1280]{2,1,0:T(8,128)S(1)} %get-tuple-element.36, f32[128]{0:T(128)S(1)} %get-tuple-element.92, f32[128]{0:T(128)S(1)} %get-tuple-element.93, ...), kind=kOutput, calls=%fused_computation.27 | convolution fusion | flops 1259438080 | bytes 12458496 | tf_op jit(solution)/shard_map/cond/branch_1_fun/fpc,ec->fpe/dot_general | solution.py:88
  (162 shorter events, 67.3 us)
Async XLA Ops:
  2.2 46.1 %collective-permute-start.6 = (bf16[640,640]{1,0:T(8,128)(2,1)}, bf16[640,640]{1,0:T(8,128)(2,1)}, u32[]{:S(2)}, u32[]{:S(2)}) collective-permute-start(bf16[640,640]{1,0:T(8,128)(2,1)} %slice.185), channel_id=1, source_target_pairs={{16,0},{17,1},{18,2},{19,3},{20,4},{21,5},{22,6},{23,7},{24,8},{25... | collective-permute-start | bytes 2457608 | tf_op jit(solution)/shard_map/ppermute | solution.py:14
  24.5 11.0 %copy-start.20 = (bf16[1,4096]{1,0:T(2,128)(2,1)S(1)}, bf16[1,4096]{1,0:T(2,128)(2,1)}, u32[]{:S(2)}) copy-start(bf16[1,4096]{1,0:T(2,128)(2,1)} %param.16) | copy-start | bytes 24580
  25.2 17.7 %all-to-all-start = ((bf16[8,32,640]{2,1,0:T(8,128)(2,1)}), bf16[8,32,640]{2,1,0:T(8,128)(2,1)}, u32[]{:S(2)}, u32[]{:S(2)}) async-start(bf16[8,32,640]{2,1,0:T(8,128)(2,1)} %bitcast.238), calls=%async_computation | async-start | bytes 655360 | tf_op jit(solution)/shard_map/all_to_all | solution.py:163
  34.2 76.2 %collective-permute-start.12 = (bf16[64,2048]{1,0:T(8,128)(2,1)}, bf16[64,2048]{1,0:T(8,128)(2,1)}, u32[]{:S(2)}, u32[]{:S(2)}) collective-permute-start(bf16[64,2048]{1,0:T(8,128)(2,1)} %slice.192), channel_id=1, source_target_pairs={{16,0},{17,1},{18,2},{19,3},{20,4},{21,5},{22,6},{23,7},{24,8},{25... | collective-permute-start | bytes 786440 | tf_op jit(solution)/shard_map/ppermute | solution.py:14
  35.5 52.6 %collective-permute-start.11 = (bf16[1,2048]{1,0:T(2,128)(2,1)S(1)}, bf16[1,2048]{1,0:T(2,128)(2,1)S(1)}, u32[]{:S(2)}, u32[]{:S(2)}) collective-permute-start(bf16[1,2048]{1,0:T(2,128)(2,1)S(1)} %slice.150), channel_id=1, source_target_pairs={{16,0},{17,1},{18,2},{19,3},{20,4},{21,5},{22,6},{23,7},{24,8},{25... | collective-permute-start | bytes 12296 | tf_op jit(solution)/shard_map/ppermute | solution.py:14
  39.7 43.7 %collective-permute-start.1 = (bf16[640,1408]{1,0:T(8,128)(2,1)}, bf16[640,1408]{1,0:T(8,128)(2,1)}, u32[]{:S(2)}, u32[]{:S(2)}) collective-permute-start(bf16[640,1408]{1,0:T(8,128)(2,1)} %slice.177), channel_id=1, source_target_pairs={{16,0},{17,1},{18,2},{19,3},{20,4},{21,5},{22,6},{23,7},{24,8},{25... | collective-permute-start | bytes 5406728 | tf_op jit(solution)/shard_map/ppermute | solution.py:14
  42.9 11.3 %collective-permute-start = (bf16[8,32,640]{2,1,0:T(8,128)(2,1)}, bf16[8,32,640]{2,1,0:T(8,128)(2,1)}, u32[]{:S(2)}, u32[]{:S(2)}) collective-permute-start(bf16[8,32,640]{2,1,0:T(8,128)(2,1)} %all-to-all-done), channel_id=1, source_target_pairs={{0,16},{1,17},{2,18},{3,19},{4,20},{5,21},{6,22},{7,23},{8,24},{9,... | collective-permute-start | bytes 983048 | tf_op jit(solution)/shard_map/ppermute | solution.py:14
  58.4 31.2 %collective-permute-start.9 = (bf16[2,64,640]{2,1,0:T(8,128)(2,1)S(1)}, bf16[2,64,640]{2,1,0:T(8,128)(2,1)S(1)}, u32[]{:S(2)}, u32[]{:S(2)}) collective-permute-start(bf16[2,64,640]{2,1,0:T(8,128)(2,1)S(1)} %convolution_convert_fusion.5), channel_id=1, source_target_pairs={{0,12},{2,14},{4,0},{6,2},{8,4},{10,6},{12,8},{14,10},{1,13},{3,15... | collective-permute-start | bytes 491528 | tf_op jit(solution)/shard_map/ppermute | solution.py:108
  62.3 27.3 %collective-permute-start.8 = (bf16[2,64,640]{2,1,0:T(8,128)(2,1)S(1)}, bf16[2,64,640]{2,1,0:T(8,128)(2,1)S(1)}, u32[]{:S(2)}, u32[]{:S(2)}) collective-permute-start(bf16[2,64,640]{2,1,0:T(8,128)(2,1)S(1)} %convolution_convert_fusion.6), channel_id=1, source_target_pairs={{0,8},{2,10},{4,12},{6,14},{8,0},{10,2},{12,4},{14,6},{1,9},{3,11}... | collective-permute-start | bytes 491528 | tf_op jit(solution)/shard_map/ppermute | solution.py:108
  83.3 7.1 %collective-permute-start.7 = (bf16[2,64,640]{2,1,0:T(8,128)(2,1)S(1)}, bf16[2,64,640]{2,1,0:T(8,128)(2,1)S(1)}, u32[]{:S(2)}, u32[]{:S(2)}) collective-permute-start(bf16[2,64,640]{2,1,0:T(8,128)(2,1)S(1)} %convolution_convert_fusion.7), channel_id=1, source_target_pairs={{0,4},{2,6},{4,8},{6,10},{8,12},{10,14},{12,0},{14,2},{1,5},{3,7},... | collective-permute-start | bytes 491528 | tf_op jit(solution)/shard_map/ppermute | solution.py:108
  87.3 17.8 %copy-start = (bf16[640,1408]{1,0:T(8,128)(2,1)}, bf16[640,1408]{1,0:T(8,128)(2,1)S(1)}, u32[]{:S(2)}) copy-start(bf16[640,1408]{1,0:T(8,128)(2,1)S(1)} %slice_select_fusion) | copy-start | bytes 5406724
  88.1 17.1 %collective-permute-start.2 = (bf16[4,64,1408]{2,1,0:T(8,128)(2,1)S(1)}, bf16[4,64,1408]{2,1,0:T(8,128)(2,1)S(1)}, u32[]{:S(2)}, u32[]{:S(2)}) collective-permute-start(bf16[4,64,1408]{2,1,0:T(8,128)(2,1)S(1)} %convolution_convert_fusion.4), channel_id=1, source_target_pairs={{0,2},{2,0},{4,6},{6,4},{8,10},{10,8},{12,14},{14,12},{1,3},{3,1},... | collective-permute-start | bytes 2162696 | tf_op jit(solution)/shard_map/ppermute | solution.py:112
  90.8 20.7 %copy-start.11 = (f32[2,64,640]{2,1,0:T(8,128)}, f32[2,64,640]{2,1,0:T(8,128)S(1)}, u32[]{:S(2)}) copy-start(f32[2,64,640]{2,1,0:T(8,128)S(1)} %fusion.38) | copy-start | bytes 983044
  90.8 19.6 %copy-start.17 = (bf16[1,64,4096]{2,1,0:T(8,128)(2,1)S(1)}, bf16[1,64,4096]{2,1,0:T(8,128)(2,1)}, u32[]{:S(2)}) copy-start(bf16[1,64,4096]{2,1,0:T(8,128)(2,1)} %param.17) | copy-start | bytes 1572868
  90.8 20.7 %collective-permute-start.10 = (bf16[64,640]{1,0:T(8,128)(2,1)S(1)}, bf16[64,640]{1,0:T(8,128)(2,1)S(1)}, u32[]{:S(2)}, u32[]{:S(2)}) collective-permute-start(bf16[64,640]{1,0:T(8,128)(2,1)S(1)} %fusion.53), channel_id=1, source_target_pairs={{0,2},{2,0},{4,6},{6,4},{8,10},{10,8},{12,14},{14,12},{1,3},{3,1},... | collective-permute-start | bytes 245768 | tf_op jit(solution)/shard_map/ppermute | solution.py:112
  105.9 8.4 %collective-permute-start.5 = (bf16[64,1408]{1,0:T(8,128)(2,1)S(1)}, bf16[64,1408]{1,0:T(8,128)(2,1)S(1)}, u32[]{:S(2)}, u32[]{:S(2)}) collective-permute-start(bf16[64,1408]{1,0:T(8,128)(2,1)S(1)} %get-tuple-element.101), channel_id=1, source_target_pairs={{0,12},{2,14},{4,0},{6,2},{8,4},{10,6},{12,8},{14,10},{1,13},{3,15... | collective-permute-start | bytes 540680 | tf_op jit(solution)/shard_map/ppermute | solution.py:108
  108.4 13.3 %collective-permute-start.4 = (bf16[64,1408]{1,0:T(8,128)(2,1)S(1)}, bf16[64,1408]{1,0:T(8,128)(2,1)S(1)}, u32[]{:S(2)}, u32[]{:S(2)}) collective-permute-start(bf16[64,1408]{1,0:T(8,128)(2,1)S(1)} %get-tuple-element.102), channel_id=1, source_target_pairs={{0,8},{2,10},{4,12},{6,14},{8,0},{10,2},{12,4},{14,6},{1,9},{3,11}... | collective-permute-start | bytes 540680 | tf_op jit(solution)/shard_map/ppermute | solution.py:108
  108.9 12.8 %collective-permute-start.3 = (bf16[64,1408]{1,0:T(8,128)(2,1)S(1)}, bf16[64,1408]{1,0:T(8,128)(2,1)S(1)}, u32[]{:S(2)}, u32[]{:S(2)}) collective-permute-start(bf16[64,1408]{1,0:T(8,128)(2,1)S(1)} %get-tuple-element.100), channel_id=1, source_target_pairs={{0,4},{2,6},{4,8},{6,10},{8,12},{10,14},{12,0},{14,2},{1,5},{3,7},... | collective-permute-start | bytes 540680 | tf_op jit(solution)/shard_map/ppermute | solution.py:108
  111.5 11.2 %copy-start.18 = (bf16[64,640]{1,0:T(8,128)(2,1)}, bf16[64,640]{1,0:T(8,128)(2,1)S(1)}, u32[]{:S(2)}) copy-start(bf16[64,640]{1,0:T(8,128)(2,1)S(1)} %collective-permute-done.10) | copy-start | bytes 245764
  129.7 18.5 %copy-start.12 = (f32[2,64,640]{2,1,0:T(8,128)S(1)}, f32[2,64,640]{2,1,0:T(8,128)}, u32[]{:S(2)}) copy-start(f32[2,64,640]{2,1,0:T(8,128)} %copy-done.11) | copy-start | bytes 983044
  129.7 18.4 %copy-start.19 = (bf16[64,640]{1,0:T(8,128)(2,1)S(1)}, bf16[64,640]{1,0:T(8,128)(2,1)}, u32[]{:S(2)}) copy-start(bf16[64,640]{1,0:T(8,128)(2,1)} %copy-done.18) | copy-start | bytes 245764
  129.7 9.4 %collective-permute-start.15 = (bf16[64,1408]{1,0:T(8,128)(2,1)S(1)}, bf16[64,1408]{1,0:T(8,128)(2,1)S(1)}, u32[]{:S(2)}, u32[]{:S(2)}) collective-permute-start(bf16[64,1408]{1,0:T(8,128)(2,1)S(1)} %subtract_convert_fusion), channel_id=1, source_target_pairs={{0,4},{2,6},{4,8},{6,10},{8,12},{10,14},{12,0},{14,2},{1,5},{3,7},... | collective-permute-start | bytes 540680 | tf_op jit(solution)/shard_map/ppermute | solution.py:108
  130.1 15.6 %collective-permute-start.14 = (bf16[64,1408]{1,0:T(8,128)(2,1)S(1)}, bf16[64,1408]{1,0:T(8,128)(2,1)S(1)}, u32[]{:S(2)}, u32[]{:S(2)}) collective-permute-start(bf16[64,1408]{1,0:T(8,128)(2,1)S(1)} %subtract_convert_fusion), channel_id=1, source_target_pairs={{0,8},{2,10},{4,12},{6,14},{8,0},{10,2},{12,4},{14,6},{1,9},{3,11}... | collective-permute-start | bytes 540680 | tf_op jit(solution)/shard_map/ppermute | solution.py:108
  132.1 13.6 %collective-permute-start.13 = (bf16[64,1408]{1,0:T(8,128)(2,1)S(1)}, bf16[64,1408]{1,0:T(8,128)(2,1)S(1)}, u32[]{:S(2)}, u32[]{:S(2)}) collective-permute-start(bf16[64,1408]{1,0:T(8,128)(2,1)S(1)} %subtract_convert_fusion), channel_id=1, source_target_pairs={{0,12},{2,14},{4,0},{6,2},{8,4},{10,6},{12,8},{14,10},{1,13},{3,15... | collective-permute-start | bytes 540680 | tf_op jit(solution)/shard_map/ppermute | solution.py:108
  147.0 36.6 %collective-permute-start.16 = (bf16[4,64,1408]{2,1,0:T(8,128)(2,1)}, bf16[4,64,1408]{2,1,0:T(8,128)(2,1)}, u32[]{:S(2)}, u32[]{:S(2)}) collective-permute-start(bf16[4,64,1408]{2,1,0:T(8,128)(2,1)} %get-tuple-element.99), channel_id=1, source_target_pairs={{0,2},{2,0},{4,6},{6,4},{8,10},{10,8},{12,14},{14,12},{1,3},{3,1},... | collective-permute-start | bytes 2162696 | tf_op jit(solution)/shard_map/ppermute | solution.py:112
  149.2 16.0 %collective-permute-start.17 = (bf16[64,640]{1,0:T(8,128)(2,1)S(1)}, bf16[64,640]{1,0:T(8,128)(2,1)S(1)}, u32[]{:S(2)}, u32[]{:S(2)}) collective-permute-start(bf16[64,640]{1,0:T(8,128)(2,1)S(1)} %subtract_convert_fusion.1), channel_id=1, source_target_pairs={{0,2},{2,0},{4,6},{6,4},{8,10},{10,8},{12,14},{14,12},{1,3},{3,1},... | collective-permute-start | bytes 245768 | tf_op jit(solution)/shard_map/ppermute | solution.py:112
  165.9 11.3 %collective-permute-start.20 = (bf16[2,64,640]{2,1,0:T(8,128)(2,1)}, bf16[2,64,640]{2,1,0:T(8,128)(2,1)}, u32[]{:S(2)}, u32[]{:S(2)}) collective-permute-start(bf16[2,64,640]{2,1,0:T(8,128)(2,1)} %get-tuple-element.106), channel_id=1, source_target_pairs={{0,4},{2,6},{4,8},{6,10},{8,12},{10,14},{12,0},{14,2},{1,5},{3,7},... | collective-permute-start | bytes 491528 | tf_op jit(solution)/shard_map/ppermute | solution.py:108
  170.3 11.1 %collective-permute-start.19 = (bf16[2,64,640]{2,1,0:T(8,128)(2,1)}, bf16[2,64,640]{2,1,0:T(8,128)(2,1)}, u32[]{:S(2)}, u32[]{:S(2)}) collective-permute-start(bf16[2,64,640]{2,1,0:T(8,128)(2,1)} %get-tuple-element.106), channel_id=1, source_target_pairs={{0,8},{2,10},{4,12},{6,14},{8,0},{10,2},{12,4},{14,6},{1,9},{3,11}... | collective-permute-start | bytes 491528 | tf_op jit(solution)/shard_map/ppermute | solution.py:108
  172.2 9.3 %collective-permute-start.18 = (bf16[2,64,640]{2,1,0:T(8,128)(2,1)}, bf16[2,64,640]{2,1,0:T(8,128)(2,1)}, u32[]{:S(2)}, u32[]{:S(2)}) collective-permute-start(bf16[2,64,640]{2,1,0:T(8,128)(2,1)} %get-tuple-element.106), channel_id=1, source_target_pairs={{0,12},{2,14},{4,0},{6,2},{8,4},{10,6},{12,8},{14,10},{1,13},{3,15... | collective-permute-start | bytes 491528 | tf_op jit(solution)/shard_map/ppermute | solution.py:108
  187.1 1.7 collective-permute-start.21
  188.9 11.6 %collective-permute-start.22 = (bf16[8,32,640]{2,1,0:T(8,128)(2,1)S(1)}, bf16[8,32,640]{2,1,0:T(8,128)(2,1)S(1)}, u32[]{:S(2)}, u32[]{:S(2)}) collective-permute-start(bf16[8,32,640]{2,1,0:T(8,128)(2,1)S(1)} %fusion.47), channel_id=1, source_target_pairs={{16,0},{17,1},{18,2},{19,3},{20,4},{21,5},{22,6},{23,7},{24,8},{25... | collective-permute-start | bytes 983048 | tf_op jit(solution)/shard_map/ppermute | solution.py:14
  201.4 16.4 %all-to-all-start.1 = ((bf16[8,32,640]{2,1,0:T(8,128)(2,1)}), bf16[8,32,640]{2,1,0:T(8,128)(2,1)S(1)}, u32[]{:S(2)}, u32[]{:S(2)}) async-start(bf16[8,32,640]{2,1,0:T(8,128)(2,1)} %add_convert_fusion), calls=%async_computation.1 | async-start | bytes 655360 | tf_op jit(solution)/shard_map/all_to_all | solution.py:232
  (16 other events, 39.6 us)

commit v2 on v1

v2 whole, which is shorter than its diff:
```python
import jax
import jax.numpy as jnp
from jax import lax
from jax.experimental import pallas as pl
from jax.experimental.pallas import tpu as pltpu
from jax.sharding import PartitionSpec as P

HEADS = 16
HDIM = 80
D = 8192
TOKF = 32
CHUNK = 640
CHUNK_HEADS = CHUNK // HDIM


def head_window(head):
    low, high = head * HDIM, (head + 1) * HDIM
    start, stop = low // 128 * 128, -(-high // 128) * 128
    return start, stop, low - start, high - start


def head_only(block, low, high):
    lane = lax.broadcasted_iota(jnp.int32, block.shape, 1)
    return jnp.where((lane >= low) & (lane < high), block, jnp.zeros_like(block))


def dot(a, b, dims):
    return lax.dot_general(a, b, (dims, ((), ())), preferred_element_type=jnp.float32)


NT = ((1,), (1,))
NN = ((1,), (0,))
TN = ((0,), (0,))


def token_order(length):
    row = lax.broadcasted_iota(jnp.int32, (length, length), 0)
    column = lax.broadcasted_iota(jnp.int32, (length, length), 1)
    tokens = length // 4
    return (row % tokens * 4 + row // tokens == column).astype(jnp.bfloat16)


def weight_copies(w_hbm, w_buf, sems):
    return [
        pltpu.make_async_copy(
            w_hbm.at[:, pl.ds(((i % 3) * 2 + i // 3) * CHUNK, CHUNK)], w_buf.at[i], sems.at[i]
        )
        for i in range(6)
    ]


def encoder_forward_kernel(
    x_ref, gain_ref, w_hbm, emb_ref, qkv_ref, probs_ref, norm_ref, inv_ref, w_buf, work, sems
):
    copies = weight_copies(w_hbm, w_buf, sems)
    for copy in copies:
        copy.start()
    x = x_ref[...]
    vis = x.shape[1]
    for half in range(2):
        for kind in range(3):
            i = half * 3 + kind
            copies[i].wait()
            qkv_ref[i] = dot(x, w_buf[i], NN).astype(jnp.bfloat16)
        work[half] = x[:, half * CHUNK : (half + 1) * CHUNK].astype(jnp.float32)
        for head in range(CHUNK_HEADS):
            start, stop, low, high = head_window(head)
            query = qkv_ref[half * 3, :, start:stop]
            key = head_only(qkv_ref[half * 3 + 1, :, start:stop], low, high)
            value = head_only(qkv_ref[half * 3 + 2, :, start:stop], low, high)
            scores = dot(query, key, NT) * HDIM ** (-0.5)
            weights = jnp.exp(scores - jnp.max(scores, axis=1, keepdims=True))
            weights = weights / jnp.sum(weights, axis=1, keepdims=True)
            probs_ref[half * CHUNK_HEADS + head] = weights
            work[half, :, start:stop] += dot(weights.astype(jnp.bfloat16), value, NN)
    first, second = work[0], work[1]
    mean = (
        jnp.sum(first, axis=1, keepdims=True) + jnp.sum(second, axis=1, keepdims=True)
    ) / vis
    first, second = first - mean, second - mean
    variance = (
        jnp.sum(first * first, axis=1, keepdims=True)
        + jnp.sum(second * second, axis=1, keepdims=True)
    ) / vis
    inverse = lax.rsqrt(variance + 1e-06)
    inv_ref[...] = inverse
    gain = gain_ref[...].astype(jnp.float32)
    tokens = x.shape[0] // 4
    order = token_order(x.shape[0])
    for half, centred in enumerate((first, second)):
        normal = centred * inverse
        norm_ref[half] = normal
        embedded = (normal * gain[:, half * CHUNK : (half + 1) * CHUNK]).astype(jnp.bfloat16)
        embedded = dot(order, embedded, NN).astype(jnp.bfloat16)
        for j in range(4):
            emb_ref[j * 2 + half] = embedded[j * tokens : (j + 1) * tokens]


def encoder_forward(frame, w_qkv, ln_gain):
    length, vis = frame.shape
    bf16, f32 = jnp.bfloat16, jnp.float32
    vmem = pl.BlockSpec(memory_space=pltpu.VMEM)
    return pl.pallas_call(
        encoder_forward_kernel,
        out_shape=(
            jax.ShapeDtypeStruct((8, length // 4, CHUNK), bf16),
            jax.ShapeDtypeStruct((6, length, CHUNK), bf16),
            jax.ShapeDtypeStruct((HEADS, length, length), f32),
            jax.ShapeDtypeStruct((2, length, CHUNK), f32),
            jax.ShapeDtypeStruct((length, 1), f32),
        ),
        in_specs=[vmem, vmem, pl.BlockSpec(memory_space=pltpu.HBM)],
        out_specs=(vmem,) * 5,
        scratch_shapes=[
            pltpu.VMEM((6, vis, CHUNK), bf16),
            pltpu.VMEM((2, length, CHUNK), f32),
            pltpu.SemaphoreType.DMA((6,)),
        ],
        compiler_params=pltpu.CompilerParams(vmem_limit_bytes=40 << 20),
        cost_estimate=pl.CostEstimate(flops=1000, transcendentals=0, bytes_accessed=1000),
        name="encoder_forward",
    )(frame, ln_gain, w_qkv)


def encoder_backward_kernel(
    flag_ref,
    grad_ref,
    gain_ref,
    qkv_ref,
    probs_ref,
    norm_ref,
    inv_ref,
    w_hbm,
    out_ref,
    w_buf,
    work,
    mix,
    sems,
):
    f32, bf16 = jnp.float32, jnp.bfloat16
    copies = weight_copies(w_hbm, w_buf, sems)
    for copy in copies:
        copy.start()
    vis = w_hbm.shape[0]
    tokens = grad_ref.shape[1]
    gain = gain_ref[...].astype(f32)
    order = token_order(4 * tokens)
    for half in range(2):
        grads = jnp.concatenate([grad_ref[j * 2 + half] for j in range(4)], axis=0)
        work[half] = dot(order, grads, TN) * gain[:, half * CHUNK : (half + 1) * CHUNK]
    mean = (
        jnp.sum(work[0], axis=1, keepdims=True) + jnp.sum(work[1], axis=1, keepdims=True)
    ) / vis
    along = (
        jnp.sum(work[0] * norm_ref[0], axis=1, keepdims=True)
        + jnp.sum(work[1] * norm_ref[1], axis=1, keepdims=True)
    ) / vis
    inverse = inv_ref[...]
    for half in range(2):
        work[half] = inverse * (work[half] - mean - norm_ref[half] * along)
    total = jnp.zeros((work.shape[1], vis), f32)
    for half in range(2):
        mixed = [jnp.zeros((work.shape[1], CHUNK), f32) for _ in range(3)]
        for kind in range(3):
            mix[kind] = mixed[kind]
        for head in range(CHUNK_HEADS):
            start, stop, low, high = head_window(head)
            grad = head_only(work[half, :, start:stop].astype(bf16), low, high)
            query = head_only(qkv_ref[half * 3, :, start:stop], low, high)
            key = head_only(qkv_ref[half * 3 + 1, :, start:stop], low, high)
            value = qkv_ref[half * 3 + 2, :, start:stop]
            probs = probs_ref[half * CHUNK_HEADS + head]
            grad_weights = dot(grad, value, NT)
            mix[2, :, start:stop] += dot(probs.astype(bf16), grad, TN)
            inner = jnp.sum(grad_weights * probs, axis=1, keepdims=True)
            scores = (probs * (grad_weights - inner) * HDIM ** (-0.5)).astype(bf16)
            mix[0, :, start:stop] += dot(scores, key, NN)
            mix[1, :, start:stop] += dot(scores, query, TN)
        for kind in range(3):
            i = half * 3 + kind
            copies[i].wait()
            total = total + dot(mix[kind].astype(bf16), w_buf[i], NT)
    keep = flag_ref[0] == 1
    for half in range(2):
        columns = slice(half * CHUNK, (half + 1) * CHUNK)
        result = work[half] + total[:, columns]
        out_ref[:, columns] = jnp.where(keep, result, jnp.zeros_like(result)).astype(bf16)


def encoder_backward(flag, w_qkv, ln_gain, qkv, probs, norm, inverse, grad):
    length, vis = norm.shape[1], w_qkv.shape[0]
    bf16, f32 = jnp.bfloat16, jnp.float32
    vmem = pl.BlockSpec(memory_space=pltpu.VMEM)
    return pl.pallas_call(
        encoder_backward_kernel,
        out_shape=jax.ShapeDtypeStruct((length, vis), bf16),
        in_specs=[pl.BlockSpec(memory_space=pltpu.SMEM)]
        + [vmem] * 6
        + [pl.BlockSpec(memory_space=pltpu.HBM)],
        out_specs=vmem,
        scratch_shapes=[
            pltpu.VMEM((6, vis, CHUNK), bf16),
            pltpu.VMEM((2, length, CHUNK), f32),
            pltpu.VMEM((3, length, CHUNK), f32),
            pltpu.SemaphoreType.DMA((6,)),
        ],
        compiler_params=pltpu.CompilerParams(vmem_limit_bytes=40 << 20),
        cost_estimate=pl.CostEstimate(flops=1000, transcendentals=0, bytes_accessed=1000),
        name="encoder_backward",
    )(flag, grad, ln_gain, qkv, probs, norm, inverse, w_qkv)


def split_columns_kernel(bounds, flag_ref, *refs):
    count = len(bounds)
    sources, outs, sems = refs[:-count - 1], refs[-count - 1 : -1], refs[-1]

    @pl.when(flag_ref[0] == 0)
    def _():
        copies = [
            pltpu.make_async_copy(
                sources[which].at[:, pl.ds(start, size)], outs[i], sems.at[i]
            )
            for i, (which, start, size) in enumerate(bounds)
        ]
        for copy in copies:
            copy.start()
        for copy in copies:
            copy.wait()


def split_columns(flag, sources, bounds):
    hbm = pl.BlockSpec(memory_space=pltpu.HBM)
    return pl.pallas_call(
        lambda *refs: split_columns_kernel(bounds, *refs),
        out_shape=tuple(
            jax.ShapeDtypeStruct((sources[which].shape[0], size), sources[which].dtype)
            for which, _, size in bounds
        ),
        in_specs=[pl.BlockSpec(memory_space=pltpu.SMEM)] + [hbm] * len(sources),
        out_specs=(hbm,) * len(bounds),
        scratch_shapes=[pltpu.SemaphoreType.DMA((len(bounds),))],
        name="split_columns",
    )(flag, *sources)


def arrange_in_kernel(flag_ref, order_ref, a_ref, b_ref, out_ref):
    keep = flag_ref[0] == 1
    for r in range(out_ref.shape[0]):
        place = order_ref[r]
        out_ref[r] = jnp.where(keep, a_ref[place], b_ref[place])


def arrange_out_kernel(order_ref, a_ref, b_ref, out_ref):
    for r in range(out_ref.shape[0]):
        value = a_ref[r].astype(jnp.float32) + b_ref[r].astype(jnp.float32)
        out_ref[order_ref[r]] = value.astype(out_ref.dtype)


def arrange(kernel, name, scalars, a, b):
    vmem = pl.BlockSpec(memory_space=pltpu.VMEM)
    return pl.pallas_call(
        kernel,
        out_shape=jax.ShapeDtypeStruct(b.shape, b.dtype),
        in_specs=[pl.BlockSpec(memory_space=pltpu.SMEM)] * len(scalars) + [vmem, vmem],
        out_specs=vmem,
        compiler_params=pltpu.CompilerParams(vmem_limit_bytes=32 << 20),
        name=name,
    )(*scalars, a, b)


def passed_along(block, axis, distance):
    devices = range(lax.axis_size(axis))
    route = [(i - distance, i) for i in devices if i - distance in devices]
    return lax.ppermute(block, axis, route)


def rotated(blocks, shift):
    count = blocks.shape[0]
    step = 1
    while step < count:
        turned = jnp.concatenate([blocks[step:], blocks[:step]], axis=0)
        blocks = jnp.where((shift // step) % 2 == 1, turned, blocks)
        step *= 2
    return blocks


def sent_round(block, distance):
    count = lax.axis_size("dp")
    return lax.ppermute(block, "dp", [(i, (i + 2 * distance) % count) for i in range(count)])


def sent_across(block):
    return lax.ppermute(block, "dp", [(i, i ^ 1) for i in range(lax.axis_size("dp"))])


def sent_tp(block, distance):
    count = lax.axis_size("tp")
    return lax.ppermute(block, "tp", [(i, (i + distance) % count) for i in range(count)])


def per_device(frames, counts, w_qkv, ln_gain, w_proj, rms_gain, cotangent):
    f32, bf16 = jnp.float32, jnp.bfloat16
    is_encoder = lax.axis_index("grp") == 0
    flag = is_encoder.astype(jnp.int32).reshape(1)
    dp_count, tp_count = lax.axis_size("dp"), lax.axis_size("tp")
    pair_count = dp_count // 2
    dp_index, tp_index = lax.axis_index("dp"), lax.axis_index("tp")
    relative = jnp.arange(dp_count, dtype=jnp.int32)
    order = (dp_index // 2 + relative // 2) % pair_count * 2 + (dp_index % 2 ^ relative % 2)

    frame = frames[0, 0]
    tokens_here = frame.shape[0] // 4
    depth = w_proj.shape[1]
    half = w_proj.shape[2] // 2
    first = half * 11 // 16 // 128 * 128
    second = half - first

    w_mine, cot_mine = w_proj[0], cotangent[0]
    give_first, give_second, give_cot = split_columns(
        flag, (w_mine, cot_mine), ((0, 0, first), (0, first, second), (1, 0, half))
    )
    got_first = passed_along(give_first, "grp", -1)
    got_second = passed_along(give_second, "grp", -1)
    got_cot = passed_along(give_cot, "grp", -1)
    got_gain = passed_along(rms_gain[:, :half], "grp", -1)

    embedded, qkv, probs, norm, inverse = encoder_forward(frame, w_qkv[0], ln_gain)

    pieces = embedded
    if depth != CHUNK:
        pieces = embedded.reshape(-1, tokens_here, CHUNK // depth, depth)
        pieces = pieces.transpose(0, 2, 1, 3).reshape(dp_count, tokens_here, depth)
    swapped = lax.all_to_all(pieces, "dp", 0, 0)
    arrived = passed_along(swapped, "grp", 1)
    features = arrange(arrange_in_kernel, "arrange_in", (flag, order), swapped, arrived)
    features = jnp.concatenate(
        [features] + [sent_tp(features, tp_count - s) for s in range(1, tp_count)], axis=1
    ).reshape(pair_count, 2, tp_count * tokens_here, depth)

    w_first = jnp.where(is_encoder, got_first, w_mine[:, half : half + first])
    w_second = jnp.where(is_encoder, got_second, w_mine[:, half + first :])
    cot = jnp.where(is_encoder, got_cot, cot_mine[:, half:])
    gain_rms = jnp.where(is_encoder, got_gain, rms_gain[:, half:])

    def product(block, weight):
        return jnp.einsum("...rk,kc->...rc", block, weight, preferred_element_type=f32)

    away = product(features[:, 1], w_first).astype(bf16)
    away = sent_across(away)
    home = product(features[:, 0], w_first) + away.astype(f32)
    home_sent = home.astype(bf16)
    parts = [sent_round(home_sent[s], s) for s in range(1, pair_count)]
    acts_first = home[0]
    around = [
        sent_round(product(features[s], w_second).astype(bf16), s) for s in range(1, pair_count)
    ]
    both = product(features[0], w_second)
    for block in around:
        both = both + block.astype(f32)
    other = sent_across(both[1].astype(bf16))
    acts_second = both[0] + other.astype(f32)
    for block in parts:
        acts_first = acts_first + block.astype(f32)

    slot = lax.broadcasted_iota(jnp.int32, (1, tokens_here), 1) // TOKF
    live_mask = (slot < rotated(counts, tp_index)[:, None]).astype(f32).reshape(-1, 1)
    cot = rotated(cot.reshape(tp_count, tokens_here, half), tp_index).reshape(-1, half)
    scaled = gain_rms.astype(f32) * cot.astype(f32) * live_mask
    scaled_first, scaled_second = scaled[:, :first], scaled[:, first:]
    squares = jnp.sum(acts_first * acts_first, axis=1) + jnp.sum(acts_second * acts_second, axis=1)
    products = jnp.sum(acts_first * scaled_first, axis=1) + jnp.sum(
        acts_second * scaled_second, axis=1
    )
    sums = jnp.stack([squares, products], axis=1).reshape(tp_count, tokens_here, 2)
    sums = lax.psum(rotated(sums, (tp_count - tp_index) % tp_count), ("grp", "tp"))
    sums = rotated(sums, tp_index).reshape(-1, 2)
    inverse_rms = lax.rsqrt(sums[:, :1] / D + 1e-06)
    fall = inverse_rms**3 * (sums[:, 1:] / D)
    grad_first = (inverse_rms * scaled_first - acts_first * fall).astype(bf16)
    grad_second = (inverse_rms * scaled_second - acts_second * fall).astype(bf16)

    row_first = [grad_first] + [None] * (pair_count - 1)
    for s in range(1, pair_count):
        row_first[pair_count - s] = sent_round(grad_first, s)
    row_first = jnp.stack(row_first)
    duo = jnp.stack([grad_second, sent_across(grad_second)])
    row_first, duo = lax.optimization_barrier((row_first, duo))
    row_first = [row_first, sent_across(row_first)]
    all_second = [duo] + [None] * (pair_count - 1)
    for s in range(1, pair_count):
        all_second[pair_count - s] = sent_round(duo, s)
    all_second = jnp.stack(all_second)

    def back(block, weight):
        return jnp.einsum("prc,kc->prk", block, weight, preferred_element_type=f32)

    terms = [
        back(row_first[j], w_first) + back(all_second[:, j], w_second) for j in range(2)
    ]
    terms = jnp.stack(
        [term.reshape(pair_count, tp_count, tokens_here, depth) for term in terms], axis=1
    ).reshape(dp_count, tp_count, tokens_here, depth)
    total = terms[:, 0]
    for s in range(1, tp_count):
        total = total + sent_tp(terms[:, s].astype(bf16), s).astype(f32)
    total = total.astype(bf16)
    returned = passed_along(total, "grp", -1)
    whole = arrange(arrange_out_kernel, "arrange_out", (order,), total, returned)
    whole = lax.all_to_all(whole, "dp", 0, 0)
    if depth != CHUNK:
        whole = whole.reshape(-1, CHUNK // depth, tokens_here, depth)
        whole = whole.transpose(0, 2, 1, 3).reshape(-1, tokens_here, CHUNK)

    grad_frames = encoder_backward(flag, w_qkv[0], ln_gain, qkv, probs, norm, inverse, whole)
    return grad_frames[None, None]


def solution(mesh):
    placed = (
        P("grp", ("dp", "tp"), None, None),
        P("dp"),
        P("grp", None, None),
        P("grp", None),
        P("grp", "dp", "tp"),
        P("grp", "tp"),
        P("grp", "dp", "tp"),
    )
    return jax.shard_map(
        per_device,
        mesh=mesh,
        in_specs=placed,
        out_specs=P("grp", ("dp", "tp"), None, None),
        check_vma=False,
    )
```

time: 241 us -> 286 us (1.19)
  starting transfers between devices: 53 us -> 134 us
  matrix products: 29.8 us -> 5.3 us
  Pallas kernels: 0 us -> 18.4 us
  local copies, waits for them, and re-layouts: 23.2 us -> 6.17 us
  waiting for transfers between devices: 107 us -> 91.3 us
  blocking collectives: 8.04 us -> 18.9 us
  other arithmetic: 18.7 us -> 9.92 us
    ppermute x6, starting transfers between devices: 11.8 us -> 101 us  [passed_along(): return lax.ppermute(block, axis, route)]
    dot_general x10 -> x4, matrix products: 25.5 us -> 2.55 us  [back(): return jnp.einsum('prc,kc->prk', block, weight, preferred_element_type=f32)]
    pallas_call x0 -> x5, Pallas kernels: none -> 18.4 us  [the longest x1 9.98 us: encoder_backward(): pl.pallas_call(encoder_backward_kernel, out_shape=jax.ShapeDtypeStruct((l...]
    all_to_all x0 -> x1, blocking collectives: none -> 13.2 us  [per_device(): whole = lax.all_to_all(whole, 'dp', 0, 0)]
    all_to_all x1 -> x0, waiting for transfers between devices: 9.75 us -> none  [per_device(): whole = lax.all_to_all(whole, 'dp', 0, 0)]
    slice x3 -> x0, local copies, waits for them, and re-layouts: 6.68 us -> none  [the longest x1 2.86 us: per_device(): got_first = passed_along(w_mine[:, :first], 'grp', -1)]
    all_to_all x1 -> x0, starting transfers between devices: 6.63 us -> none  [per_device(): whole = lax.all_to_all(whole, 'dp', 0, 0)]
    ppermute x4, waiting for transfers between devices: 27.6 us -> 21 us  [sent_across(): lax.ppermute(block, 'dp', [(i, i ^ 1) for i in range(lax.axis_size('dp'))])]
  transfers between devices with their start and end apart: 25 -> 25, of which waited for: 15 -> 14; matrix products, arithmetic and copies ran while one was open for 15% -> 5% of each run, Pallas kernels for 0% -> 3%
where the time goes in v2:
time: 286 us; the launch traced here: 285 us
  starting transfers between devices  134 us (47%)
  waiting for transfers between devices  91.3 us (32%)
  blocking collectives  18.9 us (7%)
  Pallas kernels  18.4 us (6%)
  other arithmetic  9.92 us (3%)
  local copies, waits for them, and re-layouts  6.17 us (2%)
  matrix products  5.3 us (2%)
    ppermute x6, starting transfers between devices, passed_along(): return lax.ppermute(block, axis, route)  101 us
    ppermute x12, waiting for transfers between devices, sent_round(): lax.ppermute(block, 'dp', [(i, (i + 2 * distance) % count) for i in range...  30.6 us
    ppermute x6, waiting for transfers between devices, passed_along(): return lax.ppermute(block, axis, route)  29.7 us
    ppermute x4, waiting for transfers between devices, sent_across(): lax.ppermute(block, 'dp', [(i, i ^ 1) for i in range(lax.axis_size('dp'))])  21 us
    ppermute x12, starting transfers between devices, sent_round(): lax.ppermute(block, 'dp', [(i, (i + 2 * distance) % count) for i in range...  21 us
    all_to_all x1, blocking collectives, per_device(): whole = lax.all_to_all(whole, 'dp', 0, 0)  13.2 us
    pallas_call x1, Pallas kernels, encoder_backward(): pl.pallas_call(encoder_backward_kernel, out_shape=jax.ShapeDtypeStruct((l...  9.98 us
    all_to_all x1, waiting for transfers between devices, per_device(): swapped = lax.all_to_all(pieces, 'dp', 0, 0)  8.24 us
  transfers between devices with their start and end apart: 25, of which 14 were waited for; matrix products, arithmetic and copies ran while one was open for 5% of the time, Pallas kernels for 3%

profile of v2, /device:TPU:0, one launch (start us, length us, event | category | flops | bytes accessed | tf_op | source)
XLA Modules:
  0.0 284.9 jit_solution(16489188110677952519)
XLA Ops:
  6.2 3.8 %copy-done = bf16[1,1280,3840]{2,1,0:T(8,128)(2,1)S(1)} copy-done((bf16[1,1280,3840]{2,1,0:T(8,128)(2,1)S(1)}, bf16[1,1280,3840]{2,1,0:T(8,128)(2,1)}, u32[]{:S(2)}) %copy-start) | copy-done | bytes 9830424
  9.9 7.1 %encoder_forward.1 = (bf16[8,32,640]{2,1,0:T(8,128)(2,1)}, bf16[6,128,640]{2,1,0:T(8,128)(2,1)S(1)}, f32[16,128,128]{2,1,0:T(8,128)S(1)}, f32[2,128,640]{2,1,0:T(8,128)S(1)}, f32[128,1]{1,0:T(8,128)S(1)}) custom-call(bf16[128,1280]{1,0:T(8,128)(2,1)S(1)} %bitcast.116, bf16[1,1280]{1,0:T(2,128)(2,1)S(1)} %copy-done.2, bf16[1280,3840]{1,0:T(8,128)(2,1)S(1)} %bitcast.112), custom_call_target="tpu_custom_call" | custom-call | flops 1000 | bytes 1000 | tf_op jit(solution)/shard_map/encoder_forward/pallas_call | solution.py:103
  17.1 7.3 %all-to-all-start = ((bf16[8,32,640]{2,1,0:T(8,128)(2,1)}), bf16[8,32,640]{2,1,0:T(8,128)(2,1)S(1)}, u32[]{:S(2)}, u32[]{:S(2)}) async-start(bf16[8,32,640]{2,1,0:T(8,128)(2,1)} %get-tuple-element.15), calls=%async_computation | async-start | bytes 655360 | tf_op jit(solution)/shard_map/all_to_all | solution.py:333
  26.4 8.2 %all-to-all-done.a_ref = bf16[8,32,640]{2,1,0:T(8,128)(2,1)S(1)} async-done(((bf16[8,32,640]{2,1,0:T(8,128)(2,1)}), bf16[8,32,640]{2,1,0:T(8,128)(2,1)S(1)}, u32[]{:S(2)}, u32[]{:S(2)}) %all-to-all-start) | async-done | bytes 327712 | tf_op jit(solution)/shard_map/all_to_all | solution.py:333
  34.7 94.7 %collective-permute-start = (bf16[8,32,640]{2,1,0:T(8,128)(2,1)S(1)}, bf16[8,32,640]{2,1,0:T(8,128)(2,1)S(1)}, u32[]{:S(2)}, u32[]{:S(2)}) collective-permute-start(bf16[8,32,640]{2,1,0:T(8,128)(2,1)S(1)} %all-to-all-done.a_ref), channel_id=1, source_target_pairs={{0,16},{1,17},{2,18},{3,19},{4,20},{5,21},{6,22},{7,23},{8,24},{9,... | collective-permute-start | bytes 983048 | tf_op jit(solution)/shard_map/ppermute | solution.py:274
  130.4 3.6 %collective-permute-done.b_ref = bf16[8,32,640]{2,1,0:T(8,128)(2,1)S(1)} collective-permute-done((bf16[8,32,640]{2,1,0:T(8,128)(2,1)S(1)}, bf16[8,32,640]{2,1,0:T(8,128)(2,1)S(1)}, u32[]{:S(2)}, u32[]{:S(2)}) %collective-permute-start) | collective-permute-done | bytes 327712 | tf_op jit(solution)/shard_map/ppermute | solution.py:274
  134.6 1.5 fusion.3
  136.5 2.6 collective-permute-start.10
  139.9 1.8 collective-permute-start.8
  141.8 15.8 %collective-permute-done.2 = bf16[640,1408]{1,0:T(8,128)(2,1)} collective-permute-done((bf16[640,1408]{1,0:T(8,128)(2,1)}, bf16[640,1408]{1,0:T(8,128)(2,1)}, u32[]{:S(2)}, u32[]{:S(2)}) %collective-permute-start.2) | collective-permute-done | bytes 1802272 | tf_op jit(solution)/shard_map/ppermute | solution.py:274
  157.6 2.2 fusion
  160.6 2.4 collective-permute-start.3
  163.5 15.6 %collective-permute-done.3 = bf16[4,64,1408]{2,1,0:T(8,128)(2,1)S(1)} collective-permute-done((bf16[4,64,1408]{2,1,0:T(8,128)(2,1)S(1)}, bf16[4,64,1408]{2,1,0:T(8,128)(2,1)S(1)}, u32[]{:S(2)}, u32[]{:S(2)}) %collective-permute-start.3) | collective-permute-done | bytes 720928 | tf_op jit(solution)/shard_map/ppermute | solution.py:293
  180.0 1.9 collective-permute-start.4
  181.8 2.1 collective-permute-start.6
  185.1 4.2 %collective-permute-done.4 = bf16[64,1408]{1,0:T(8,128)(2,1)S(1)} collective-permute-done((bf16[64,1408]{1,0:T(8,128)(2,1)S(1)}, bf16[64,1408]{1,0:T(8,128)(2,1)S(1)}, u32[]{:S(2)}, u32[]{:S(2)}) %collective-permute-start.4) | collective-permute-done | bytes 180256 | tf_op jit(solution)/shard_map/ppermute | solution.py:289
  189.4 7.9 %collective-permute-done.5 = bf16[64,1408]{1,0:T(8,128)(2,1)S(1)} collective-permute-done((bf16[64,1408]{1,0:T(8,128)(2,1)S(1)}, bf16[64,1408]{1,0:T(8,128)(2,1)S(1)}, u32[]{:S(2)}, u32[]{:S(2)}) %collective-permute-start.5) | collective-permute-done | bytes 180256 | tf_op jit(solution)/shard_map/ppermute | solution.py:289
  198.5 5.8 %psum.7 = f32[2,32,2]{1,2,0:T(2,128)S(1)} all-reduce(f32[2,32,2]{1,2,0:T(2,128)S(1)} %maximum_select_fusion), channel_id=1, replica_groups=mesh['grp'=2,'dp'=8,'tp'=2] {'grp','tp'}, use_global_device_ids=true, to_apply=%region_4.5 | all-reduce | flops 128 | bytes 1024 | tf_op jit(solution)/shard_map/psum | solution.py:375
  205.4 1.6 collective-permute-start.17
  208.2 2.2 collective-permute-start.15
  210.4 1.6 collective-permute-start.14
  212.0 5.5 %collective-permute-done.16 = bf16[64,1408]{1,0:T(8,128)(2,1)S(1)} collective-permute-done((bf16[64,1408]{1,0:T(8,128)(2,1)S(1)}, bf16[64,1408]{1,0:T(8,128)(2,1)S(1)}, u32[]{:S(2)}, u32[]{:S(2)}) %collective-permute-start.16) | collective-permute-done | bytes 180256 | tf_op jit(solution)/shard_map/ppermute | solution.py:289
  217.6 6.3 %collective-permute-done.15 = bf16[64,1408]{1,0:T(8,128)(2,1)S(1)} collective-permute-done((bf16[64,1408]{1,0:T(8,128)(2,1)S(1)}, bf16[64,1408]{1,0:T(8,128)(2,1)S(1)}, u32[]{:S(2)}, u32[]{:S(2)}) %collective-permute-start.15) | collective-permute-done | bytes 180256 | tf_op jit(solution)/shard_map/ppermute | solution.py:289
  224.0 5.2 %collective-permute-start.20 = (bf16[2,64,640]{2,1,0:T(8,128)(2,1)S(1)}, bf16[2,64,640]{2,1,0:T(8,128)(2,1)S(1)}, u32[]{:S(2)}, u32[]{:S(2)}) collective-permute-start(bf16[2,64,640]{2,1,0:T(8,128)(2,1)S(1)} %pad_maximum_fusion.5), channel_id=1, source_target_pairs={{0,4},{2,6},{4,8},{6,10},{8,12},{10,14},{12,0},{14,2},{1,5},{3,7},... | collective-permute-start | bytes 491528 | tf_op jit(solution)/shard_map/ppermute | solution.py:289
  229.2 2.4 collective-permute-start.18
  232.2 1.6 collective-permute-done.20
  233.8 5.0 %collective-permute-done.19 = bf16[2,64,640]{2,1,0:T(8,128)(2,1)S(1)} collective-permute-done((bf16[2,64,640]{2,1,0:T(8,128)(2,1)S(1)}, bf16[2,64,640]{2,1,0:T(8,128)(2,1)S(1)}, u32[]{:S(2)}, u32[]{:S(2)}) %collective-permute-start.19) | collective-permute-done | bytes 163872 | tf_op jit(solution)/shard_map/ppermute | solution.py:289
  241.1 5.4 %collective-permute-done.21 = bf16[4,64,1408]{2,1,0:T(8,128)(2,1)S(1)} collective-permute-done((bf16[4,64,1408]{2,1,0:T(8,128)(2,1)S(1)}, bf16[4,64,1408]{2,1,0:T(8,128)(2,1)S(1)}, u32[]{:S(2)}, u32[]{:S(2)}) %collective-permute-start.21) | collective-permute-done | bytes 720928 | tf_op jit(solution)/shard_map/ppermute | solution.py:293
  247.7 1.6 collective-permute-done.22
  250.6 10.3 %collective-permute-done.23.b_ref = bf16[8,32,640]{2,1,0:T(8,128)(2,1)S(1)} collective-permute-done((bf16[8,32,640]{2,1,0:T(8,128)(2,1)S(1)}, bf16[8,32,640]{2,1,0:T(8,128)(2,1)S(1)}, u32[]{:S(2)}, u32[]{:S(2)}) %collective-permute-start.23) | collective-permute-done | bytes 327712 | tf_op jit(solution)/shard_map/ppermute | solution.py:274
  261.6 13.2 %all_to_all.10.grad_ref = bf16[8,32,640]{2,1,0:T(8,128)(2,1)S(1)} all-to-all(bf16[8,32,640]{2,1,0:T(8,128)(2,1)S(1)} %arrange_out.1), channel_id=1, replica_groups=mesh['grp'=2,'dp'=8,'tp'=2] {'dp'}, dimensions={0} | all-to-all | bytes 655360 | tf_op jit(solution)/shard_map/all_to_all | solution.py:409
  274.8 10.0 %encoder_backward.1 = bf16[128,1280]{1,0:T(8,128)(2,1)} custom-call(s32[1]{0:T(128)} %bitcast.flag_ref.refs_0_, bf16[8,32,640]{2,1,0:T(8,128)(2,1)S(1)} %all_to_all.10.grad_ref, bf16[1,1280]{1,0:T(2,128)(2,1)S(1)} %copy-done.2, bf16[6,128,640]{2,1,0:T(8,128)(2,1)S(1)} %get-tuple-element.21.qkv_ref, f32[16,128,128]{2,1,0:T(8,128)S(1)} %get-tuple-element.22.probs_ref, ...), custom_call_target="tpu_custom_call" | custom-call | flops 1000 | bytes 1000 | tf_op jit(solution)/shard_map/encoder_backward/pallas_call | solution.py:194
  (102 shorter events, 23.7 us)
Async XLA Ops:
  0.7 25.7 %collective-permute-start.12 = (bf16[1,2048]{1,0:T(2,128)(2,1)S(1)}, bf16[1,2048]{1,0:T(2,128)(2,1)S(1)}, u32[]{:S(2)}, u32[]{:S(2)}) collective-permute-start(bf16[1,2048]{1,0:T(2,128)(2,1)S(1)} %slice.131), channel_id=1, source_target_pairs={{16,0},{17,1},{18,2},{19,3},{20,4},{21,5},{22,6},{23,7},{24,8},{25... | collective-permute-start | bytes 12296 | tf_op jit(solution)/shard_map/ppermute | solution.py:274
  2.1 127.3 %collective-permute-start.13 = (bf16[64,2048]{1,0:T(8,128)(2,1)}, bf16[64,2048]{1,0:T(8,128)(2,1)S(1)}, u32[]{:S(2)}, u32[]{:S(2)}) collective-permute-start(bf16[64,2048]{1,0:T(8,128)(2,1)} %get-tuple-element.18), channel_id=1, source_target_pairs={{16,0},{17,1},{18,2},{19,3},{20,4},{21,5},{22,6},{23,7},{24,8},{25... | collective-permute-start | bytes 786440 | tf_op jit(solution)/shard_map/ppermute | solution.py:274
  3.5 131.1 %collective-permute-start.7 = (bf16[640,640]{1,0:T(8,128)(2,1)}, bf16[640,640]{1,0:T(8,128)(2,1)}, u32[]{:S(2)}, u32[]{:S(2)}) collective-permute-start(bf16[640,640]{1,0:T(8,128)(2,1)} %get-tuple-element.17), channel_id=1, source_target_pairs={{16,0},{17,1},{18,2},{19,3},{20,4},{21,5},{22,6},{23,7},{24,8},{25... | collective-permute-start | bytes 2457608 | tf_op jit(solution)/shard_map/ppermute | solution.py:274
  4.8 152.8 %collective-permute-start.2 = (bf16[640,1408]{1,0:T(8,128)(2,1)}, bf16[640,1408]{1,0:T(8,128)(2,1)}, u32[]{:S(2)}, u32[]{:S(2)}) collective-permute-start(bf16[640,1408]{1,0:T(8,128)(2,1)} %get-tuple-element.16), channel_id=1, source_target_pairs={{16,0},{17,1},{18,2},{19,3},{20,4},{21,5},{22,6},{23,7},{24,8},{25... | collective-permute-start | bytes 5406728 | tf_op jit(solution)/shard_map/ppermute | solution.py:274
  17.1 17.6 %all-to-all-start = ((bf16[8,32,640]{2,1,0:T(8,128)(2,1)}), bf16[8,32,640]{2,1,0:T(8,128)(2,1)S(1)}, u32[]{:S(2)}, u32[]{:S(2)}) async-start(bf16[8,32,640]{2,1,0:T(8,128)(2,1)} %get-tuple-element.15), calls=%async_computation | async-start | bytes 655360 | tf_op jit(solution)/shard_map/all_to_all | solution.py:333
  34.7 99.2 %collective-permute-start = (bf16[8,32,640]{2,1,0:T(8,128)(2,1)S(1)}, bf16[8,32,640]{2,1,0:T(8,128)(2,1)S(1)}, u32[]{:S(2)}, u32[]{:S(2)}) collective-permute-start(bf16[8,32,640]{2,1,0:T(8,128)(2,1)S(1)} %all-to-all-done.a_ref), channel_id=1, source_target_pairs={{0,16},{1,17},{2,18},{3,19},{4,20},{5,21},{6,22},{7,23},{8,24},{9,... | collective-permute-start | bytes 983048 | tf_op jit(solution)/shard_map/ppermute | solution.py:274
  134.5 1.7 collective-permute-start.1
  136.1 26.9 %copy-start.5 = (bf16[640,640,1]{1,0,2:T(8,128)(2,1)}, bf16[640,640,1]{1,0,2:T(8,128)(2,1)S(1)}, u32[]{:S(2)}) copy-start(bf16[640,640,1]{1,0,2:T(8,128)(2,1)S(1)} %fusion.3) | copy-start | bytes 2457604
  136.5 26.5 %collective-permute-start.10 = (bf16[2,64,640]{2,1,0:T(8,128)(2,1)S(1)}, bf16[2,64,640]{2,1,0:T(8,128)(2,1)S(1)}, u32[]{:S(2)}, u32[]{:S(2)}) collective-permute-start(bf16[2,64,640]{2,1,0:T(8,128)(2,1)S(1)} %convolution_convert_fusion.1), channel_id=1, source_target_pairs={{0,12},{2,14},{4,0},{6,2},{8,4},{10,6},{12,8},{14,10},{1,13},{3,15... | collective-permute-start | bytes 491528 | tf_op jit(solution)/shard_map/ppermute | solution.py:289
  139.5 23.5 %collective-permute-start.9 = (bf16[2,64,640]{2,1,0:T(8,128)(2,1)S(1)}, bf16[2,64,640]{2,1,0:T(8,128)(2,1)S(1)}, u32[]{:S(2)}, u32[]{:S(2)}) collective-permute-start(bf16[2,64,640]{2,1,0:T(8,128)(2,1)S(1)} %convolution_convert_fusion.2), channel_id=1, source_target_pairs={{0,8},{2,10},{4,12},{6,14},{8,0},{10,2},{12,4},{14,6},{1,9},{3,11}... | collective-permute-start | bytes 491528 | tf_op jit(solution)/shard_map/ppermute | solution.py:289
  139.9 23.2 %collective-permute-start.8 = (bf16[2,64,640]{2,1,0:T(8,128)(2,1)S(1)}, bf16[2,64,640]{2,1,0:T(8,128)(2,1)S(1)}, u32[]{:S(2)}, u32[]{:S(2)}) collective-permute-start(bf16[2,64,640]{2,1,0:T(8,128)(2,1)S(1)} %convolution_convert_fusion.3), channel_id=1, source_target_pairs={{0,4},{2,6},{4,8},{6,10},{8,12},{10,14},{12,0},{14,2},{1,5},{3,7},... | collective-permute-start | bytes 491528 | tf_op jit(solution)/shard_map/ppermute | solution.py:289
  159.8 19.3 %copy-start.3 = (bf16[640,1408,1]{1,0,2:T(8,128)(2,1)}, bf16[640,1408,1]{1,0,2:T(8,128)(2,1)S(1)}, u32[]{:S(2)}) copy-start(bf16[640,1408,1]{1,0,2:T(8,128)(2,1)S(1)} %fusion) | copy-start | bytes 5406724
  160.6 18.6 %collective-permute-start.3 = (bf16[4,64,1408]{2,1,0:T(8,128)(2,1)S(1)}, bf16[4,64,1408]{2,1,0:T(8,128)(2,1)S(1)}, u32[]{:S(2)}, u32[]{:S(2)}) collective-permute-start(bf16[4,64,1408]{2,1,0:T(8,128)(2,1)S(1)} %convolution_convert_fusion), channel_id=1, source_target_pairs={{0,2},{2,0},{4,6},{6,4},{8,10},{10,8},{12,14},{14,12},{1,3},{3,1},... | collective-permute-start | bytes 2162696 | tf_op jit(solution)/shard_map/ppermute | solution.py:293
  163.4 21.6 %copy-start.7 = (f32[2,64,640]{2,1,0:T(8,128)}, f32[2,64,640]{2,1,0:T(8,128)S(1)}, u32[]{:S(2)}) copy-start(f32[2,64,640]{2,1,0:T(8,128)S(1)} %fusion.2) | copy-start | bytes 983044
  163.4 21.6 %collective-permute-start.11 = (bf16[64,640]{1,0:T(8,128)(2,1)S(1)}, bf16[64,640]{1,0:T(8,128)(2,1)S(1)}, u32[]{:S(2)}, u32[]{:S(2)}) collective-permute-start(bf16[64,640]{1,0:T(8,128)(2,1)S(1)} %fusion.13), channel_id=1, source_target_pairs={{0,2},{2,0},{4,6},{6,4},{8,10},{10,8},{12,14},{14,12},{1,3},{3,1},... | collective-permute-start | bytes 245768 | tf_op jit(solution)/shard_map/ppermute | solution.py:293
  180.0 9.4 %collective-permute-start.4 = (bf16[64,1408]{1,0:T(8,128)(2,1)S(1)}, bf16[64,1408]{1,0:T(8,128)(2,1)S(1)}, u32[]{:S(2)}, u32[]{:S(2)}) collective-permute-start(bf16[64,1408]{1,0:T(8,128)(2,1)S(1)} %get-tuple-element.30), channel_id=1, source_target_pairs={{0,4},{2,6},{4,8},{6,10},{8,12},{10,14},{12,0},{14,2},{1,5},{3,7},... | collective-permute-start | bytes 540680 | tf_op jit(solution)/shard_map/ppermute | solution.py:289
  181.8 7.6 %collective-permute-start.6 = (bf16[64,1408]{1,0:T(8,128)(2,1)S(1)}, bf16[64,1408]{1,0:T(8,128)(2,1)S(1)}, u32[]{:S(2)}, u32[]{:S(2)}) collective-permute-start(bf16[64,1408]{1,0:T(8,128)(2,1)S(1)} %get-tuple-element.31), channel_id=1, source_target_pairs={{0,12},{2,14},{4,0},{6,2},{8,4},{10,6},{12,8},{14,10},{1,13},{3,15... | collective-permute-start | bytes 540680 | tf_op jit(solution)/shard_map/ppermute | solution.py:289
  183.9 13.4 %collective-permute-start.5 = (bf16[64,1408]{1,0:T(8,128)(2,1)S(1)}, bf16[64,1408]{1,0:T(8,128)(2,1)S(1)}, u32[]{:S(2)}, u32[]{:S(2)}) collective-permute-start(bf16[64,1408]{1,0:T(8,128)(2,1)S(1)} %get-tuple-element.32), channel_id=1, source_target_pairs={{0,8},{2,10},{4,12},{6,14},{8,0},{10,2},{12,4},{14,6},{1,9},{3,11}... | collective-permute-start | bytes 540680 | tf_op jit(solution)/shard_map/ppermute | solution.py:289
  205.4 6.6 %collective-permute-start.17 = (bf16[64,640]{1,0:T(8,128)(2,1)S(1)}, bf16[64,640]{1,0:T(8,128)(2,1)S(1)}, u32[]{:S(2)}, u32[]{:S(2)}) collective-permute-start(bf16[64,640]{1,0:T(8,128)(2,1)S(1)} %subtract_convert_fusion.1), channel_id=1, source_target_pairs={{0,2},{2,0},{4,6},{6,4},{8,10},{10,8},{12,14},{14,12},{1,3},{3,1},... | collective-permute-start | bytes 245768 | tf_op jit(solution)/shard_map/ppermute | solution.py:293
  208.1 9.4 %collective-permute-start.16 = (bf16[64,1408]{1,0:T(8,128)(2,1)S(1)}, bf16[64,1408]{1,0:T(8,128)(2,1)S(1)}, u32[]{:S(2)}, u32[]{:S(2)}) collective-permute-start(bf16[64,1408]{1,0:T(8,128)(2,1)S(1)} %subtract_convert_fusion), channel_id=1, source_target_pairs={{0,4},{2,6},{4,8},{6,10},{8,12},{10,14},{12,0},{14,2},{1,5},{3,7},... | collective-permute-start | bytes 540680 | tf_op jit(solution)/shard_map/ppermute | solution.py:289
  208.2 15.7 %collective-permute-start.15 = (bf16[64,1408]{1,0:T(8,128)(2,1)S(1)}, bf16[64,1408]{1,0:T(8,128)(2,1)S(1)}, u32[]{:S(2)}, u32[]{:S(2)}) collective-permute-start(bf16[64,1408]{1,0:T(8,128)(2,1)S(1)} %subtract_convert_fusion), channel_id=1, source_target_pairs={{0,8},{2,10},{4,12},{6,14},{8,0},{10,2},{12,4},{14,6},{1,9},{3,11}... | collective-permute-start | bytes 540680 | tf_op jit(solution)/shard_map/ppermute | solution.py:289
  210.4 13.4 %collective-permute-start.14 = (bf16[64,1408]{1,0:T(8,128)(2,1)S(1)}, bf16[64,1408]{1,0:T(8,128)(2,1)S(1)}, u32[]{:S(2)}, u32[]{:S(2)}) collective-permute-start(bf16[64,1408]{1,0:T(8,128)(2,1)S(1)} %subtract_convert_fusion), channel_id=1, source_target_pairs={{0,12},{2,14},{4,0},{6,2},{8,4},{10,6},{12,8},{14,10},{1,13},{3,15... | collective-permute-start | bytes 540680 | tf_op jit(solution)/shard_map/ppermute | solution.py:289
  212.0 26.9 %copy-start.6 = (bf16[640,640,1]{1,0,2:T(8,128)(2,1)S(1)}, bf16[640,640,1]{1,0,2:T(8,128)(2,1)}, u32[]{:S(2)}) copy-start(bf16[640,640,1]{1,0,2:T(8,128)(2,1)} %copy-done.5) | copy-start | bytes 2457604
  224.0 9.8 %collective-permute-start.20 = (bf16[2,64,640]{2,1,0:T(8,128)(2,1)S(1)}, bf16[2,64,640]{2,1,0:T(8,128)(2,1)S(1)}, u32[]{:S(2)}, u32[]{:S(2)}) collective-permute-start(bf16[2,64,640]{2,1,0:T(8,128)(2,1)S(1)} %pad_maximum_fusion.5), channel_id=1, source_target_pairs={{0,4},{2,6},{4,8},{6,10},{8,12},{10,14},{12,0},{14,2},{1,5},{3,7},... | collective-permute-start | bytes 491528 | tf_op jit(solution)/shard_map/ppermute | solution.py:289
  229.2 9.6 %collective-permute-start.19 = (bf16[2,64,640]{2,1,0:T(8,128)(2,1)S(1)}, bf16[2,64,640]{2,1,0:T(8,128)(2,1)S(1)}, u32[]{:S(2)}, u32[]{:S(2)}) collective-permute-start(bf16[2,64,640]{2,1,0:T(8,128)(2,1)S(1)} %pad_maximum_fusion.5), channel_id=1, source_target_pairs={{0,8},{2,10},{4,12},{6,14},{8,0},{10,2},{12,4},{14,6},{1,9},{3,11}... | collective-permute-start | bytes 491528 | tf_op jit(solution)/shard_map/ppermute | solution.py:289
  229.2 9.6 %collective-permute-start.18 = (bf16[2,64,640]{2,1,0:T(8,128)(2,1)S(1)}, bf16[2,64,640]{2,1,0:T(8,128)(2,1)S(1)}, u32[]{:S(2)}, u32[]{:S(2)}) collective-permute-start(bf16[2,64,640]{2,1,0:T(8,128)(2,1)S(1)} %pad_maximum_fusion.5), channel_id=1, source_target_pairs={{0,12},{2,14},{4,0},{6,2},{8,4},{10,6},{12,8},{14,10},{1,13},{3,15... | collective-permute-start | bytes 491528 | tf_op jit(solution)/shard_map/ppermute | solution.py:289
  231.6 14.9 %collective-permute-start.21 = (bf16[4,64,1408]{2,1,0:T(8,128)(2,1)S(1)}, bf16[4,64,1408]{2,1,0:T(8,128)(2,1)S(1)}, u32[]{:S(2)}, u32[]{:S(2)}) collective-permute-start(bf16[4,64,1408]{2,1,0:T(8,128)(2,1)S(1)} %pad_maximum_fusion.1), channel_id=1, source_target_pairs={{0,2},{2,0},{4,6},{6,4},{8,10},{10,8},{12,14},{14,12},{1,3},{3,1},... | collective-permute-start | bytes 2162696 | tf_op jit(solution)/shard_map/ppermute | solution.py:293
  238.9 35.9 %slice-start = ((s8[9830400]{0:T(1024)(128)(4,1)}), s8[4194304]{0:T(1024)(128)(4,1)S(1)}, s32[]{:S(2)}) async-start(s8[9830400]{0:T(1024)(128)(4,1)} %bitcast.113), calls=%async_computation.2 | async-start | bytes 8388608
  240.3 34.5 %slice-start.1 = ((s8[9830400]{0:T(1024)(128)(4,1)}), s8[4194304]{0:T(1024)(128)(4,1)S(1)}, s32[]{:S(2)}) async-start(s8[9830400]{0:T(1024)(128)(4,1)} %bitcast.113), calls=%async_computation.3 | async-start | bytes 8388608
  247.3 27.5 %slice-start.2 = ((s8[9830400]{0:T(1024)(128)(4,1)}), s8[1441792]{0:T(1024)(128)(4,1)S(1)}, s32[]{:S(2)}) async-start(s8[9830400]{0:T(1024)(128)(4,1)} %bitcast.113), calls=%async_computation.4 | async-start | bytes 2883584
  247.6 1.7 collective-permute-start.22
  249.3 11.6 %collective-permute-start.23 = (bf16[8,32,640]{2,1,0:T(8,128)(2,1)S(1)}, bf16[8,32,640]{2,1,0:T(8,128)(2,1)S(1)}, u32[]{:S(2)}, u32[]{:S(2)}) collective-permute-start(bf16[8,32,640]{2,1,0:T(8,128)(2,1)S(1)} %fusion.5.a_ref), channel_id=1, source_target_pairs={{16,0},{17,1},{18,2},{19,3},{20,4},{21,5},{22,6},{23,7},{24,8},{25... | collective-permute-start | bytes 983048 | tf_op jit(solution)/shard_map/ppermute | solution.py:274
  (6 other events, 44.4 us)

commit v3 on v2

v3 whole, which is shorter than its diff:
```python
import jax
import jax.numpy as jnp
from jax import lax
from jax.experimental import pallas as pl
from jax.experimental.pallas import tpu as pltpu
from jax.sharding import PartitionSpec as P

HEADS = 16
HDIM = 80
D = 8192
TOKF = 32
FIRST_PART = 9
GAIN_ROWS = 16
CHUNK = 640
CHUNK_HEADS = CHUNK // HDIM


def head_window(head):
    low, high = head * HDIM, (head + 1) * HDIM
    start, stop = low // 128 * 128, -(-high // 128) * 128
    return start, stop, low - start, high - start


def head_only(block, low, high):
    lane = lax.broadcasted_iota(jnp.int32, block.shape, 1)
    return jnp.where((lane >= low) & (lane < high), block, jnp.zeros_like(block))


def dot(a, b, dims):
    return lax.dot_general(a, b, (dims, ((), ())), preferred_element_type=jnp.float32)


NT = ((1,), (1,))
NN = ((1,), (0,))
TN = ((0,), (0,))


def token_order(length):
    row = lax.broadcasted_iota(jnp.int32, (length, length), 0)
    column = lax.broadcasted_iota(jnp.int32, (length, length), 1)
    tokens = length // 4
    return (row % tokens * 4 + row // tokens == column).astype(jnp.bfloat16)


def weight_copies(w_hbm, w_buf, sems):
    return [
        pltpu.make_async_copy(
            w_hbm.at[:, pl.ds(((i % 3) * 2 + i // 3) * CHUNK, CHUNK)], w_buf.at[i], sems.at[i]
        )
        for i in range(6)
    ]


def encoder_forward_kernel(
    flag_ref,
    x_ref,
    gain_ref,
    w_hbm,
    emb_ref,
    qkv_hbm,
    probs_hbm,
    norm_hbm,
    inv_ref,
    w_buf,
    qkv_ref,
    probs_ref,
    norm_ref,
    work,
    sems,
    out_sems,
):
    @pl.when(flag_ref[0] == 1)
    def _():
        copies = weight_copies(w_hbm, w_buf, sems)
        for copy in copies:
            copy.start()
        outs = []
        x = x_ref[...]
        vis = x.shape[1]
        for half in range(2):
            for kind in range(3):
                i = half * 3 + kind
                copies[i].wait()
                qkv_ref[i] = dot(x, w_buf[i], NN).astype(jnp.bfloat16)
            heads = pl.ds(half * CHUNK_HEADS, CHUNK_HEADS)
            outs.append(
                pltpu.make_async_copy(
                    qkv_ref.at[pl.ds(half * 3, 3)],
                    qkv_hbm.at[pl.ds(half * 3, 3)],
                    out_sems.at[half],
                )
            )
            outs[-1].start()
            work[half] = x[:, half * CHUNK : (half + 1) * CHUNK].astype(jnp.float32)
            for head in range(CHUNK_HEADS):
                start, stop, low, high = head_window(head)
                query = qkv_ref[half * 3, :, start:stop]
                key = head_only(qkv_ref[half * 3 + 1, :, start:stop], low, high)
                value = head_only(qkv_ref[half * 3 + 2, :, start:stop], low, high)
                scores = dot(query, key, NT) * HDIM ** (-0.5)
                weights = jnp.exp(scores - jnp.max(scores, axis=1, keepdims=True))
                weights = weights / jnp.sum(weights, axis=1, keepdims=True)
                probs_ref[half * CHUNK_HEADS + head] = weights
                work[half, :, start:stop] += dot(weights.astype(jnp.bfloat16), value, NN)
            outs.append(
                pltpu.make_async_copy(probs_ref.at[heads], probs_hbm.at[heads], out_sems.at[2 + half])
            )
            outs[-1].start()
        first, second = work[0], work[1]
        mean = (
            jnp.sum(first, axis=1, keepdims=True) + jnp.sum(second, axis=1, keepdims=True)
        ) / vis
        first, second = first - mean, second - mean
        variance = (
            jnp.sum(first * first, axis=1, keepdims=True)
            + jnp.sum(second * second, axis=1, keepdims=True)
        ) / vis
        inverse = lax.rsqrt(variance + 1e-06)
        inv_ref[...] = inverse
        gain = gain_ref[...].astype(jnp.float32)
        tokens = x.shape[0] // 4
        order = token_order(x.shape[0])
        for half, centred in enumerate((first, second)):
            normal = centred * inverse
            norm_ref[half] = normal
            embedded = (normal * gain[:, half * CHUNK : (half + 1) * CHUNK]).astype(jnp.bfloat16)
            embedded = dot(order, embedded, NN).astype(jnp.bfloat16)
            for j in range(4):
                emb_ref[j * 2 + half] = embedded[j * tokens : (j + 1) * tokens]
        outs.append(pltpu.make_async_copy(norm_ref, norm_hbm, out_sems.at[4]))
        outs[-1].start()
        for copy in outs:
            copy.wait()


def encoder_forward(flag, frame, w_qkv, ln_gain):
    length, vis = frame.shape
    bf16, f32 = jnp.bfloat16, jnp.float32
    vmem = pl.BlockSpec(memory_space=pltpu.VMEM)
    hbm = pl.BlockSpec(memory_space=pltpu.HBM)
    return pl.pallas_call(
        encoder_forward_kernel,
        out_shape=(
            jax.ShapeDtypeStruct((8, length // 4, CHUNK), bf16),
            jax.ShapeDtypeStruct((6, length, CHUNK), bf16),
            jax.ShapeDtypeStruct((HEADS, length, length), f32),
            jax.ShapeDtypeStruct((2, length, CHUNK), f32),
            jax.ShapeDtypeStruct((length, 1), f32),
        ),
        in_specs=[pl.BlockSpec(memory_space=pltpu.SMEM), vmem, vmem, hbm],
        out_specs=(vmem, hbm, hbm, hbm, vmem),
        scratch_shapes=[
            pltpu.VMEM((6, vis, CHUNK), bf16),
            pltpu.VMEM((6, length, CHUNK), bf16),
            pltpu.VMEM((HEADS, length, length), f32),
            pltpu.VMEM((2, length, CHUNK), f32),
            pltpu.VMEM((2, length, CHUNK), f32),
            pltpu.SemaphoreType.DMA((6,)),
            pltpu.SemaphoreType.DMA((5,)),
        ],
        compiler_params=pltpu.CompilerParams(vmem_limit_bytes=40 << 20),
        cost_estimate=pl.CostEstimate(flops=1000, transcendentals=0, bytes_accessed=1000),
        name="encoder_forward",
    )(flag, frame, ln_gain, in_hbm(w_qkv))


def encoder_backward_kernel(
    flag_ref,
    grad_ref,
    gain_ref,
    qkv_ref,
    probs_ref,
    norm_ref,
    inv_ref,
    w_hbm,
    out_ref,
    w_buf,
    work,
    mix,
    sems,
):
    @pl.when(flag_ref[0] == 0)
    def _():
        out_ref[...] = jnp.zeros_like(out_ref)

    @pl.when(flag_ref[0] == 1)
    def _():
        f32, bf16 = jnp.float32, jnp.bfloat16
        copies = weight_copies(w_hbm, w_buf, sems)
        for copy in copies:
            copy.start()
        vis = w_hbm.shape[0]
        tokens = grad_ref.shape[1]
        gain = gain_ref[...].astype(f32)
        order = token_order(4 * tokens)
        for half in range(2):
            grads = jnp.concatenate([grad_ref[j * 2 + half] for j in range(4)], axis=0)
            work[half] = dot(order, grads, TN) * gain[:, half * CHUNK : (half + 1) * CHUNK]
        mean = (
            jnp.sum(work[0], axis=1, keepdims=True) + jnp.sum(work[1], axis=1, keepdims=True)
        ) / vis
        along = (
            jnp.sum(work[0] * norm_ref[0], axis=1, keepdims=True)
            + jnp.sum(work[1] * norm_ref[1], axis=1, keepdims=True)
        ) / vis
        inverse = inv_ref[...]
        for half in range(2):
            work[half] = inverse * (work[half] - mean - norm_ref[half] * along)
        total = jnp.zeros((work.shape[1], vis), f32)
        for half in range(2):
            mixed = [jnp.zeros((work.shape[1], CHUNK), f32) for _ in range(3)]
            for kind in range(3):
                mix[kind] = mixed[kind]
            for head in range(CHUNK_HEADS):
                start, stop, low, high = head_window(head)
                grad = head_only(work[half, :, start:stop].astype(bf16), low, high)
                query = head_only(qkv_ref[half * 3, :, start:stop], low, high)
                key = head_only(qkv_ref[half * 3 + 1, :, start:stop], low, high)
                value = qkv_ref[half * 3 + 2, :, start:stop]
                probs = probs_ref[half * CHUNK_HEADS + head]
                grad_weights = dot(grad, value, NT)
                mix[2, :, start:stop] += dot(probs.astype(bf16), grad, TN)
                inner = jnp.sum(grad_weights * probs, axis=1, keepdims=True)
                scores = (probs * (grad_weights - inner) * HDIM ** (-0.5)).astype(bf16)
                mix[0, :, start:stop] += dot(scores, key, NN)
                mix[1, :, start:stop] += dot(scores, query, TN)
            for kind in range(3):
                i = half * 3 + kind
                copies[i].wait()
                total = total + dot(mix[kind].astype(bf16), w_buf[i], NT)
        for half in range(2):
            columns = slice(half * CHUNK, (half + 1) * CHUNK)
            out_ref[:, columns] = (work[half] + total[:, columns]).astype(bf16)


def encoder_backward(flag, w_qkv, ln_gain, qkv, probs, norm, inverse, grad):
    length, vis = norm.shape[1], w_qkv.shape[0]
    bf16, f32 = jnp.bfloat16, jnp.float32
    vmem = pl.BlockSpec(memory_space=pltpu.VMEM)
    return pl.pallas_call(
        encoder_backward_kernel,
        out_shape=jax.ShapeDtypeStruct((length, vis), bf16),
        in_specs=[pl.BlockSpec(memory_space=pltpu.SMEM)]
        + [vmem] * 6
        + [pl.BlockSpec(memory_space=pltpu.HBM)],
        out_specs=vmem,
        scratch_shapes=[
            pltpu.VMEM((6, vis, CHUNK), bf16),
            pltpu.VMEM((2, length, CHUNK), f32),
            pltpu.VMEM((3, length, CHUNK), f32),
            pltpu.SemaphoreType.DMA((6,)),
        ],
        compiler_params=pltpu.CompilerParams(vmem_limit_bytes=40 << 20),
        cost_estimate=pl.CostEstimate(flops=1000, transcendentals=0, bytes_accessed=1000),
        name="encoder_backward",
    )(flag, grad, ln_gain, qkv, probs, norm, inverse, in_hbm(w_qkv))


def give_columns_kernel(start, flag_ref, after_ref, w_hbm, out_ref, sem):
    @pl.when(flag_ref[0] == 0)
    def _():
        copy = pltpu.make_async_copy(w_hbm.at[:, pl.ds(start, out_ref.shape[1])], out_ref, sem)
        copy.start()
        copy.wait()


def give_columns(flag, after, matrix, start, size):
    return pl.pallas_call(
        lambda *refs: give_columns_kernel(start, *refs),
        out_shape=jax.ShapeDtypeStruct((matrix.shape[0], size), matrix.dtype),
        in_specs=[
            pl.BlockSpec(memory_space=pltpu.SMEM),
            pl.BlockSpec(memory_space=pl.ANY),
            pl.BlockSpec(memory_space=pltpu.HBM),
        ],
        out_specs=pl.BlockSpec(memory_space=pltpu.VMEM),
        scratch_shapes=[pltpu.SemaphoreType.DMA],
        compiler_params=pltpu.CompilerParams(vmem_limit_bytes=16 << 20),
        cost_estimate=pl.CostEstimate(flops=1000, transcendentals=0, bytes_accessed=1000),
        name="give_columns",
    )(flag, after, in_hbm(matrix))


def give_cotangent_kernel(flag_ref, after_ref, gain_ref, cot_hbm, out_ref, sem):
    @pl.when(flag_ref[0] == 0)
    def _():
        rows, size = cot_hbm.shape[0], out_ref.shape[1]
        copy = pltpu.make_async_copy(
            cot_hbm.at[:, pl.ds(0, size)], out_ref.at[pl.ds(0, rows)], sem
        )
        copy.start()
        out_ref[rows:] = jnp.broadcast_to(gain_ref[:, :size], (GAIN_ROWS, size))
        copy.wait()


def give_cotangent(flag, after, gain, cot, size):
    return pl.pallas_call(
        give_cotangent_kernel,
        out_shape=jax.ShapeDtypeStruct((cot.shape[0] + GAIN_ROWS, size), cot.dtype),
        in_specs=[
            pl.BlockSpec(memory_space=pltpu.SMEM),
            pl.BlockSpec(memory_space=pl.ANY),
            pl.BlockSpec(memory_space=pltpu.VMEM),
            pl.BlockSpec(memory_space=pltpu.HBM),
        ],
        out_specs=pl.BlockSpec(memory_space=pltpu.VMEM),
        scratch_shapes=[pltpu.SemaphoreType.DMA],
        compiler_params=pltpu.CompilerParams(vmem_limit_bytes=16 << 20),
        cost_estimate=pl.CostEstimate(flops=1000, transcendentals=0, bytes_accessed=1000),
        name="give_cotangent",
    )(flag, after, gain, in_hbm(cot))


def in_hbm(array):
    return pltpu.with_memory_space_constraint(array, pltpu.HBM)


def partial_kernel(start, flag_ref, x_ref, got_ref, mine_ref, away_ref, home_ref, w_ref, sem):
    size = w_ref.shape[1]

    @pl.when(flag_ref[0] == 1)
    def _():
        copy = pltpu.make_async_copy(got_ref, w_ref, sem)
        copy.start()
        copy.wait()

    @pl.when(flag_ref[0] == 0)
    def _():
        copy = pltpu.make_async_copy(mine_ref.at[:, pl.ds(start, size)], w_ref, sem)
        copy.start()
        copy.wait()

    pairs, _, rows, depth = x_ref.shape
    weight = w_ref[...]
    away = dot(x_ref[:, 1].reshape(pairs * rows, depth), weight, NN)
    away_ref[...] = away.reshape(away_ref.shape).astype(away_ref.dtype)
    home = dot(x_ref[:, 0].reshape(pairs * rows, depth), weight, NN)
    home_ref[...] = home.reshape(home_ref.shape)


def partial_products(flag, features, got, matrix, start):
    pairs, _, rows, depth = features.shape
    size = got.shape[1]
    vmem = pl.BlockSpec(memory_space=pltpu.VMEM)
    return pl.pallas_call(
        lambda *refs: partial_kernel(start, *refs),
        out_shape=(
            jax.ShapeDtypeStruct((pairs, rows, size), jnp.bfloat16),
            jax.ShapeDtypeStruct((pairs, rows, size), jnp.float32),
            jax.ShapeDtypeStruct((depth, size), got.dtype),
        ),
        in_specs=[
            pl.BlockSpec(memory_space=pltpu.SMEM),
            vmem,
            pl.BlockSpec(memory_space=pl.ANY),
            pl.BlockSpec(memory_space=pltpu.HBM),
        ],
        out_specs=(vmem,) * 3,
        scratch_shapes=[pltpu.SemaphoreType.DMA],
        compiler_params=pltpu.CompilerParams(vmem_limit_bytes=32 << 20),
        cost_estimate=pl.CostEstimate(
            flops=4 * pairs * rows * depth * size, transcendentals=0, bytes_accessed=4 * depth * size
        ),
        name="partial_products",
    )(flag, features, got, in_hbm(matrix))


def arrange_in_kernel(flag_ref, order_ref, a_ref, b_ref, out_ref):
    keep = flag_ref[0] == 1
    for r in range(out_ref.shape[0]):
        place = order_ref[r]
        out_ref[r] = jnp.where(keep, a_ref[place], b_ref[place])


def arrange_out_kernel(order_ref, a_ref, b_ref, out_ref):
    for r in range(out_ref.shape[0]):
        value = a_ref[r].astype(jnp.float32) + b_ref[r].astype(jnp.float32)
        out_ref[order_ref[r]] = value.astype(out_ref.dtype)


def arrange(kernel, name, scalars, a, b):
    vmem = pl.BlockSpec(memory_space=pltpu.VMEM)
    return pl.pallas_call(
        kernel,
        out_shape=jax.ShapeDtypeStruct(b.shape, b.dtype),
        in_specs=[pl.BlockSpec(memory_space=pltpu.SMEM)] * len(scalars) + [vmem, vmem],
        out_specs=vmem,
        compiler_params=pltpu.CompilerParams(vmem_limit_bytes=32 << 20),
        name=name,
    )(*scalars, a, b)


def passed_along(block, axis, distance):
    devices = range(lax.axis_size(axis))
    route = [(i - distance, i) for i in devices if i - distance in devices]
    return lax.ppermute(block, axis, route)


def rotated(blocks, shift):
    count = blocks.shape[0]
    step = 1
    while step < count:
        turned = jnp.concatenate([blocks[step:], blocks[:step]], axis=0)
        blocks = jnp.where((shift // step) % 2 == 1, turned, blocks)
        step *= 2
    return blocks


def sent_round(block, distance):
    count = lax.axis_size("dp")
    return lax.ppermute(block, "dp", [(i, (i + 2 * distance) % count) for i in range(count)])


def sent_across(block):
    return lax.ppermute(block, "dp", [(i, i ^ 1) for i in range(lax.axis_size("dp"))])


def sent_tp(block, distance):
    count = lax.axis_size("tp")
    return lax.ppermute(block, "tp", [(i, (i + distance) % count) for i in range(count)])


def per_device(frames, counts, w_qkv, ln_gain, w_proj, rms_gain, cotangent):
    f32, bf16 = jnp.float32, jnp.bfloat16
    is_encoder = lax.axis_index("grp") == 0
    flag = is_encoder.astype(jnp.int32).reshape(1)
    dp_count, tp_count = lax.axis_size("dp"), lax.axis_size("tp")
    pair_count = dp_count // 2
    dp_index, tp_index = lax.axis_index("dp"), lax.axis_index("tp")
    relative = jnp.arange(dp_count, dtype=jnp.int32)
    order = (dp_index // 2 + relative // 2) % pair_count * 2 + (dp_index % 2 ^ relative % 2)

    frame = frames[0, 0]
    tokens_here = frame.shape[0] // 4
    depth = w_proj.shape[1]
    half = w_proj.shape[2] // 2
    first = half * FIRST_PART // 16 // 128 * 128
    sizes = (first, half - first)

    w_mine, cot_mine = w_proj[0], cotangent[0]
    give = [give_columns(flag, flag, w_mine, 0, sizes[0])]
    give.append(give_columns(flag, give[0], w_mine, first, sizes[1]))
    got = [passed_along(block, "grp", -1) for block in give]
    got_cot = passed_along(give_cotangent(flag, give[1], rms_gain, cot_mine, half), "grp", -1)

    embedded, qkv, probs, norm, inverse = encoder_forward(flag, frame, w_qkv[0], ln_gain)

    pieces = embedded
    if depth != CHUNK:
        pieces = embedded.reshape(-1, tokens_here, CHUNK // depth, depth)
        pieces = pieces.transpose(0, 2, 1, 3).reshape(dp_count, tokens_here, depth)
    swapped = lax.all_to_all(pieces, "dp", 0, 0)
    arrived = passed_along(swapped, "grp", 1)
    features = arrange(arrange_in_kernel, "arrange_in", (flag, order), swapped, arrived)
    features = jnp.concatenate(
        [features] + [sent_tp(features, tp_count - s) for s in range(1, tp_count)], axis=1
    ).reshape(pair_count, 2, tp_count * tokens_here, depth)

    acts, weights = [], []
    for c in range(2):
        away, home, weight = partial_products(flag, features, got[c], w_mine, half + c * first)
        weights.append(weight)
        home = home + sent_across(away).astype(f32)
        sent = home.astype(bf16)
        sent, features = lax.optimization_barrier((sent, features))
        parts = [sent_round(sent[s], s) for s in range(1, pair_count)]
        total = home[0]
        for block in parts:
            total = total + block.astype(f32)
        acts.append(total)

    got_cot, acts[0] = lax.optimization_barrier((got_cot, acts[0]))
    rows = cot_mine.shape[0]
    cot = jnp.where(is_encoder, got_cot[:rows], cot_mine[:, half:])
    gain_rms = jnp.where(is_encoder, got_cot[rows : rows + 1], rms_gain[:, half:])
    slot = lax.broadcasted_iota(jnp.int32, (1, tokens_here), 1) // TOKF
    live_mask = (slot < rotated(counts, tp_index)[:, None]).astype(f32).reshape(-1, 1)
    cot = rotated(cot.reshape(tp_count, tokens_here, half), tp_index).reshape(-1, half)
    scaled = gain_rms.astype(f32) * cot.astype(f32) * live_mask
    scaled = (scaled[:, :first], scaled[:, first:])
    squares = sum(jnp.sum(act * act, axis=1) for act in acts)
    products = sum(jnp.sum(act * part, axis=1) for act, part in zip(acts, scaled))
    sums = jnp.stack([squares, products], axis=1).reshape(tp_count, tokens_here, 2)
    sums = lax.psum(rotated(sums, (tp_count - tp_index) % tp_count), ("grp", "tp"))
    sums = rotated(sums, tp_index).reshape(-1, 2)
    inverse_rms = lax.rsqrt(sums[:, :1] / D + 1e-06)
    fall = inverse_rms**3 * (sums[:, 1:] / D)
    grads = [
        (inverse_rms * part - act * fall).astype(bf16) for act, part in zip(acts, scaled)
    ]

    def gathered_round(block):
        blocks = [block] + [None] * (pair_count - 1)
        for s in range(1, pair_count):
            blocks[pair_count - s] = sent_round(block, s)
        return jnp.stack(blocks)

    near = gathered_round(grads[0])
    duo = jnp.stack([grads[1], sent_across(grads[1])])
    near, duo = lax.optimization_barrier((near, duo))
    far = sent_across(near)
    duos = gathered_round(duo)
    near, far = (near, duos[:, 0]), (far, duos[:, 1])

    def back(blocks):
        return sum(
            jnp.einsum("prc,kc->prk", block, weight, preferred_element_type=f32)
            for block, weight in zip(blocks, weights)
        )

    terms = [back(near), back(far)]
    terms = jnp.stack(
        [term.reshape(pair_count, tp_count, tokens_here, depth) for term in terms], axis=1
    ).reshape(dp_count, tp_count, tokens_here, depth)
    total = terms[:, 0]
    for s in range(1, tp_count):
        total = total + sent_tp(terms[:, s].astype(bf16), s).astype(f32)
    total = total.astype(bf16)
    returned = passed_along(total, "grp", -1)
    whole = arrange(arrange_out_kernel, "arrange_out", (order,), total, returned)
    whole = lax.all_to_all(whole, "dp", 0, 0)
    if depth != CHUNK:
        whole = whole.reshape(-1, CHUNK // depth, tokens_here, depth)
        whole = whole.transpose(0, 2, 1, 3).reshape(-1, tokens_here, CHUNK)

    grad_frames = encoder_backward(flag, w_qkv[0], ln_gain, qkv, probs, norm, inverse, whole)
    return grad_frames[None, None]


def solution(mesh):
    placed = (
        P("grp", ("dp", "tp"), None, None),
        P("dp"),
        P("grp", None, None),
        P("grp", None),
        P("grp", "dp", "tp"),
        P("grp", "tp"),
        P("grp", "dp", "tp"),
    )
    return jax.shard_map(
        per_device,
        mesh=mesh,
        in_specs=placed,
        out_specs=P("grp", ("dp", "tp"), None, None),
        check_vma=False,
    )
```

time: 286 us -> 187 us (0.65)
  starting transfers between devices: 134 us -> 29.1 us
  blocking collectives: 18.9 us -> 43.2 us
  waiting for transfers between devices: 91.3 us -> 71.1 us
  Pallas kernels: 18.4 us -> 24.7 us
    ppermute x6 -> x5, starting transfers between devices: 101 us -> 6.72 us  [passed_along(): return lax.ppermute(block, axis, route)]
    all_to_all x0 -> x1, blocking collectives: none -> 18 us  [per_device(): swapped = lax.all_to_all(pieces, 'dp', 0, 0)]
    all_to_all x1 -> x0, waiting for transfers between devices: 8.24 us -> none  [per_device(): swapped = lax.all_to_all(pieces, 'dp', 0, 0)]
    all_to_all x1 -> x0, starting transfers between devices: 7.29 us -> none  [per_device(): swapped = lax.all_to_all(pieces, 'dp', 0, 0)]
    ppermute x4, waiting for transfers between devices: 21 us -> 14.3 us  [sent_across(): lax.ppermute(block, 'dp', [(i, i ^ 1) for i in range(lax.axis_size('dp'))])]
    all_to_all x1, blocking collectives: 13.2 us -> 19.5 us  [per_device(): whole = lax.all_to_all(whole, 'dp', 0, 0)]
    pallas_call x1 -> x5, Pallas kernels: 0.04 us -> 5.98 us  [the longest x2 5.22 us: partial_products(): pl.pallas_call(lambda *refs: partial_kernel(start, *refs), out_shape=(jax...]
    ppermute x6 -> x5, waiting for transfers between devices: 29.7 us -> 25.2 us  [passed_along(): return lax.ppermute(block, axis, route)]
  transfers between devices with their start and end apart: 25 -> 23, of which waited for: 14 -> 15; matrix products, arithmetic and copies ran while one was open for 5% -> 6% of each run, Pallas kernels for 3% -> 6%
where the time goes in v3:
time: 187 us; the launch traced here: 186 us
  waiting for transfers between devices  71.1 us (38%)
  blocking collectives  43.2 us (23%)
  starting transfers between devices  29.1 us (16%)
  Pallas kernels  24.7 us (13%)
  other arithmetic  9.92 us (5%)
  local copies, waits for them, and re-layouts  4.84 us (3%)
  matrix products  2.62 us (1%)
    ppermute x12, waiting for transfers between devices, sent_round(): lax.ppermute(block, 'dp', [(i, (i + 2 * distance) % count) for i in range...  28.3 us
    ppermute x5, waiting for transfers between devices, passed_along(): return lax.ppermute(block, axis, route)  25.2 us
    all_to_all x1, blocking collectives, per_device(): whole = lax.all_to_all(whole, 'dp', 0, 0)  19.5 us
    all_to_all x1, blocking collectives, per_device(): swapped = lax.all_to_all(pieces, 'dp', 0, 0)  18 us
    ppermute x12, starting transfers between devices, sent_round(): lax.ppermute(block, 'dp', [(i, (i + 2 * distance) % count) for i in range...  18 us
    ppermute x4, waiting for transfers between devices, sent_across(): lax.ppermute(block, 'dp', [(i, i ^ 1) for i in range(lax.axis_size('dp'))])  14.3 us
    pallas_call x1, Pallas kernels, encoder_backward(): pl.pallas_call(encoder_backward_kernel, out_shape=jax.ShapeDtypeStruct((l...  9.13 us
    pallas_call x1, Pallas kernels, encoder_forward(): pl.pallas_call(encoder_forward_kernel, out_shape=(jax.ShapeDtypeStruct((8...  8.35 us
  transfers between devices with their start and end apart: 23, of which 15 were waited for; matrix products, arithmetic and copies ran while one was open for 6% of the time, Pallas kernels for 6%

profile of v3, /device:TPU:0, one launch (start us, length us, event | category | flops | bytes accessed | tf_op | source)
XLA Modules:
  0.0 186.0 jit_solution(3996607775230960279)
XLA Ops:
  0.0 1.4 collective-permute-start.3
  1.5 8.3 %encoder_forward.1 = (bf16[8,32,640]{2,1,0:T(8,128)(2,1)S(1)}, bf16[6,128,640]{2,1,0:T(8,128)(2,1)S(1)}, f32[16,128,128]{2,1,0:T(8,128)S(1)}, f32[2,128,640]{2,1,0:T(8,128)S(1)}, f32[128,1]{1,0:T(8,128)S(1)}) custom-call(s32[1]{0:T(128)} %bitcast.refs_0_.refs_1_.flag_ref, bf16[128,1280]{1,0:T(8,128)(2,1)S(1)} %bitcast.104, bf16[1,1280]{1,0:T(2,128)(2,1)S(1)} %copy-done.11, ...), custom_call_target="tpu_custom_call" | custom-call | flops 1000 | bytes 1000 | tf_op jit(solution)/shard_map/encoder_forward/pallas_call | solution.py:141
  12.6 18.0 %all_to_all.10.a_ref = bf16[8,32,640]{2,1,0:T(8,128)(2,1)S(1)} all-to-all(bf16[8,32,640]{2,1,0:T(8,128)(2,1)S(1)} %get-tuple-element.23), channel_id=1, replica_groups=mesh['grp'=2,'dp'=8,'tp'=2] {'dp'}, dimensions={0} | all-to-all | bytes 655360 | tf_op jit(solution)/shard_map/all_to_all | solution.py:452
  30.6 1.3 collective-permute-start.1
  31.9 4.9 %collective-permute-done.1.b_ref = bf16[8,32,640]{2,1,0:T(8,128)(2,1)S(1)} collective-permute-done((bf16[8,32,640]{2,1,0:T(8,128)(2,1)S(1)}, bf16[8,32,640]{2,1,0:T(8,128)(2,1)S(1)}, u32[]{:S(2)}, u32[]{:S(2)}) %collective-permute-start.1) | collective-permute-done | bytes 327712 | tf_op jit(solution)/shard_map/ppermute | solution.py:396
  37.5 1.6 collective-permute-done.2
  39.2 3.0 %partial_products.2 = (bf16[4,64,1152]{2,1,0:T(8,128)(2,1)}, f32[4,64,1152]{2,1,0:T(8,128)S(1)}, bf16[640,1152]{1,0:T(8,128)(2,1)S(1)}) custom-call(s32[1]{0:T(128)} %bitcast.refs_0_.refs_1_.flag_ref, bf16[4,2,64,640]{3,2,1,0:T(8,128)(2,1)S(1)} %bitcast.102, bf16[640,1152]{1,0:T(8,128)(2,1)} %collective-permute-done.3.refs_2_, bf16[640,4096]{1,0:T(8,128)(2,1)} %bitcast.106), custom_call_target="tpu_custom_call" | custom-call | flops 754974720 | bytes 2949120 | tf_op jit(solution)/shard_map/partial_products/pallas_call | solution.py:345
  43.3 1.4 collective-permute-start.8
  45.5 1.3 collective-permute-start
  47.4 1.3 broadcast_select_fusion.1
  48.7 9.3 %collective-permute-done.4 = bf16[4,64,1152]{2,1,0:T(8,128)(2,1)} collective-permute-done((bf16[4,64,1152]{2,1,0:T(8,128)(2,1)}, bf16[4,64,1152]{2,1,0:T(8,128)(2,1)}, u32[]{:S(2)}, u32[]{:S(2)}) %collective-permute-start.4) | collective-permute-done | bytes 589856 | tf_op jit(solution)/shard_map/ppermute | solution.py:415
  58.0 2.6 %fusion.34 = (bf16[4,64,1152]{2,1,0:T(8,128)(2,1)S(1)}, f32[4,64,1152]{2,1,0:T(8,128)}) fusion(f32[4,64,1152]{2,1,0:T(8,128)} %copy-done.2, bf16[4,64,1152]{2,1,0:T(8,128)(2,1)} %collective-permute-done.4), kind=kLoop, calls=%fused_computation.82 | loop fusion | flops 884736 | bytes 3538944 | tf_op jit(solution)/shard_map/convert_element_type | solution.py:464
  62.4 2.9 %collective-permute-start.7 = (bf16[64,1152]{1,0:T(8,128)(2,1)}, bf16[64,1152]{1,0:T(8,128)(2,1)}, u32[]{:S(2)}, u32[]{:S(2)}) collective-permute-start(bf16[64,1152]{1,0:T(8,128)(2,1)} %get-tuple-element.51), channel_id=1, source_target_pairs={{0,12},{2,14},{4,0},{6,2},{8,4},{10,6},{12,8},{14,10},{1,13},{3,15... | collective-permute-start | bytes 442376 | tf_op jit(solution)/shard_map/ppermute | solution.py:411
  66.0 8.5 %collective-permute-done.8.refs_2_ = bf16[640,896]{1,0:T(8,128)(2,1)} collective-permute-done((bf16[640,896]{1,0:T(8,128)(2,1)S(1)}, bf16[640,896]{1,0:T(8,128)(2,1)}, u32[]{:S(2)}, u32[]{:S(2)}) %collective-permute-start.8) | collective-permute-done | bytes 1146912 | tf_op jit(solution)/shard_map/ppermute | solution.py:396
  74.5 2.2 %partial_products.3 = (bf16[4,64,896]{2,1,0:T(8,128)(2,1)S(1)}, f32[4,64,896]{2,1,0:T(8,128)S(1)}, bf16[640,896]{1,0:T(8,128)(2,1)S(1)}) custom-call(s32[1]{0:T(128)} %bitcast.refs_0_.refs_1_.flag_ref, bf16[4,2,64,640]{3,2,1,0:T(8,128)(2,1)S(1)} %bitcast.103, bf16[640,896]{1,0:T(8,128)(2,1)} %collective-permute-done.8.refs_2_, bf16[640,4096]{1,0:T(8,128)(2,1)} %bitcast.108), custom_call_target="tpu_custom_call" | custom-call | flops 587202560 | bytes 2293760 | tf_op jit(solution)/shard_map/partial_products/pallas_call | solution.py:345
  79.3 1.4 collective-permute-done
  82.7 5.0 %collective-permute-done.9 = bf16[4,64,896]{2,1,0:T(8,128)(2,1)S(1)} collective-permute-done((bf16[4,64,896]{2,1,0:T(8,128)(2,1)S(1)}, bf16[4,64,896]{2,1,0:T(8,128)(2,1)S(1)}, u32[]{:S(2)}, u32[]{:S(2)}) %collective-permute-start.9) | collective-permute-done | bytes 458784 | tf_op jit(solution)/shard_map/ppermute | solution.py:415
  88.7 3.1 %collective-permute-start.12 = (bf16[64,896]{1,0:T(8,128)(2,1)S(1)}, bf16[64,896]{1,0:T(8,128)(2,1)S(1)}, u32[]{:S(2)}, u32[]{:S(2)}) collective-permute-start(bf16[64,896]{1,0:T(8,128)(2,1)S(1)} %get-tuple-element.54), channel_id=1, source_target_pairs={{0,12},{2,14},{4,0},{6,2},{8,4},{10,6},{12,8},{14,10},{1,13},{3,15... | collective-permute-start | bytes 344072 | tf_op jit(solution)/shard_map/ppermute | solution.py:411
  92.4 2.7 %collective-permute-done.10 = bf16[64,896]{1,0:T(8,128)(2,1)S(1)} collective-permute-done((bf16[64,896]{1,0:T(8,128)(2,1)S(1)}, bf16[64,896]{1,0:T(8,128)(2,1)S(1)}, u32[]{:S(2)}, u32[]{:S(2)}) %collective-permute-start.10) | collective-permute-done | bytes 114720 | tf_op jit(solution)/shard_map/ppermute | solution.py:411
  95.1 4.7 %collective-permute-done.11 = bf16[64,896]{1,0:T(8,128)(2,1)S(1)} collective-permute-done((bf16[64,896]{1,0:T(8,128)(2,1)S(1)}, bf16[64,896]{1,0:T(8,128)(2,1)S(1)}, u32[]{:S(2)}, u32[]{:S(2)}) %collective-permute-start.11) | collective-permute-done | bytes 114720 | tf_op jit(solution)/shard_map/ppermute | solution.py:411
  100.9 5.8 %psum.7 = f32[2,32,2]{1,2,0:T(2,128)S(1)} all-reduce(f32[2,32,2]{1,2,0:T(2,128)S(1)} %maximum_select_fusion), channel_id=1, replica_groups=mesh['grp'=2,'dp'=8,'tp'=2] {'grp','tp'}, use_global_device_ids=true, to_apply=%region_4.5 | all-reduce | flops 128 | bytes 1024 | tf_op jit(solution)/shard_map/psum | solution.py:484
  109.2 2.9 %collective-permute-start.14 = (bf16[64,1152]{1,0:T(8,128)(2,1)S(1)}, bf16[64,1152]{1,0:T(8,128)(2,1)S(1)}, u32[]{:S(2)}, u32[]{:S(2)}) collective-permute-start(bf16[64,1152]{1,0:T(8,128)(2,1)S(1)} %subtract_convert_fusion), channel_id=1, source_target_pairs={{0,8},{2,10},{4,12},{6,14},{8,0},{10,2},{12,4},{14,6},{1,9},{3,11}... | collective-permute-start | bytes 442376 | tf_op jit(solution)/shard_map/ppermute | solution.py:411
  113.0 4.8 %collective-permute-done.15 = bf16[64,1152]{1,0:T(8,128)(2,1)S(1)} collective-permute-done((bf16[64,1152]{1,0:T(8,128)(2,1)S(1)}, bf16[64,1152]{1,0:T(8,128)(2,1)S(1)}, u32[]{:S(2)}, u32[]{:S(2)}) %collective-permute-start.15) | collective-permute-done | bytes 147488 | tf_op jit(solution)/shard_map/ppermute | solution.py:411
  117.8 4.9 %collective-permute-done.14 = bf16[64,1152]{1,0:T(8,128)(2,1)S(1)} collective-permute-done((bf16[64,1152]{1,0:T(8,128)(2,1)S(1)}, bf16[64,1152]{1,0:T(8,128)(2,1)S(1)}, u32[]{:S(2)}, u32[]{:S(2)}) %collective-permute-start.14) | collective-permute-done | bytes 147488 | tf_op jit(solution)/shard_map/ppermute | solution.py:411
  122.8 2.8 %collective-permute-start.19 = (bf16[2,64,896]{2,1,0:T(8,128)(2,1)S(1)}, bf16[2,64,896]{2,1,0:T(8,128)(2,1)S(1)}, u32[]{:S(2)}, u32[]{:S(2)}) collective-permute-start(bf16[2,64,896]{2,1,0:T(8,128)(2,1)S(1)} %pad_maximum_fusion.5), channel_id=1, source_target_pairs={{0,4},{2,6},{4,8},{6,10},{8,12},{10,14},{12,0},{14,2},{1,5},{3,7},... | collective-permute-start | bytes 688136 | tf_op jit(solution)/shard_map/ppermute | solution.py:411
  125.9 2.1 %collective-permute-start.17 = (bf16[2,64,896]{2,1,0:T(8,128)(2,1)S(1)}, bf16[2,64,896]{2,1,0:T(8,128)(2,1)S(1)}, u32[]{:S(2)}, u32[]{:S(2)}) collective-permute-start(bf16[2,64,896]{2,1,0:T(8,128)(2,1)S(1)} %pad_maximum_fusion.5), channel_id=1, source_target_pairs={{0,12},{2,14},{4,0},{6,2},{8,4},{10,6},{12,8},{14,10},{1,13},{3,15... | collective-permute-start | bytes 688136 | tf_op jit(solution)/shard_map/ppermute | solution.py:411
  128.9 4.4 %collective-permute-done.19 = bf16[2,64,896]{2,1,0:T(8,128)(2,1)S(1)} collective-permute-done((bf16[2,64,896]{2,1,0:T(8,128)(2,1)S(1)}, bf16[2,64,896]{2,1,0:T(8,128)(2,1)S(1)}, u32[]{:S(2)}, u32[]{:S(2)}) %collective-permute-start.19) | collective-permute-done | bytes 229408 | tf_op jit(solution)/shard_map/ppermute | solution.py:411
  133.3 6.9 %collective-permute-done.18 = bf16[2,64,896]{2,1,0:T(8,128)(2,1)S(1)} collective-permute-done((bf16[2,64,896]{2,1,0:T(8,128)(2,1)S(1)}, bf16[2,64,896]{2,1,0:T(8,128)(2,1)S(1)}, u32[]{:S(2)}, u32[]{:S(2)}) %collective-permute-start.18) | collective-permute-done | bytes 229408 | tf_op jit(solution)/shard_map/ppermute | solution.py:411
  143.3 1.6 collective-permute-done.21
  146.3 10.3 %collective-permute-done.22.b_ref = bf16[8,32,640]{2,1,0:T(8,128)(2,1)S(1)} collective-permute-done((bf16[8,32,640]{2,1,0:T(8,128)(2,1)S(1)}, bf16[8,32,640]{2,1,0:T(8,128)(2,1)S(1)}, u32[]{:S(2)}, u32[]{:S(2)}) %collective-permute-start.22) | collective-permute-done | bytes 327712 | tf_op jit(solution)/shard_map/ppermute | solution.py:396
  157.3 19.5 %all_to_all.11.grad_ref = bf16[8,32,640]{2,1,0:T(8,128)(2,1)S(1)} all-to-all(bf16[8,32,640]{2,1,0:T(8,128)(2,1)S(1)} %arrange_out.1), channel_id=1, replica_groups=mesh['grp'=2,'dp'=8,'tp'=2] {'dp'}, dimensions={0} | all-to-all | bytes 655360 | tf_op jit(solution)/shard_map/all_to_all | solution.py:521
  176.7 9.1 %encoder_backward.1 = bf16[128,1280]{1,0:T(8,128)(2,1)} custom-call(s32[1]{0:T(128)} %bitcast.refs_0_.refs_1_.flag_ref, bf16[8,32,640]{2,1,0:T(8,128)(2,1)S(1)} %all_to_all.11.grad_ref, bf16[1,1280]{1,0:T(2,128)(2,1)S(1)} %copy-done.11, bf16[6,128,640]{2,1,0:T(8,128)(2,1)S(1)} %copy-done.6, f32[16,128,128]{2,1,0:T(8,128)S(1)} %copy-done.4, ...), custom_call_target="tpu_custom_call" | custom-call | flops 1000 | bytes 1000 | tf_op jit(solution)/shard_map/encoder_backward/pallas_call | solution.py:240
  (98 shorter events, 25.5 us)
Async XLA Ops:
  0.0 1.5 copy-start.11
  0.0 9.8 %copy-start = (bf16[640,1152]{1,0:T(8,128)(2,1)}, bf16[640,1152]{1,0:T(8,128)(2,1)S(1)}, u32[]{:S(2)}) copy-start(bf16[640,1152]{1,0:T(8,128)(2,1)S(1)} %give_columns.2.refs_1_) | copy-start | bytes 4423684
  0.0 39.2 %collective-permute-start.3 = (bf16[640,1152]{1,0:T(8,128)(2,1)S(1)}, bf16[640,1152]{1,0:T(8,128)(2,1)}, u32[]{:S(2)}, u32[]{:S(2)}) collective-permute-start(bf16[640,1152]{1,0:T(8,128)(2,1)S(1)} %give_columns.2.refs_1_), channel_id=1, source_target_pairs={{16,0},{17,1},{18,2},{19,3},{20,4},{21,5},{22,6},{23,7},{24,8},{25... | collective-permute-start | bytes 4423688 | tf_op jit(solution)/shard_map/ppermute | solution.py:396
  30.6 6.3 %collective-permute-start.1 = (bf16[8,32,640]{2,1,0:T(8,128)(2,1)S(1)}, bf16[8,32,640]{2,1,0:T(8,128)(2,1)S(1)}, u32[]{:S(2)}, u32[]{:S(2)}) collective-permute-start(bf16[8,32,640]{2,1,0:T(8,128)(2,1)S(1)} %all_to_all.10.a_ref), channel_id=1, source_target_pairs={{0,16},{1,17},{2,18},{3,19},{4,20},{5,21},{6,22},{7,23},{8,24},{9,... | collective-permute-start | bytes 983048 | tf_op jit(solution)/shard_map/ppermute | solution.py:396
  37.5 1.7 collective-permute-start.2
  39.2 4.0 %copy-start.1 = (bf16[640,1152]{1,0:T(8,128)(2,1)S(1)}, bf16[640,1152]{1,0:T(8,128)(2,1)}, u32[]{:S(2)}) copy-start(bf16[640,1152]{1,0:T(8,128)(2,1)} %copy-done) | copy-start | bytes 4423684
  42.3 2.5 %copy-start.10 = (bf16[1,4096]{1,0:T(2,128)(2,1)S(1)}, bf16[1,4096]{1,0:T(2,128)(2,1)}, u32[]{:S(2)}) copy-start(bf16[1,4096]{1,0:T(2,128)(2,1)} %gain_ref.3) | copy-start | bytes 24580
  42.3 15.8 %collective-permute-start.4 = (bf16[4,64,1152]{2,1,0:T(8,128)(2,1)}, bf16[4,64,1152]{2,1,0:T(8,128)(2,1)}, u32[]{:S(2)}, u32[]{:S(2)}) collective-permute-start(bf16[4,64,1152]{2,1,0:T(8,128)(2,1)} %get-tuple-element.25), channel_id=1, source_target_pairs={{0,2},{2,0},{4,6},{6,4},{8,10},{10,8},{12,14},{14,12},{1,3},{3,1},... | collective-permute-start | bytes 1769480 | tf_op jit(solution)/shard_map/ppermute | solution.py:415
  43.3 3.5 %copy-start.13 = (s32[2]{0:T(128)S(1)}, s32[2]{0:T(128)}, u32[]{:S(2)}) copy-start(s32[2]{0:T(128)} %param.8) | copy-start | bytes 28
  43.3 31.2 %collective-permute-start.8 = (bf16[640,896]{1,0:T(8,128)(2,1)S(1)}, bf16[640,896]{1,0:T(8,128)(2,1)}, u32[]{:S(2)}, u32[]{:S(2)}) collective-permute-start(bf16[640,896]{1,0:T(8,128)(2,1)S(1)} %give_columns.3.after_ref), channel_id=1, source_target_pairs={{16,0},{17,1},{18,2},{19,3},{20,4},{21,5},{22,6},{23,7},{24,8},{25... | collective-permute-start | bytes 3440648 | tf_op jit(solution)/shard_map/ppermute | solution.py:396
  45.5 35.2 %collective-permute-start = (bf16[80,2048]{1,0:T(8,128)(2,1)}, bf16[80,2048]{1,0:T(8,128)(2,1)}, u32[]{:S(2)}, u32[]{:S(2)}) collective-permute-start(bf16[80,2048]{1,0:T(8,128)(2,1)} %give_cotangent.1), channel_id=1, source_target_pairs={{16,0},{17,1},{18,2},{19,3},{20,4},{21,5},{22,6},{23,7},{24,8},{25... | collective-permute-start | bytes 983048 | tf_op jit(solution)/shard_map/ppermute | solution.py:396
  61.4 16.5 %collective-permute-start.5 = (bf16[64,1152]{1,0:T(8,128)(2,1)}, bf16[64,1152]{1,0:T(8,128)(2,1)}, u32[]{:S(2)}, u32[]{:S(2)}) collective-permute-start(bf16[64,1152]{1,0:T(8,128)(2,1)} %get-tuple-element.50), channel_id=1, source_target_pairs={{0,4},{2,6},{4,8},{6,10},{8,12},{10,14},{12,0},{14,2},{1,5},{3,7},... | collective-permute-start | bytes 442376 | tf_op jit(solution)/shard_map/ppermute | solution.py:411
  62.4 15.5 %collective-permute-start.7 = (bf16[64,1152]{1,0:T(8,128)(2,1)}, bf16[64,1152]{1,0:T(8,128)(2,1)}, u32[]{:S(2)}, u32[]{:S(2)}) collective-permute-start(bf16[64,1152]{1,0:T(8,128)(2,1)} %get-tuple-element.51), channel_id=1, source_target_pairs={{0,12},{2,14},{4,0},{6,2},{8,4},{10,6},{12,8},{14,10},{1,13},{3,15... | collective-permute-start | bytes 442376 | tf_op jit(solution)/shard_map/ppermute | solution.py:411
  65.2 12.8 %collective-permute-start.6 = (bf16[64,1152]{1,0:T(8,128)(2,1)S(1)}, bf16[64,1152]{1,0:T(8,128)(2,1)}, u32[]{:S(2)}, u32[]{:S(2)}) collective-permute-start(bf16[64,1152]{1,0:T(8,128)(2,1)S(1)} %get-tuple-element.52), channel_id=1, source_target_pairs={{0,8},{2,10},{4,12},{6,14},{8,0},{10,2},{12,4},{14,6},{1,9},{3,11}... | collective-permute-start | bytes 442376 | tf_op jit(solution)/shard_map/ppermute | solution.py:411
  66.0 15.5 %copy-start.12 = (bf16[1,64,4096]{2,1,0:T(8,128)(2,1)S(1)}, bf16[1,64,4096]{2,1,0:T(8,128)(2,1)}, u32[]{:S(2)}) copy-start(bf16[1,64,4096]{2,1,0:T(8,128)(2,1)} %param.13) | copy-start | bytes 1572868
  76.7 11.0 %collective-permute-start.9 = (bf16[4,64,896]{2,1,0:T(8,128)(2,1)S(1)}, bf16[4,64,896]{2,1,0:T(8,128)(2,1)S(1)}, u32[]{:S(2)}, u32[]{:S(2)}) collective-permute-start(bf16[4,64,896]{2,1,0:T(8,128)(2,1)S(1)} %get-tuple-element.30), channel_id=1, source_target_pairs={{0,2},{2,0},{4,6},{6,4},{8,10},{10,8},{12,14},{14,12},{1,3},{3,1},... | collective-permute-start | bytes 1376264 | tf_op jit(solution)/shard_map/ppermute | solution.py:415
  87.9 7.2 %collective-permute-start.10 = (bf16[64,896]{1,0:T(8,128)(2,1)S(1)}, bf16[64,896]{1,0:T(8,128)(2,1)S(1)}, u32[]{:S(2)}, u32[]{:S(2)}) collective-permute-start(bf16[64,896]{1,0:T(8,128)(2,1)S(1)} %get-tuple-element.53), channel_id=1, source_target_pairs={{0,4},{2,6},{4,8},{6,10},{8,12},{10,14},{12,0},{14,2},{1,5},{3,7},... | collective-permute-start | bytes 344072 | tf_op jit(solution)/shard_map/ppermute | solution.py:411
  88.7 6.4 %collective-permute-start.12 = (bf16[64,896]{1,0:T(8,128)(2,1)S(1)}, bf16[64,896]{1,0:T(8,128)(2,1)S(1)}, u32[]{:S(2)}, u32[]{:S(2)}) collective-permute-start(bf16[64,896]{1,0:T(8,128)(2,1)S(1)} %get-tuple-element.54), channel_id=1, source_target_pairs={{0,12},{2,14},{4,0},{6,2},{8,4},{10,6},{12,8},{14,10},{1,13},{3,15... | collective-permute-start | bytes 344072 | tf_op jit(solution)/shard_map/ppermute | solution.py:411
  91.7 8.0 %collective-permute-start.11 = (bf16[64,896]{1,0:T(8,128)(2,1)S(1)}, bf16[64,896]{1,0:T(8,128)(2,1)S(1)}, u32[]{:S(2)}, u32[]{:S(2)}) collective-permute-start(bf16[64,896]{1,0:T(8,128)(2,1)S(1)} %get-tuple-element.55), channel_id=1, source_target_pairs={{0,8},{2,10},{4,12},{6,14},{8,0},{10,2},{12,4},{14,6},{1,9},{3,11}... | collective-permute-start | bytes 344072 | tf_op jit(solution)/shard_map/ppermute | solution.py:411
  107.8 5.2 %collective-permute-start.16 = (bf16[64,896]{1,0:T(8,128)(2,1)S(1)}, bf16[64,896]{1,0:T(8,128)(2,1)S(1)}, u32[]{:S(2)}, u32[]{:S(2)}) collective-permute-start(bf16[64,896]{1,0:T(8,128)(2,1)S(1)} %subtract_convert_fusion.1), channel_id=1, source_target_pairs={{0,2},{2,0},{4,6},{6,4},{8,10},{10,8},{12,14},{14,12},{1,3},{3,1},... | collective-permute-start | bytes 344072 | tf_op jit(solution)/shard_map/ppermute | solution.py:415
  109.1 8.7 %collective-permute-start.15 = (bf16[64,1152]{1,0:T(8,128)(2,1)S(1)}, bf16[64,1152]{1,0:T(8,128)(2,1)S(1)}, u32[]{:S(2)}, u32[]{:S(2)}) collective-permute-start(bf16[64,1152]{1,0:T(8,128)(2,1)S(1)} %subtract_convert_fusion), channel_id=1, source_target_pairs={{0,4},{2,6},{4,8},{6,10},{8,12},{10,14},{12,0},{14,2},{1,5},{3,7},... | collective-permute-start | bytes 442376 | tf_op jit(solution)/shard_map/ppermute | solution.py:411
  109.2 13.5 %collective-permute-start.14 = (bf16[64,1152]{1,0:T(8,128)(2,1)S(1)}, bf16[64,1152]{1,0:T(8,128)(2,1)S(1)}, u32[]{:S(2)}, u32[]{:S(2)}) collective-permute-start(bf16[64,1152]{1,0:T(8,128)(2,1)S(1)} %subtract_convert_fusion), channel_id=1, source_target_pairs={{0,8},{2,10},{4,12},{6,14},{8,0},{10,2},{12,4},{14,6},{1,9},{3,11}... | collective-permute-start | bytes 442376 | tf_op jit(solution)/shard_map/ppermute | solution.py:411
  112.0 10.6 %collective-permute-start.13 = (bf16[64,1152]{1,0:T(8,128)(2,1)S(1)}, bf16[64,1152]{1,0:T(8,128)(2,1)S(1)}, u32[]{:S(2)}, u32[]{:S(2)}) collective-permute-start(bf16[64,1152]{1,0:T(8,128)(2,1)S(1)} %subtract_convert_fusion), channel_id=1, source_target_pairs={{0,12},{2,14},{4,0},{6,2},{8,4},{10,6},{12,8},{14,10},{1,13},{3,15... | collective-permute-start | bytes 442376 | tf_op jit(solution)/shard_map/ppermute | solution.py:411
  122.8 10.5 %collective-permute-start.19 = (bf16[2,64,896]{2,1,0:T(8,128)(2,1)S(1)}, bf16[2,64,896]{2,1,0:T(8,128)(2,1)S(1)}, u32[]{:S(2)}, u32[]{:S(2)}) collective-permute-start(bf16[2,64,896]{2,1,0:T(8,128)(2,1)S(1)} %pad_maximum_fusion.5), channel_id=1, source_target_pairs={{0,4},{2,6},{4,8},{6,10},{8,12},{10,14},{12,0},{14,2},{1,5},{3,7},... | collective-permute-start | bytes 688136 | tf_op jit(solution)/shard_map/ppermute | solution.py:411
  125.6 14.6 %collective-permute-start.18 = (bf16[2,64,896]{2,1,0:T(8,128)(2,1)S(1)}, bf16[2,64,896]{2,1,0:T(8,128)(2,1)S(1)}, u32[]{:S(2)}, u32[]{:S(2)}) collective-permute-start(bf16[2,64,896]{2,1,0:T(8,128)(2,1)S(1)} %pad_maximum_fusion.5), channel_id=1, source_target_pairs={{0,8},{2,10},{4,12},{6,14},{8,0},{10,2},{12,4},{14,6},{1,9},{3,11}... | collective-permute-start | bytes 688136 | tf_op jit(solution)/shard_map/ppermute | solution.py:411
  125.9 14.3 %collective-permute-start.17 = (bf16[2,64,896]{2,1,0:T(8,128)(2,1)S(1)}, bf16[2,64,896]{2,1,0:T(8,128)(2,1)S(1)}, u32[]{:S(2)}, u32[]{:S(2)}) collective-permute-start(bf16[2,64,896]{2,1,0:T(8,128)(2,1)S(1)} %pad_maximum_fusion.5), channel_id=1, source_target_pairs={{0,12},{2,14},{4,0},{6,2},{8,4},{10,6},{12,8},{14,10},{1,13},{3,15... | collective-permute-start | bytes 688136 | tf_op jit(solution)/shard_map/ppermute | solution.py:411
  128.0 14.2 %collective-permute-start.20 = (bf16[4,64,1152]{2,1,0:T(8,128)(2,1)S(1)}, bf16[4,64,1152]{2,1,0:T(8,128)(2,1)S(1)}, u32[]{:S(2)}, u32[]{:S(2)}) collective-permute-start(bf16[4,64,1152]{2,1,0:T(8,128)(2,1)S(1)} %pad_maximum_fusion.3), channel_id=1, source_target_pairs={{0,2},{2,0},{4,6},{6,4},{8,10},{10,8},{12,14},{14,12},{1,3},{3,1},... | collective-permute-start | bytes 1769480 | tf_op jit(solution)/shard_map/ppermute | solution.py:415
  143.2 33.5 %copy-start.4 = (f32[16,128,128]{2,1,0:T(8,128)S(1)}, f32[16,128,128]{2,1,0:T(8,128)}, u32[]{:S(2)}) copy-start(f32[16,128,128]{2,1,0:T(8,128)} %copy-done.3) | copy-start | bytes 3145732
  143.2 33.5 %copy-start.6 = (bf16[6,128,640]{2,1,0:T(8,128)(2,1)S(1)}, bf16[6,128,640]{2,1,0:T(8,128)(2,1)}, u32[]{:S(2)}) copy-start(bf16[6,128,640]{2,1,0:T(8,128)(2,1)} %copy-done.5) | copy-start | bytes 2949124
  143.2 33.5 %copy-start.8 = (f32[2,128,640]{2,1,0:T(8,128)S(1)}, f32[2,128,640]{2,1,0:T(8,128)}, u32[]{:S(2)}) copy-start(f32[2,128,640]{2,1,0:T(8,128)} %copy-done.7) | copy-start | bytes 1966084
  143.2 1.7 collective-permute-start.21
  145.0 11.6 %collective-permute-start.22 = (bf16[8,32,640]{2,1,0:T(8,128)(2,1)S(1)}, bf16[8,32,640]{2,1,0:T(8,128)(2,1)S(1)}, u32[]{:S(2)}, u32[]{:S(2)}) collective-permute-start(bf16[8,32,640]{2,1,0:T(8,128)(2,1)S(1)} %fusion.15.a_ref), channel_id=1, source_target_pairs={{16,0},{17,1},{18,2},{19,3},{20,4},{21,5},{22,6},{23,7},{24,8},{25... | collective-permute-start | bytes 983048 | tf_op jit(solution)/shard_map/ppermute | solution.py:396
  (5 other events, 5.3 us)

commit v4 on v3

--- a/solution.py
+++ b/solution.py
@@ -142,9 +142,9 @@
         encoder_forward_kernel,
         out_shape=(
             jax.ShapeDtypeStruct((8, length // 4, CHUNK), bf16),
-            jax.ShapeDtypeStruct((6, length, CHUNK), bf16),
-            jax.ShapeDtypeStruct((HEADS, length, length), f32),
-            jax.ShapeDtypeStruct((2, length, CHUNK), f32),
+            pltpu.HBM((6, length, CHUNK), bf16),
+            pltpu.HBM((HEADS, length, length), f32),
+            pltpu.HBM((2, length, CHUNK), f32),
             jax.ShapeDtypeStruct((length, 1), f32),
         ),
         in_specs=[pl.BlockSpec(memory_space=pltpu.SMEM), vmem, vmem, hbm],
@@ -315,7 +315,8 @@
     return pltpu.with_memory_space_constraint(array, pltpu.HBM)
 
 
-def partial_kernel(start, flag_ref, x_ref, got_ref, mine_ref, away_ref, home_ref, w_ref, sem):
+def partial_kernel(start, flag_ref, x_ref, got_ref, mine_ref, near_ref, late_ref, *refs):
+    *homes, w_ref, sem = refs
     size = w_ref.shape[1]
 
     @pl.when(flag_ref[0] == 1)
@@ -333,36 +334,47 @@
     pairs, _, rows, depth = x_ref.shape
     weight = w_ref[...]
     away = dot(x_ref[:, 1].reshape(pairs * rows, depth), weight, NN)
-    away_ref[...] = away.reshape(away_ref.shape).astype(away_ref.dtype)
+    away = [away[s * rows : (s + 1) * rows].astype(near_ref.dtype) for s in range(pairs)]
+    for i, s in enumerate(near_blocks(pairs)):
+        near_ref[i] = away[s]
+    for i, s in enumerate(late_blocks(pairs)):
+        late_ref[i] = away[s]
     home = dot(x_ref[:, 0].reshape(pairs * rows, depth), weight, NN)
-    home_ref[...] = home.reshape(home_ref.shape)
+    for s in range(pairs):
+        homes[s][...] = home[s * rows : (s + 1) * rows]
+
+
+def near_blocks(pairs):
+    return list(range(1, pairs // 2 + 1))
+
+
+def late_blocks(pairs):
+    return list(range(pairs // 2 + 1, pairs)) + [0]
 
 
 def partial_products(flag, features, got, matrix, start):
     pairs, _, rows, depth = features.shape
     size = got.shape[1]
     vmem = pl.BlockSpec(memory_space=pltpu.VMEM)
-    return pl.pallas_call(
+    half = jax.ShapeDtypeStruct((pairs // 2, rows, size), jnp.bfloat16)
+    near, late, *home, weight = pl.pallas_call(
         lambda *refs: partial_kernel(start, *refs),
-        out_shape=(
-            jax.ShapeDtypeStruct((pairs, rows, size), jnp.bfloat16),
-            jax.ShapeDtypeStruct((pairs, rows, size), jnp.float32),
-            jax.ShapeDtypeStruct((depth, size), got.dtype),
-        ),
+        out_shape=(half, half)
+        + (jax.ShapeDtypeStruct((rows, size), jnp.float32),) * pairs
+        + (jax.ShapeDtypeStruct((depth, size), got.dtype),),
         in_specs=[
             pl.BlockSpec(memory_space=pltpu.SMEM),
             vmem,
             pl.BlockSpec(memory_space=pl.ANY),
             pl.BlockSpec(memory_space=pltpu.HBM),
         ],
-        out_specs=(vmem,) * 3,
+        out_specs=(vmem,) * (3 + pairs),
         scratch_shapes=[pltpu.SemaphoreType.DMA],
         compiler_params=pltpu.CompilerParams(vmem_limit_bytes=32 << 20),
-        cost_estimate=pl.CostEstimate(
-            flops=4 * pairs * rows * depth * size, transcendentals=0, bytes_accessed=4 * depth * size
-        ),
+        cost_estimate=pl.CostEstimate(flops=1000, transcendentals=0, bytes_accessed=1000),
         name="partial_products",
-    )(flag, features, got, in_hbm(matrix))
+    )(flag, features, in_hbm(got), in_hbm(matrix))
+    return near, late, home, weight
 
 
 def arrange_in_kernel(flag_ref, order_ref, a_ref, b_ref, out_ref):
@@ -406,9 +418,9 @@
     return blocks
 
 
-def sent_round(block, distance):
+def sent_round(block, move):
     count = lax.axis_size("dp")
-    return lax.ppermute(block, "dp", [(i, (i + 2 * distance) % count) for i in range(count)])
+    return lax.ppermute(block, "dp", [(i, i ^ (2 * move)) for i in range(count)])
 
 
 def sent_across(block):
@@ -428,7 +440,7 @@
     pair_count = dp_count // 2
     dp_index, tp_index = lax.axis_index("dp"), lax.axis_index("tp")
     relative = jnp.arange(dp_count, dtype=jnp.int32)
-    order = (dp_index // 2 + relative // 2) % pair_count * 2 + (dp_index % 2 ^ relative % 2)
+    order = dp_index ^ relative
 
     frame = frames[0, 0]
     tokens_here = frame.shape[0] // 4
@@ -458,15 +470,19 @@
 
     acts, weights = [], []
     for c in range(2):
-        away, home, weight = partial_products(flag, features, got[c], w_mine, half + c * first)
+        near, late, home, weight = partial_products(flag, features, got[c], w_mine, half + c * first)
         weights.append(weight)
-        home = home + sent_across(away).astype(f32)
-        sent = home.astype(bf16)
-        sent, features = lax.optimization_barrier((sent, features))
-        parts = [sent_round(sent[s], s) for s in range(1, pair_count)]
+        near, late = sent_across(near), sent_across(late)
+        for i, s in enumerate(near_blocks(pair_count)):
+            home[s] = home[s] + near[i].astype(f32)
+        for i, s in enumerate(late_blocks(pair_count)):
+            home[s] = home[s] + late[i].astype(f32)
+        sends = [block.astype(bf16) for block in home[1:]]
+        if c == 0:
+            sends, features = lax.optimization_barrier((sends, features))
         total = home[0]
-        for block in parts:
-            total = total + block.astype(f32)
+        for s, block in enumerate(sends):
+            total = total + sent_round(block, s + 1).astype(f32)
         acts.append(total)
 
     got_cot, acts[0] = lax.optimization_barrier((got_cot, acts[0]))
@@ -492,7 +508,7 @@
     def gathered_round(block):
         blocks = [block] + [None] * (pair_count - 1)
         for s in range(1, pair_count):
-            blocks[pair_count - s] = sent_round(block, s)
+            blocks[s] = sent_round(block, s)
         return jnp.stack(blocks)
 
     near = gathered_round(grads[0])

time: 187 us -> 179 us (0.957)
  waiting for transfers between devices: 71.1 us -> 63.9 us
  starting transfers between devices: 29.1 us -> 32.9 us
  local copies, waits for them, and re-layouts: 4.84 us -> 1.83 us
    ppermute x5, waiting for transfers between devices: 25.2 us -> 17.7 us  [passed_along(): return lax.ppermute(block, axis, route)]
    psum x1, blocking collectives: 5.76 us -> 11.6 us  [per_device(): lax.psum(rotated(sums, (tp_count - tp_index) % tp_count), ('grp', 'tp'))]
    all_to_all x1, blocking collectives: 19.5 us -> 13.6 us  [per_device(): whole = lax.all_to_all(whole, 'dp', 0, 0)]
    ppermute x12, waiting for transfers between devices: 28.3 us -> 33.2 us  [sent_round(): return lax.ppermute(block, 'dp', [(i, i ^ 2 * move) for i in range(count)])]
    ppermute x4 -> x6, waiting for transfers between devices: 14.3 us -> 11.4 us  [sent_across(): lax.ppermute(block, 'dp', [(i, i ^ 1) for i in range(lax.axis_size('dp'))])]
    unnamed x28 -> x26, local copies, waits for them, and re-layouts: 2.85 us -> 0.66 us
    ppermute x12, starting transfers between devices: 18 us -> 19.9 us  [sent_round(): return lax.ppermute(block, 'dp', [(i, i ^ 2 * move) for i in range(count)])]
    ppermute x4 -> x6, starting transfers between devices: 4.25 us -> 6.12 us  [sent_across(): lax.ppermute(block, 'dp', [(i, i ^ 1) for i in range(lax.axis_size('dp'))])]
  transfers between devices with their start and end apart: 23 -> 25, of which waited for: 15 -> 14; matrix products, arithmetic and copies ran while one was open for 6% -> 6% of each run, Pallas kernels for 6% -> 8%
where the time goes in v4:
time: 179 us
  waiting for transfers between devices  63.9 us (36%)
  blocking collectives  43.2 us (24%)
  starting transfers between devices  32.9 us (18%)
  Pallas kernels  23.8 us (13%)
  other arithmetic  9.79 us (5%)
  matrix products  2.62 us (1%)
  local copies, waits for them, and re-layouts  1.83 us (1%)
    ppermute x12, waiting for transfers between devices, sent_round(): return lax.ppermute(block, 'dp', [(i, i ^ 2 * move) for i in range(count)])  33.2 us
    ppermute x12, starting transfers between devices, sent_round(): return lax.ppermute(block, 'dp', [(i, i ^ 2 * move) for i in range(count)])  19.9 us
    all_to_all x1, blocking collectives, per_device(): swapped = lax.all_to_all(pieces, 'dp', 0, 0)  18 us
    ppermute x5, waiting for transfers between devices, passed_along(): return lax.ppermute(block, axis, route)  17.7 us
    all_to_all x1, blocking collectives, per_device(): whole = lax.all_to_all(whole, 'dp', 0, 0)  13.6 us
    psum x1, blocking collectives, per_device(): lax.psum(rotated(sums, (tp_count - tp_index) % tp_count), ('grp', 'tp'))  11.6 us
    ppermute x6, waiting for transfers between devices, sent_across(): lax.ppermute(block, 'dp', [(i, i ^ 1) for i in range(lax.axis_size('dp'))])  11.4 us
    pallas_call x1, Pallas kernels, encoder_backward(): pl.pallas_call(encoder_backward_kernel, out_shape=jax.ShapeDtypeStruct((l...  9.31 us
  transfers between devices with their start and end apart: 25, of which 14 were waited for; matrix products, arithmetic and copies ran while one was open for 6% of the time, Pallas kernels for 8%

profile of v4, /device:TPU:0, one launch (start us, length us, event | category | flops | bytes accessed | tf_op | source)
XLA Modules:
  0.0 178.7 jit_solution(15305125210429405691)
XLA Ops:
  0.0 1.4 collective-permute-start.3
  1.5 7.8 %encoder_forward.1 = (bf16[8,32,640]{2,1,0:T(8,128)(2,1)S(1)}, bf16[6,128,640]{2,1,0:T(8,128)(2,1)}, f32[16,128,128]{2,1,0:T(8,128)}, f32[2,128,640]{2,1,0:T(8,128)}, f32[128,1]{1,0:T(8,128)S(1)}) custom-call(s32[1]{0:T(128)} %bitcast.refs_0_.refs_1_.flag_ref, bf16[128,1280]{1,0:T(8,128)(2,1)S(1)} %bitcast.116, bf16[1,1280]{1,0:T(2,128)(2,1)S(1)} %copy-done.8, ...), custom_call_target="tpu_custom_call" | custom-call | flops 1000 | bytes 1000 | tf_op jit(solution)/shard_map/encoder_forward/pallas_call | solution.py:141
  9.2 18.0 %all_to_all.10.a_ref = bf16[8,32,640]{2,1,0:T(8,128)(2,1)S(1)} all-to-all(bf16[8,32,640]{2,1,0:T(8,128)(2,1)S(1)} %get-tuple-element.32), channel_id=1, replica_groups=mesh['grp'=2,'dp'=8,'tp'=2] {'dp'}, dimensions={0} | all-to-all | bytes 655360 | tf_op jit(solution)/shard_map/all_to_all | solution.py:464
  27.2 1.3 collective-permute-start.1
  28.6 4.9 %collective-permute-done.1.b_ref = bf16[8,32,640]{2,1,0:T(8,128)(2,1)S(1)} collective-permute-done((bf16[8,32,640]{2,1,0:T(8,128)(2,1)S(1)}, bf16[8,32,640]{2,1,0:T(8,128)(2,1)S(1)}, u32[]{:S(2)}, u32[]{:S(2)}) %collective-permute-start.1) | collective-permute-done | bytes 327712 | tf_op jit(solution)/shard_map/ppermute | solution.py:408
  34.8 1.4 collective-permute-start.9
  37.0 1.3 collective-permute-start
  40.1 2.5 %partial_products.2 = (bf16[2,64,1152]{2,1,0:T(8,128)(2,1)S(1)}, bf16[2,64,1152]{2,1,0:T(8,128)(2,1)S(1)}, f32[64,1152]{1,0:T(8,128)S(1)}, f32[64,1152]{1,0:T(8,...) custom-call(s32[1]{0:T(128)} %bitcast.refs_0_.refs_1_.flag_ref, ...), custom_call_target="tpu_custom_call" | custom-call | flops 1000 | bytes 1000 | tf_op jit(solution)/shard_map/partial_products/pallas_call | solution.py:360
  43.6 1.4 broadcast_select_fusion.1
  46.1 6.5 %collective-permute-done.4 = bf16[2,64,1152]{2,1,0:T(8,128)(2,1)S(1)} collective-permute-done((bf16[2,64,1152]{2,1,0:T(8,128)(2,1)S(1)}, bf16[2,64,1152]{2,1,0:T(8,128)(2,1)S(1)}, u32[]{:S(2)}, u32[]{:S(2)}) %collective-permute-start.4) | collective-permute-done | bytes 294944 | tf_op jit(solution)/shard_map/ppermute | solution.py:427
  53.4 4.4 %collective-permute-done.5 = bf16[2,64,1152]{2,1,0:T(8,128)(2,1)S(1)} collective-permute-done((bf16[2,64,1152]{2,1,0:T(8,128)(2,1)S(1)}, bf16[2,64,1152]{2,1,0:T(8,128)(2,1)S(1)}, u32[]{:S(2)}, u32[]{:S(2)}) %collective-permute-start.5) | collective-permute-done | bytes 294944 | tf_op jit(solution)/shard_map/ppermute | solution.py:427
  59.5 2.6 %collective-permute-start.7 = (bf16[64,1152]{1,0:T(8,128)(2,1)}, bf16[64,1152]{1,0:T(8,128)(2,1)}, u32[]{:S(2)}, u32[]{:S(2)}) collective-permute-start(bf16[64,1152]{1,0:T(8,128)(2,1)} %get-tuple-element.40), channel_id=1, source_target_pairs={{0,8},{2,10},{4,12},{6,14},{8,0},{10,2},{12,4},{14,6},{1,9},{3,11}... | collective-permute-start | bytes 442376 | tf_op jit(solution)/shard_map/ppermute | solution.py:423
  63.1 2.4 %collective-permute-done.9.refs_2_ = bf16[640,896]{1,0:T(8,128)(2,1)} collective-permute-done((bf16[640,896]{1,0:T(8,128)(2,1)S(1)}, bf16[640,896]{1,0:T(8,128)(2,1)}, u32[]{:S(2)}, u32[]{:S(2)}) %collective-permute-start.9) | collective-permute-done | bytes 1146912 | tf_op jit(solution)/shard_map/ppermute | solution.py:408
  65.5 2.2 %partial_products.3 = (bf16[2,64,896]{2,1,0:T(8,128)(2,1)S(1)}, bf16[2,64,896]{2,1,0:T(8,128)(2,1)S(1)}, f32[64,896]{1,0:T(8,128)S(1)}, f32[64,896]{1,0:T(8,128)...) custom-call(s32[1]{0:T(128)} %bitcast.refs_0_.refs_1_.flag_ref, ...), custom_call_target="tpu_custom_call" | custom-call | flops 1000 | bytes 1000 | tf_op jit(solution)/shard_map/partial_products/pallas_call | solution.py:360
  69.8 3.4 %collective-permute-done.7 = bf16[64,1152]{1,0:T(8,128)(2,1)} collective-permute-done((bf16[64,1152]{1,0:T(8,128)(2,1)}, bf16[64,1152]{1,0:T(8,128)(2,1)}, u32[]{:S(2)}, u32[]{:S(2)}) %collective-permute-start.7) | collective-permute-done | bytes 147488 | tf_op jit(solution)/shard_map/ppermute | solution.py:423
  76.4 3.0 %collective-permute-start.14 = (bf16[64,896]{1,0:T(8,128)(2,1)S(1)}, bf16[64,896]{1,0:T(8,128)(2,1)S(1)}, u32[]{:S(2)}, u32[]{:S(2)}) collective-permute-start(bf16[64,896]{1,0:T(8,128)(2,1)S(1)} %fusion.23), channel_id=1, source_target_pairs={{0,12},{2,14},{4,8},{6,10},{8,4},{10,6},{12,0},{14,2},{1,13},{3,15... | collective-permute-start | bytes 344072 | tf_op jit(solution)/shard_map/ppermute | solution.py:423
  81.0 2.6 %collective-permute-start.13 = (bf16[64,896]{1,0:T(8,128)(2,1)S(1)}, bf16[64,896]{1,0:T(8,128)(2,1)S(1)}, u32[]{:S(2)}, u32[]{:S(2)}) collective-permute-start(bf16[64,896]{1,0:T(8,128)(2,1)S(1)} %get-tuple-element.69), channel_id=1, source_target_pairs={{0,8},{2,10},{4,12},{6,14},{8,0},{10,2},{12,4},{14,6},{1,9},{3,11}... | collective-permute-start | bytes 344072 | tf_op jit(solution)/shard_map/ppermute | solution.py:423
  83.7 2.1 %collective-permute-done.12 = bf16[64,896]{1,0:T(8,128)(2,1)S(1)} collective-permute-done((bf16[64,896]{1,0:T(8,128)(2,1)S(1)}, bf16[64,896]{1,0:T(8,128)(2,1)S(1)}, u32[]{:S(2)}, u32[]{:S(2)}) %collective-permute-start.12) | collective-permute-done | bytes 114720 | tf_op jit(solution)/shard_map/ppermute | solution.py:423
  85.8 3.2 %collective-permute-done.13 = bf16[64,896]{1,0:T(8,128)(2,1)S(1)} collective-permute-done((bf16[64,896]{1,0:T(8,128)(2,1)S(1)}, bf16[64,896]{1,0:T(8,128)(2,1)S(1)}, u32[]{:S(2)}, u32[]{:S(2)}) %collective-permute-start.13) | collective-permute-done | bytes 114720 | tf_op jit(solution)/shard_map/ppermute | solution.py:423
  90.1 11.6 %psum.7 = f32[2,32,2]{1,2,0:T(2,128)S(1)} all-reduce(f32[2,32,2]{1,2,0:T(2,128)S(1)} %maximum_select_fusion), channel_id=1, replica_groups=mesh['grp'=2,'dp'=8,'tp'=2] {'grp','tp'}, use_global_device_ids=true, to_apply=%region_4.5 | all-reduce | flops 128 | bytes 1024 | tf_op jit(solution)/shard_map/psum | solution.py:500
  105.1 3.3 %collective-permute-start.15 = (bf16[64,1152]{1,0:T(8,128)(2,1)S(1)}, bf16[64,1152]{1,0:T(8,128)(2,1)S(1)}, u32[]{:S(2)}, u32[]{:S(2)}) collective-permute-start(bf16[64,1152]{1,0:T(8,128)(2,1)S(1)} %subtract_convert_fusion), channel_id=1, source_target_pairs={{0,4},{2,6},{4,0},{6,2},{8,12},{10,14},{12,8},{14,10},{1,5},{3,7},... | collective-permute-start | bytes 442376 | tf_op jit(solution)/shard_map/ppermute | solution.py:423
  108.4 4.2 %collective-permute-done.17 = bf16[64,1152]{1,0:T(8,128)(2,1)S(1)} collective-permute-done((bf16[64,1152]{1,0:T(8,128)(2,1)S(1)}, bf16[64,1152]{1,0:T(8,128)(2,1)S(1)}, u32[]{:S(2)}, u32[]{:S(2)}) %collective-permute-start.17) | collective-permute-done | bytes 147488 | tf_op jit(solution)/shard_map/ppermute | solution.py:423
  112.7 4.5 %collective-permute-done.16 = bf16[64,1152]{1,0:T(8,128)(2,1)S(1)} collective-permute-done((bf16[64,1152]{1,0:T(8,128)(2,1)S(1)}, bf16[64,1152]{1,0:T(8,128)(2,1)S(1)}, u32[]{:S(2)}, u32[]{:S(2)}) %collective-permute-start.16) | collective-permute-done | bytes 147488 | tf_op jit(solution)/shard_map/ppermute | solution.py:423
  117.3 2.1 %collective-permute-start.21 = (bf16[2,64,896]{2,1,0:T(8,128)(2,1)S(1)}, bf16[2,64,896]{2,1,0:T(8,128)(2,1)S(1)}, u32[]{:S(2)}, u32[]{:S(2)}) collective-permute-start(bf16[2,64,896]{2,1,0:T(8,128)(2,1)S(1)} %pad_maximum_fusion.5), channel_id=1, source_target_pairs={{0,12},{2,14},{4,8},{6,10},{8,4},{10,6},{12,0},{14,2},{1,13},{3,15... | collective-permute-start | bytes 688136 | tf_op jit(solution)/shard_map/ppermute | solution.py:423
  119.4 2.4 %collective-permute-start.19 = (bf16[2,64,896]{2,1,0:T(8,128)(2,1)S(1)}, bf16[2,64,896]{2,1,0:T(8,128)(2,1)S(1)}, u32[]{:S(2)}, u32[]{:S(2)}) collective-permute-start(bf16[2,64,896]{2,1,0:T(8,128)(2,1)S(1)} %pad_maximum_fusion.5), channel_id=1, source_target_pairs={{0,4},{2,6},{4,0},{6,2},{8,12},{10,14},{12,8},{14,10},{1,5},{3,7},... | collective-permute-start | bytes 688136 | tf_op jit(solution)/shard_map/ppermute | solution.py:423
  122.7 5.0 %collective-permute-done.21 = bf16[2,64,896]{2,1,0:T(8,128)(2,1)S(1)} collective-permute-done((bf16[2,64,896]{2,1,0:T(8,128)(2,1)S(1)}, bf16[2,64,896]{2,1,0:T(8,128)(2,1)S(1)}, u32[]{:S(2)}, u32[]{:S(2)}) %collective-permute-start.21) | collective-permute-done | bytes 229408 | tf_op jit(solution)/shard_map/ppermute | solution.py:423
  127.8 10.6 %collective-permute-done.20 = bf16[2,64,896]{2,1,0:T(8,128)(2,1)S(1)} collective-permute-done((bf16[2,64,896]{2,1,0:T(8,128)(2,1)S(1)}, bf16[2,64,896]{2,1,0:T(8,128)(2,1)S(1)}, u32[]{:S(2)}, u32[]{:S(2)}) %collective-permute-start.20) | collective-permute-done | bytes 229408 | tf_op jit(solution)/shard_map/ppermute | solution.py:423
  141.6 1.6 collective-permute-done.23
  143.3 1.3 collective-permute-start.24
  144.6 10.3 %collective-permute-done.24.b_ref = bf16[8,32,640]{2,1,0:T(8,128)(2,1)S(1)} collective-permute-done((bf16[8,32,640]{2,1,0:T(8,128)(2,1)S(1)}, bf16[8,32,640]{2,1,0:T(8,128)(2,1)S(1)}, u32[]{:S(2)}, u32[]{:S(2)}) %collective-permute-start.24) | collective-permute-done | bytes 327712 | tf_op jit(solution)/shard_map/ppermute | solution.py:408
  155.6 13.6 %all_to_all.11.grad_ref = bf16[8,32,640]{2,1,0:T(8,128)(2,1)S(1)} all-to-all(bf16[8,32,640]{2,1,0:T(8,128)(2,1)S(1)} %arrange_out.1), channel_id=1, replica_groups=mesh['grp'=2,'dp'=8,'tp'=2] {'dp'}, dimensions={0} | all-to-all | bytes 655360 | tf_op jit(solution)/shard_map/all_to_all | solution.py:537
  169.2 9.3 %encoder_backward.1 = bf16[128,1280]{1,0:T(8,128)(2,1)} custom-call(s32[1]{0:T(128)} %bitcast.refs_0_.refs_1_.flag_ref, bf16[8,32,640]{2,1,0:T(8,128)(2,1)S(1)} %all_to_all.11.grad_ref, bf16[1,1280]{1,0:T(2,128)(2,1)S(1)} %copy-done.8, bf16[6,128,640]{2,1,0:T(8,128)(2,1)S(1)} %copy-done.2, f32[16,128,128]{2,1,0:T(8,128)S(1)} %copy-done.1, ...), custom_call_target="tpu_custom_call" | custom-call | flops 1000 | bytes 1000 | tf_op jit(solution)/shard_map/encoder_backward/pallas_call | solution.py:240
  (100 shorter events, 25.7 us)
Async XLA Ops:
  0.0 40.1 %collective-permute-start.3 = (bf16[640,1152]{1,0:T(8,128)(2,1)S(1)}, bf16[640,1152]{1,0:T(8,128)(2,1)}, u32[]{:S(2)}, u32[]{:S(2)}) collective-permute-start(bf16[640,1152]{1,0:T(8,128)(2,1)S(1)} %give_columns.2.refs_1_), channel_id=1, source_target_pairs={{16,0},{17,1},{18,2},{19,3},{20,4},{21,5},{22,6},{23,7},{24,8},{25... | collective-permute-start | bytes 4423688 | tf_op jit(solution)/shard_map/ppermute | solution.py:408
  27.2 6.3 %collective-permute-start.1 = (bf16[8,32,640]{2,1,0:T(8,128)(2,1)S(1)}, bf16[8,32,640]{2,1,0:T(8,128)(2,1)S(1)}, u32[]{:S(2)}, u32[]{:S(2)}) collective-permute-start(bf16[8,32,640]{2,1,0:T(8,128)(2,1)S(1)} %all_to_all.10.a_ref), channel_id=1, source_target_pairs={{0,16},{1,17},{2,18},{3,19},{4,20},{5,21},{6,22},{7,23},{8,24},{9,... | collective-permute-start | bytes 983048 | tf_op jit(solution)/shard_map/ppermute | solution.py:408
  34.1 4.8 %collective-permute-start.2 = (bf16[8,32,640]{2,1,0:T(8,128)(2,1)S(1)}, bf16[8,32,640]{2,1,0:T(8,128)(2,1)}, u32[]{:S(2)}, u32[]{:S(2)}) collective-permute-start(bf16[8,32,640]{2,1,0:T(8,128)(2,1)S(1)} %arrange_in.1), channel_id=1, source_target_pairs={{0,1},{1,0},{2,3},{3,2},{4,5},{5,4},{6,7},{7,6},{8,9},{9,8},{10,11... | collective-permute-start | bytes 983048 | tf_op jit(solution)/shard_map/ppermute | solution.py:432
  34.8 30.7 %collective-permute-start.9 = (bf16[640,896]{1,0:T(8,128)(2,1)S(1)}, bf16[640,896]{1,0:T(8,128)(2,1)}, u32[]{:S(2)}, u32[]{:S(2)}) collective-permute-start(bf16[640,896]{1,0:T(8,128)(2,1)S(1)} %give_columns.3.after_ref), channel_id=1, source_target_pairs={{16,0},{17,1},{18,2},{19,3},{20,4},{21,5},{22,6},{23,7},{24,8},{25... | collective-permute-start | bytes 3440648 | tf_op jit(solution)/shard_map/ppermute | solution.py:408
  37.0 37.4 %collective-permute-start = (bf16[80,2048]{1,0:T(8,128)(2,1)}, bf16[80,2048]{1,0:T(8,128)(2,1)}, u32[]{:S(2)}, u32[]{:S(2)}) collective-permute-start(bf16[80,2048]{1,0:T(8,128)(2,1)} %give_cotangent.1), channel_id=1, source_target_pairs={{16,0},{17,1},{18,2},{19,3},{20,4},{21,5},{22,6},{23,7},{24,8},{25... | collective-permute-start | bytes 983048 | tf_op jit(solution)/shard_map/ppermute | solution.py:408
  42.6 10.7 %copy-start.5 = (f32[64,1152]{1,0:T(8,128)}, f32[64,1152]{1,0:T(8,128)S(1)}, u32[]{:S(2)}) copy-start(f32[64,1152]{1,0:T(8,128)S(1)} %get-tuple-element.33) | copy-start | bytes 884740
  42.7 10.0 %collective-permute-start.4 = (bf16[2,64,1152]{2,1,0:T(8,128)(2,1)S(1)}, bf16[2,64,1152]{2,1,0:T(8,128)(2,1)S(1)}, u32[]{:S(2)}, u32[]{:S(2)}) collective-permute-start(bf16[2,64,1152]{2,1,0:T(8,128)(2,1)S(1)} %get-tuple-element.34), channel_id=1, source_target_pairs={{0,2},{2,0},{4,6},{6,4},{8,10},{10,8},{12,14},{14,12},{1,3},{3,1},... | collective-permute-start | bytes 884744 | tf_op jit(solution)/shard_map/ppermute | solution.py:427
  45.0 12.8 %collective-permute-start.5 = (bf16[2,64,1152]{2,1,0:T(8,128)(2,1)S(1)}, bf16[2,64,1152]{2,1,0:T(8,128)(2,1)S(1)}, u32[]{:S(2)}, u32[]{:S(2)}) collective-permute-start(bf16[2,64,1152]{2,1,0:T(8,128)(2,1)S(1)} %get-tuple-element.36), channel_id=1, source_target_pairs={{0,2},{2,0},{4,6},{6,4},{8,10},{10,8},{12,14},{14,12},{1,3},{3,1},... | collective-permute-start | bytes 884744 | tf_op jit(solution)/shard_map/ppermute | solution.py:427
  58.5 10.2 %collective-permute-start.6 = (bf16[64,1152]{1,0:T(8,128)(2,1)}, bf16[64,1152]{1,0:T(8,128)(2,1)S(1)}, u32[]{:S(2)}, u32[]{:S(2)}) collective-permute-start(bf16[64,1152]{1,0:T(8,128)(2,1)} %get-tuple-element.39), channel_id=1, source_target_pairs={{0,4},{2,6},{4,0},{6,2},{8,12},{10,14},{12,8},{14,10},{1,5},{3,7},... | collective-permute-start | bytes 442376 | tf_op jit(solution)/shard_map/ppermute | solution.py:423
  59.5 13.8 %collective-permute-start.7 = (bf16[64,1152]{1,0:T(8,128)(2,1)}, bf16[64,1152]{1,0:T(8,128)(2,1)}, u32[]{:S(2)}, u32[]{:S(2)}) collective-permute-start(bf16[64,1152]{1,0:T(8,128)(2,1)} %get-tuple-element.40), channel_id=1, source_target_pairs={{0,8},{2,10},{4,12},{6,14},{8,0},{10,2},{12,4},{14,6},{1,9},{3,11}... | collective-permute-start | bytes 442376 | tf_op jit(solution)/shard_map/ppermute | solution.py:423
  62.1 11.2 %collective-permute-start.8 = (bf16[64,1152]{1,0:T(8,128)(2,1)}, bf16[64,1152]{1,0:T(8,128)(2,1)}, u32[]{:S(2)}, u32[]{:S(2)}) collective-permute-start(bf16[64,1152]{1,0:T(8,128)(2,1)} %fusion.17), channel_id=1, source_target_pairs={{0,12},{2,14},{4,8},{6,10},{8,4},{10,6},{12,0},{14,2},{1,13},{3,15... | collective-permute-start | bytes 442376 | tf_op jit(solution)/shard_map/ppermute | solution.py:423
  63.1 10.2 %copy-start.6 = (f32[64,1152]{1,0:T(8,128)S(1)}, f32[64,1152]{1,0:T(8,128)}, u32[]{:S(2)}) copy-start(f32[64,1152]{1,0:T(8,128)} %copy-done.5) | copy-start | bytes 884740
  63.1 10.2 %copy-start.11 = (bf16[2,64,1152]{2,1,0:T(8,128)(2,1)S(1)}, bf16[2,64,1152]{2,1,0:T(8,128)(2,1)}, u32[]{:S(2)}) copy-start(bf16[2,64,1152]{2,1,0:T(8,128)(2,1)} %copy-done.10) | copy-start | bytes 884740
  67.7 7.4 %copy-start.9 = (bf16[1,64,4096]{2,1,0:T(8,128)(2,1)S(1)}, bf16[1,64,4096]{2,1,0:T(8,128)(2,1)}, u32[]{:S(2)}) copy-start(bf16[1,64,4096]{2,1,0:T(8,128)(2,1)} %param.13) | copy-start | bytes 1572868
  67.8 8.6 %collective-permute-start.10 = (bf16[2,64,896]{2,1,0:T(8,128)(2,1)S(1)}, bf16[2,64,896]{2,1,0:T(8,128)(2,1)S(1)}, u32[]{:S(2)}, u32[]{:S(2)}) collective-permute-start(bf16[2,64,896]{2,1,0:T(8,128)(2,1)S(1)} %get-tuple-element.45), channel_id=1, source_target_pairs={{0,2},{2,0},{4,6},{6,4},{8,10},{10,8},{12,14},{14,12},{1,3},{3,1},... | collective-permute-start | bytes 688136 | tf_op jit(solution)/shard_map/ppermute | solution.py:427
  68.7 11.2 %collective-permute-start.11 = (bf16[2,64,896]{2,1,0:T(8,128)(2,1)S(1)}, bf16[2,64,896]{2,1,0:T(8,128)(2,1)S(1)}, u32[]{:S(2)}, u32[]{:S(2)}) collective-permute-start(bf16[2,64,896]{2,1,0:T(8,128)(2,1)S(1)} %get-tuple-element.47), channel_id=1, source_target_pairs={{0,2},{2,0},{4,6},{6,4},{8,10},{10,8},{12,14},{14,12},{1,3},{3,1},... | collective-permute-start | bytes 688136 | tf_op jit(solution)/shard_map/ppermute | solution.py:427
  76.4 7.3 %collective-permute-start.14 = (bf16[64,896]{1,0:T(8,128)(2,1)S(1)}, bf16[64,896]{1,0:T(8,128)(2,1)S(1)}, u32[]{:S(2)}, u32[]{:S(2)}) collective-permute-start(bf16[64,896]{1,0:T(8,128)(2,1)S(1)} %fusion.23), channel_id=1, source_target_pairs={{0,12},{2,14},{4,8},{6,10},{8,4},{10,6},{12,0},{14,2},{1,13},{3,15... | collective-permute-start | bytes 344072 | tf_op jit(solution)/shard_map/ppermute | solution.py:423
  79.9 5.8 %collective-permute-start.12 = (bf16[64,896]{1,0:T(8,128)(2,1)S(1)}, bf16[64,896]{1,0:T(8,128)(2,1)S(1)}, u32[]{:S(2)}, u32[]{:S(2)}) collective-permute-start(bf16[64,896]{1,0:T(8,128)(2,1)S(1)} %get-tuple-element.68), channel_id=1, source_target_pairs={{0,4},{2,6},{4,0},{6,2},{8,12},{10,14},{12,8},{14,10},{1,5},{3,7},... | collective-permute-start | bytes 344072 | tf_op jit(solution)/shard_map/ppermute | solution.py:423
  81.0 8.0 %collective-permute-start.13 = (bf16[64,896]{1,0:T(8,128)(2,1)S(1)}, bf16[64,896]{1,0:T(8,128)(2,1)S(1)}, u32[]{:S(2)}, u32[]{:S(2)}) collective-permute-start(bf16[64,896]{1,0:T(8,128)(2,1)S(1)} %get-tuple-element.69), channel_id=1, source_target_pairs={{0,8},{2,10},{4,12},{6,14},{8,0},{10,2},{12,4},{14,6},{1,9},{3,11}... | collective-permute-start | bytes 344072 | tf_op jit(solution)/shard_map/ppermute | solution.py:423
  102.9 5.5 %collective-permute-start.18 = (bf16[64,896]{1,0:T(8,128)(2,1)S(1)}, bf16[64,896]{1,0:T(8,128)(2,1)S(1)}, u32[]{:S(2)}, u32[]{:S(2)}) collective-permute-start(bf16[64,896]{1,0:T(8,128)(2,1)S(1)} %subtract_convert_fusion.1), channel_id=1, source_target_pairs={{0,2},{2,0},{4,6},{6,4},{8,10},{10,8},{12,14},{14,12},{1,3},{3,1},... | collective-permute-start | bytes 344072 | tf_op jit(solution)/shard_map/ppermute | solution.py:427
  104.0 8.7 %collective-permute-start.17 = (bf16[64,1152]{1,0:T(8,128)(2,1)S(1)}, bf16[64,1152]{1,0:T(8,128)(2,1)S(1)}, u32[]{:S(2)}, u32[]{:S(2)}) collective-permute-start(bf16[64,1152]{1,0:T(8,128)(2,1)S(1)} %subtract_convert_fusion), channel_id=1, source_target_pairs={{0,12},{2,14},{4,8},{6,10},{8,4},{10,6},{12,0},{14,2},{1,13},{3,15... | collective-permute-start | bytes 442376 | tf_op jit(solution)/shard_map/ppermute | solution.py:423
  105.1 12.1 %collective-permute-start.16 = (bf16[64,1152]{1,0:T(8,128)(2,1)S(1)}, bf16[64,1152]{1,0:T(8,128)(2,1)S(1)}, u32[]{:S(2)}, u32[]{:S(2)}) collective-permute-start(bf16[64,1152]{1,0:T(8,128)(2,1)S(1)} %subtract_convert_fusion), channel_id=1, source_target_pairs={{0,8},{2,10},{4,12},{6,14},{8,0},{10,2},{12,4},{14,6},{1,9},{3,11}... | collective-permute-start | bytes 442376 | tf_op jit(solution)/shard_map/ppermute | solution.py:423
  105.1 12.1 %collective-permute-start.15 = (bf16[64,1152]{1,0:T(8,128)(2,1)S(1)}, bf16[64,1152]{1,0:T(8,128)(2,1)S(1)}, u32[]{:S(2)}, u32[]{:S(2)}) collective-permute-start(bf16[64,1152]{1,0:T(8,128)(2,1)S(1)} %subtract_convert_fusion), channel_id=1, source_target_pairs={{0,4},{2,6},{4,0},{6,2},{8,12},{10,14},{12,8},{14,10},{1,5},{3,7},... | collective-permute-start | bytes 442376 | tf_op jit(solution)/shard_map/ppermute | solution.py:423
  117.3 10.5 %collective-permute-start.21 = (bf16[2,64,896]{2,1,0:T(8,128)(2,1)S(1)}, bf16[2,64,896]{2,1,0:T(8,128)(2,1)S(1)}, u32[]{:S(2)}, u32[]{:S(2)}) collective-permute-start(bf16[2,64,896]{2,1,0:T(8,128)(2,1)S(1)} %pad_maximum_fusion.5), channel_id=1, source_target_pairs={{0,12},{2,14},{4,8},{6,10},{8,4},{10,6},{12,0},{14,2},{1,13},{3,15... | collective-permute-start | bytes 688136 | tf_op jit(solution)/shard_map/ppermute | solution.py:423
  119.4 19.1 %collective-permute-start.20 = (bf16[2,64,896]{2,1,0:T(8,128)(2,1)S(1)}, bf16[2,64,896]{2,1,0:T(8,128)(2,1)S(1)}, u32[]{:S(2)}, u32[]{:S(2)}) collective-permute-start(bf16[2,64,896]{2,1,0:T(8,128)(2,1)S(1)} %pad_maximum_fusion.5), channel_id=1, source_target_pairs={{0,8},{2,10},{4,12},{6,14},{8,0},{10,2},{12,4},{14,6},{1,9},{3,11}... | collective-permute-start | bytes 688136 | tf_op jit(solution)/shard_map/ppermute | solution.py:423
  119.4 19.1 %collective-permute-start.19 = (bf16[2,64,896]{2,1,0:T(8,128)(2,1)S(1)}, bf16[2,64,896]{2,1,0:T(8,128)(2,1)S(1)}, u32[]{:S(2)}, u32[]{:S(2)}) collective-permute-start(bf16[2,64,896]{2,1,0:T(8,128)(2,1)S(1)} %pad_maximum_fusion.5), channel_id=1, source_target_pairs={{0,4},{2,6},{4,0},{6,2},{8,12},{10,14},{12,8},{14,10},{1,5},{3,7},... | collective-permute-start | bytes 688136 | tf_op jit(solution)/shard_map/ppermute | solution.py:423
  121.8 18.7 %collective-permute-start.22 = (bf16[4,64,1152]{2,1,0:T(8,128)(2,1)S(1)}, bf16[4,64,1152]{2,1,0:T(8,128)(2,1)S(1)}, u32[]{:S(2)}, u32[]{:S(2)}) collective-permute-start(bf16[4,64,1152]{2,1,0:T(8,128)(2,1)S(1)} %pad_maximum_fusion.3), channel_id=1, source_target_pairs={{0,2},{2,0},{4,6},{6,4},{8,10},{10,8},{12,14},{14,12},{1,3},{3,1},... | collective-permute-start | bytes 1769480 | tf_op jit(solution)/shard_map/ppermute | solution.py:427
  141.5 27.7 %copy-start.1 = (f32[16,128,128]{2,1,0:T(8,128)S(1)}, f32[16,128,128]{2,1,0:T(8,128)}, u32[]{:S(2)}) copy-start(f32[16,128,128]{2,1,0:T(8,128)} %get-tuple-element.56.probs_ref) | copy-start | bytes 3145732
  141.5 27.7 %copy-start.2 = (bf16[6,128,640]{2,1,0:T(8,128)(2,1)S(1)}, bf16[6,128,640]{2,1,0:T(8,128)(2,1)}, u32[]{:S(2)}) copy-start(bf16[6,128,640]{2,1,0:T(8,128)(2,1)} %get-tuple-element.55.qkv_ref) | copy-start | bytes 2949124
  141.5 27.7 %copy-start.3 = (f32[2,128,640]{2,1,0:T(8,128)S(1)}, f32[2,128,640]{2,1,0:T(8,128)}, u32[]{:S(2)}) copy-start(f32[2,128,640]{2,1,0:T(8,128)} %get-tuple-element.57.norm_ref) | copy-start | bytes 1966084
  141.5 1.7 collective-permute-start.23
  143.3 11.6 %collective-permute-start.24 = (bf16[8,32,640]{2,1,0:T(8,128)(2,1)S(1)}, bf16[8,32,640]{2,1,0:T(8,128)(2,1)S(1)}, u32[]{:S(2)}, u32[]{:S(2)}) collective-permute-start(bf16[8,32,640]{2,1,0:T(8,128)(2,1)S(1)} %fusion.15.a_ref), channel_id=1, source_target_pairs={{16,0},{17,1},{18,2},{19,3},{20,4},{21,5},{22,6},{23,7},{24,8},{25... | collective-permute-start | bytes 983048 | tf_op jit(solution)/shard_map/ppermute | solution.py:408
  (6 other events, 14.4 us)

commit v5 on v4

--- a/solution.py
+++ b/solution.py
@@ -28,6 +28,13 @@
 
 def dot(a, b, dims):
     return lax.dot_general(a, b, (dims, ((), ())), preferred_element_type=jnp.float32)
+
+
+def add_tiles(tiles, block, start):
+    for i in range(block.shape[1] // 128):
+        tile = start // 128 + i
+        part = block[:, i * 128 : (i + 1) * 128]
+        tiles[tile] = part if tile not in tiles else tiles[tile] + part
 
 
 NT = ((1,), (1,))
@@ -91,7 +98,8 @@
                 )
             )
             outs[-1].start()
-            work[half] = x[:, half * CHUNK : (half + 1) * CHUNK].astype(jnp.float32)
+            tiles = {}
+            add_tiles(tiles, x[:, half * CHUNK : (half + 1) * CHUNK].astype(jnp.float32), 0)
             for head in range(CHUNK_HEADS):
                 start, stop, low, high = head_window(head)
                 query = qkv_ref[half * 3, :, start:stop]
@@ -101,7 +109,9 @@
                 weights = jnp.exp(scores - jnp.max(scores, axis=1, keepdims=True))
                 weights = weights / jnp.sum(weights, axis=1, keepdims=True)
                 probs_ref[half * CHUNK_HEADS + head] = weights
-                work[half, :, start:stop] += dot(weights.astype(jnp.bfloat16), value, NN)
+                add_tiles(tiles, dot(weights.astype(jnp.bfloat16), value, NN), start)
+            for tile, part in tiles.items():
+                work[half, :, tile * 128 : (tile + 1) * 128] = part
             outs.append(
                 pltpu.make_async_copy(probs_ref.at[heads], probs_hbm.at[heads], out_sems.at[2 + half])
             )
@@ -208,9 +218,7 @@
             work[half] = inverse * (work[half] - mean - norm_ref[half] * along)
         total = jnp.zeros((work.shape[1], vis), f32)
         for half in range(2):
-            mixed = [jnp.zeros((work.shape[1], CHUNK), f32) for _ in range(3)]
-            for kind in range(3):
-                mix[kind] = mixed[kind]
+            mixed = [{}, {}, {}]
             for head in range(CHUNK_HEADS):
                 start, stop, low, high = head_window(head)
                 grad = head_only(work[half, :, start:stop].astype(bf16), low, high)
@@ -219,15 +227,18 @@
                 value = qkv_ref[half * 3 + 2, :, start:stop]
                 probs = probs_ref[half * CHUNK_HEADS + head]
                 grad_weights = dot(grad, value, NT)
-                mix[2, :, start:stop] += dot(probs.astype(bf16), grad, TN)
                 inner = jnp.sum(grad_weights * probs, axis=1, keepdims=True)
                 scores = (probs * (grad_weights - inner) * HDIM ** (-0.5)).astype(bf16)
-                mix[0, :, start:stop] += dot(scores, key, NN)
-                mix[1, :, start:stop] += dot(scores, query, TN)
+                add_tiles(mixed[2], dot(probs.astype(bf16), grad, TN), start)
+                add_tiles(mixed[0], dot(scores, key, NN), start)
+                add_tiles(mixed[1], dot(scores, query, TN), start)
+            for kind in range(3):
+                for tile, part in mixed[kind].items():
+                    mix[kind, :, tile * 128 : (tile + 1) * 128] = part.astype(bf16)
             for kind in range(3):
                 i = half * 3 + kind
                 copies[i].wait()
-                total = total + dot(mix[kind].astype(bf16), w_buf[i], NT)
+                total = total + dot(mix[kind], w_buf[i], NT)
         for half in range(2):
             columns = slice(half * CHUNK, (half + 1) * CHUNK)
             out_ref[:, columns] = (work[half] + total[:, columns]).astype(bf16)
@@ -247,7 +258,7 @@
         scratch_shapes=[
             pltpu.VMEM((6, vis, CHUNK), bf16),
             pltpu.VMEM((2, length, CHUNK), f32),
-            pltpu.VMEM((3, length, CHUNK), f32),
+            pltpu.VMEM((3, length, CHUNK), bf16),
             pltpu.SemaphoreType.DMA((6,)),
         ],
         compiler_params=pltpu.CompilerParams(vmem_limit_bytes=40 << 20),
@@ -453,7 +464,7 @@
     give = [give_columns(flag, flag, w_mine, 0, sizes[0])]
     give.append(give_columns(flag, give[0], w_mine, first, sizes[1]))
     got = [passed_along(block, "grp", -1) for block in give]
-    got_cot = passed_along(give_cotangent(flag, give[1], rms_gain, cot_mine, half), "grp", -1)
+    give_cot = give_cotangent(flag, give[1], rms_gain, cot_mine, half)
 
     embedded, qkv, probs, norm, inverse = encoder_forward(flag, frame, w_qkv[0], ln_gain)
 
@@ -463,6 +474,8 @@
         pieces = pieces.transpose(0, 2, 1, 3).reshape(dp_count, tokens_here, depth)
     swapped = lax.all_to_all(pieces, "dp", 0, 0)
     arrived = passed_along(swapped, "grp", 1)
+    swapped, give_cot = lax.optimization_barrier((swapped, give_cot))
+    got_cot = passed_along(give_cot, "grp", -1)
     features = arrange(arrange_in_kernel, "arrange_in", (flag, order), swapped, arrived)
     features = jnp.concatenate(
         [features] + [sent_tp(features, tp_count - s) for s in range(1, tp_count)], axis=1

time: 179 us -> 173 us (0.966)
  blocking collectives: 43.2 us -> 38.8 us
    psum x1, blocking collectives: 11.6 us -> 7.65 us  [per_device(): lax.psum(rotated(sums, (tp_count - tp_index) % tp_count), ('grp', 'tp'))]
    ppermute x6, waiting for transfers between devices: 11.4 us -> 13.9 us  [sent_across(): lax.ppermute(block, 'dp', [(i, i ^ 1) for i in range(lax.axis_size('dp'))])]
    ppermute x5, waiting for transfers between devices: 17.7 us -> 15.8 us  [passed_along(): return lax.ppermute(block, axis, route)]
  transfers between devices with their start and end apart: 25 -> 25, of which waited for: 14 -> 16; matrix products, arithmetic and copies ran while one was open for 6% -> 5% of each run, Pallas kernels for 8% -> 8%
where the time goes in v5:
time: 173 us; the launch traced here: 172 us
  waiting for transfers between devices  63.3 us (37%)
  blocking collectives  38.8 us (22%)
  starting transfers between devices  33.8 us (20%)
  Pallas kernels  23.1 us (13%)
  other arithmetic  8.02 us (5%)
  matrix products  2.64 us (2%)
  local copies, waits for them, and re-layouts  1.95 us (1%)
    ppermute x12, waiting for transfers between devices, sent_round(): return lax.ppermute(block, 'dp', [(i, i ^ 2 * move) for i in range(count)])  31.9 us
    ppermute x12, starting transfers between devices, sent_round(): return lax.ppermute(block, 'dp', [(i, i ^ 2 * move) for i in range(count)])  19.9 us
    all_to_all x1, blocking collectives, per_device(): swapped = lax.all_to_all(pieces, 'dp', 0, 0)  18 us
    ppermute x5, waiting for transfers between devices, passed_along(): return lax.ppermute(block, axis, route)  15.8 us
    ppermute x6, waiting for transfers between devices, sent_across(): lax.ppermute(block, 'dp', [(i, i ^ 1) for i in range(lax.axis_size('dp'))])  13.9 us
    all_to_all x1, blocking collectives, per_device(): whole = lax.all_to_all(whole, 'dp', 0, 0)  13.1 us
    pallas_call x1, Pallas kernels, encoder_backward(): pl.pallas_call(encoder_backward_kernel, out_shape=jax.ShapeDtypeStruct((l...  8.92 us
    pallas_call x1, Pallas kernels, encoder_forward(): pl.pallas_call(encoder_forward_kernel, out_shape=(jax.ShapeDtypeStruct((8...  7.77 us
  transfers between devices with their start and end apart: 25, of which 16 were waited for; matrix products, arithmetic and copies ran while one was open for 5% of the time, Pallas kernels for 8%

profile of v5, /device:TPU:0, one launch (start us, length us, event | category | flops | bytes accessed | tf_op | source)
XLA Modules:
  0.0 172.3 jit_solution(9470833184981947989)
XLA Ops:
  0.0 1.4 collective-permute-start.3
  1.5 7.8 %encoder_forward.1 = (bf16[8,32,640]{2,1,0:T(8,128)(2,1)S(1)}, bf16[6,128,640]{2,1,0:T(8,128)(2,1)}, f32[16,128,128]{2,1,0:T(8,128)}, f32[2,128,640]{2,1,0:T(8,128)}, f32[128,1]{1,0:T(8,128)S(1)}) custom-call(s32[1]{0:T(128)} %bitcast.flag_ref.refs_0_.refs_1_, bf16[128,1280]{1,0:T(8,128)(2,1)S(1)} %bitcast.116, bf16[1,1280]{1,0:T(2,128)(2,1)S(1)} %copy-done.9, ...), custom_call_target="tpu_custom_call" | custom-call | flops 1000 | bytes 1000 | tf_op jit(solution)/shard_map/encoder_forward/pallas_call | solution.py:151
  9.2 18.0 %all_to_all.10.a_ref = bf16[8,32,640]{2,1,0:T(8,128)(2,1)S(1)} all-to-all(bf16[8,32,640]{2,1,0:T(8,128)(2,1)S(1)} %get-tuple-element.34), channel_id=1, replica_groups=mesh['grp'=2,'dp'=8,'tp'=2] {'dp'}, dimensions={0} | all-to-all | bytes 655360 | tf_op jit(solution)/shard_map/all_to_all | solution.py:475
  27.2 2.2 %collective-permute-start.1 = (bf16[8,32,640]{2,1,0:T(8,128)(2,1)S(1)}, bf16[8,32,640]{2,1,0:T(8,128)(2,1)}, u32[]{:S(2)}, u32[]{:S(2)}) collective-permute-start(bf16[8,32,640]{2,1,0:T(8,128)(2,1)S(1)} %all_to_all.10.a_ref), channel_id=1, source_target_pairs={{0,16},{1,17},{2,18},{3,19},{4,20},{5,21},{6,22},{7,23},{8,24},{9,... | collective-permute-start | bytes 983048 | tf_op jit(solution)/shard_map/ppermute | solution.py:419
  30.2 3.4 %collective-permute-done.1.b_ref = bf16[8,32,640]{2,1,0:T(8,128)(2,1)} collective-permute-done((bf16[8,32,640]{2,1,0:T(8,128)(2,1)S(1)}, bf16[8,32,640]{2,1,0:T(8,128)(2,1)}, u32[]{:S(2)}, u32[]{:S(2)}) %collective-permute-start.1) | collective-permute-done | bytes 327712 | tf_op jit(solution)/shard_map/ppermute | solution.py:419
  34.8 1.3 collective-permute-start.9
  38.0 2.5 %partial_products.2 = (bf16[2,64,1152]{2,1,0:T(8,128)(2,1)S(1)}, bf16[2,64,1152]{2,1,0:T(8,128)(2,1)S(1)}, f32[64,1152]{1,0:T(8,128)S(1)}, f32[64,1152]{1,0:T(8,...) custom-call(s32[1]{0:T(128)} %bitcast.flag_ref.refs_0_.refs_1_, ...), custom_call_target="tpu_custom_call" | custom-call | flops 1000 | bytes 1000 | tf_op jit(solution)/shard_map/partial_products/pallas_call | solution.py:371
  40.6 1.6 collective-permute-start.4
  44.0 6.5 %collective-permute-done.4 = bf16[2,64,1152]{2,1,0:T(8,128)(2,1)S(1)} collective-permute-done((bf16[2,64,1152]{2,1,0:T(8,128)(2,1)S(1)}, bf16[2,64,1152]{2,1,0:T(8,128)(2,1)S(1)}, u32[]{:S(2)}, u32[]{:S(2)}) %collective-permute-start.4) | collective-permute-done | bytes 294944 | tf_op jit(solution)/shard_map/ppermute | solution.py:438
  51.2 5.0 %collective-permute-done.5 = bf16[2,64,1152]{2,1,0:T(8,128)(2,1)S(1)} collective-permute-done((bf16[2,64,1152]{2,1,0:T(8,128)(2,1)S(1)}, bf16[2,64,1152]{2,1,0:T(8,128)(2,1)S(1)}, u32[]{:S(2)}, u32[]{:S(2)}) %collective-permute-start.5) | collective-permute-done | bytes 294944 | tf_op jit(solution)/shard_map/ppermute | solution.py:438
  58.0 2.6 %collective-permute-start.7 = (bf16[64,1152]{1,0:T(8,128)(2,1)}, bf16[64,1152]{1,0:T(8,128)(2,1)}, u32[]{:S(2)}, u32[]{:S(2)}) collective-permute-start(bf16[64,1152]{1,0:T(8,128)(2,1)} %get-tuple-element.44), channel_id=1, source_target_pairs={{0,8},{2,10},{4,12},{6,14},{8,0},{10,2},{12,4},{14,6},{1,9},{3,11}... | collective-permute-start | bytes 442376 | tf_op jit(solution)/shard_map/ppermute | solution.py:434
  61.6 1.4 collective-permute-start
  63.0 1.7 collective-permute-done.9.refs_2_
  64.7 2.2 %partial_products.3 = (bf16[2,64,896]{2,1,0:T(8,128)(2,1)S(1)}, bf16[2,64,896]{2,1,0:T(8,128)(2,1)S(1)}, f32[64,896]{1,0:T(8,128)S(1)}, f32[64,896]{1,0:T(8,128)...) custom-call(s32[1]{0:T(128)} %bitcast.flag_ref.refs_0_.refs_1_, ...), custom_call_target="tpu_custom_call" | custom-call | flops 1000 | bytes 1000 | tf_op jit(solution)/shard_map/partial_products/pallas_call | solution.py:371
  69.0 3.2 %collective-permute-done.7 = bf16[64,1152]{1,0:T(8,128)(2,1)} collective-permute-done((bf16[64,1152]{1,0:T(8,128)(2,1)}, bf16[64,1152]{1,0:T(8,128)(2,1)}, u32[]{:S(2)}, u32[]{:S(2)}) %collective-permute-start.7) | collective-permute-done | bytes 147488 | tf_op jit(solution)/shard_map/ppermute | solution.py:434
  73.7 1.7 %collective-permute-done.10 = bf16[2,64,896]{2,1,0:T(8,128)(2,1)S(1)} collective-permute-done((bf16[2,64,896]{2,1,0:T(8,128)(2,1)S(1)}, bf16[2,64,896]{2,1,0:T(8,128)(2,1)S(1)}, u32[]{:S(2)}, u32[]{:S(2)}) %collective-permute-start.10) | collective-permute-done | bytes 229408 | tf_op jit(solution)/shard_map/ppermute | solution.py:438
  75.5 3.0 %collective-permute-start.14 = (bf16[64,896]{1,0:T(8,128)(2,1)S(1)}, bf16[64,896]{1,0:T(8,128)(2,1)S(1)}, u32[]{:S(2)}, u32[]{:S(2)}) collective-permute-start(bf16[64,896]{1,0:T(8,128)(2,1)S(1)} %fusion.23), channel_id=1, source_target_pairs={{0,12},{2,14},{4,8},{6,10},{8,4},{10,6},{12,0},{14,2},{1,13},{3,15... | collective-permute-start | bytes 344072 | tf_op jit(solution)/shard_map/ppermute | solution.py:434
  80.3 2.6 %collective-permute-start.13 = (bf16[64,896]{1,0:T(8,128)(2,1)S(1)}, bf16[64,896]{1,0:T(8,128)(2,1)S(1)}, u32[]{:S(2)}, u32[]{:S(2)}) collective-permute-start(bf16[64,896]{1,0:T(8,128)(2,1)S(1)} %get-tuple-element.73), channel_id=1, source_target_pairs={{0,8},{2,10},{4,12},{6,14},{8,0},{10,2},{12,4},{14,6},{1,9},{3,11}... | collective-permute-start | bytes 344072 | tf_op jit(solution)/shard_map/ppermute | solution.py:434
  83.0 4.0 %collective-permute-done.12 = bf16[64,896]{1,0:T(8,128)(2,1)S(1)} collective-permute-done((bf16[64,896]{1,0:T(8,128)(2,1)S(1)}, bf16[64,896]{1,0:T(8,128)(2,1)S(1)}, u32[]{:S(2)}, u32[]{:S(2)}) %collective-permute-start.12) | collective-permute-done | bytes 114720 | tf_op jit(solution)/shard_map/ppermute | solution.py:434
  88.2 7.7 %psum.7 = f32[2,32,2]{1,2,0:T(2,128)S(1)} all-reduce(f32[2,32,2]{1,2,0:T(2,128)S(1)} %maximum_select_fusion), channel_id=1, replica_groups=mesh['grp'=2,'dp'=8,'tp'=2] {'grp','tp'}, use_global_device_ids=true, to_apply=%region_4.5 | all-reduce | flops 128 | bytes 1024 | tf_op jit(solution)/shard_map/psum | solution.py:513
  97.9 2.0 %collective-permute-start.17 = (bf16[64,1152]{1,0:T(8,128)(2,1)S(1)}, bf16[64,1152]{1,0:T(8,128)(2,1)S(1)}, u32[]{:S(2)}, u32[]{:S(2)}) collective-permute-start(bf16[64,1152]{1,0:T(8,128)(2,1)S(1)} %subtract_convert_fusion), channel_id=1, source_target_pairs={{0,12},{2,14},{4,8},{6,10},{8,4},{10,6},{12,0},{14,2},{1,13},{3,15... | collective-permute-start | bytes 442376 | tf_op jit(solution)/shard_map/ppermute | solution.py:434
  99.9 2.5 %collective-permute-start.15 = (bf16[64,1152]{1,0:T(8,128)(2,1)S(1)}, bf16[64,1152]{1,0:T(8,128)(2,1)S(1)}, u32[]{:S(2)}, u32[]{:S(2)}) collective-permute-start(bf16[64,1152]{1,0:T(8,128)(2,1)S(1)} %subtract_convert_fusion), channel_id=1, source_target_pairs={{0,4},{2,6},{4,0},{6,2},{8,12},{10,14},{12,8},{14,10},{1,5},{3,7},... | collective-permute-start | bytes 442376 | tf_op jit(solution)/shard_map/ppermute | solution.py:434
  102.4 4.2 %collective-permute-done.17 = bf16[64,1152]{1,0:T(8,128)(2,1)S(1)} collective-permute-done((bf16[64,1152]{1,0:T(8,128)(2,1)S(1)}, bf16[64,1152]{1,0:T(8,128)(2,1)S(1)}, u32[]{:S(2)}, u32[]{:S(2)}) %collective-permute-start.17) | collective-permute-done | bytes 147488 | tf_op jit(solution)/shard_map/ppermute | solution.py:434
  106.6 5.1 %collective-permute-done.16 = bf16[64,1152]{1,0:T(8,128)(2,1)S(1)} collective-permute-done((bf16[64,1152]{1,0:T(8,128)(2,1)S(1)}, bf16[64,1152]{1,0:T(8,128)(2,1)S(1)}, u32[]{:S(2)}, u32[]{:S(2)}) %collective-permute-start.16) | collective-permute-done | bytes 147488 | tf_op jit(solution)/shard_map/ppermute | solution.py:434
  111.7 2.4 %collective-permute-start.21 = (bf16[2,64,896]{2,1,0:T(8,128)(2,1)S(1)}, bf16[2,64,896]{2,1,0:T(8,128)(2,1)S(1)}, u32[]{:S(2)}, u32[]{:S(2)}) collective-permute-start(bf16[2,64,896]{2,1,0:T(8,128)(2,1)S(1)} %pad_maximum_fusion.5), channel_id=1, source_target_pairs={{0,12},{2,14},{4,8},{6,10},{8,4},{10,6},{12,0},{14,2},{1,13},{3,15... | collective-permute-start | bytes 688136 | tf_op jit(solution)/shard_map/ppermute | solution.py:434
  114.1 2.1 %collective-permute-start.19 = (bf16[2,64,896]{2,1,0:T(8,128)(2,1)S(1)}, bf16[2,64,896]{2,1,0:T(8,128)(2,1)S(1)}, u32[]{:S(2)}, u32[]{:S(2)}) collective-permute-start(bf16[2,64,896]{2,1,0:T(8,128)(2,1)S(1)} %pad_maximum_fusion.5), channel_id=1, source_target_pairs={{0,4},{2,6},{4,0},{6,2},{8,12},{10,14},{12,8},{14,10},{1,5},{3,7},... | collective-permute-start | bytes 688136 | tf_op jit(solution)/shard_map/ppermute | solution.py:434
  117.3 4.9 %collective-permute-done.21 = bf16[2,64,896]{2,1,0:T(8,128)(2,1)S(1)} collective-permute-done((bf16[2,64,896]{2,1,0:T(8,128)(2,1)S(1)}, bf16[2,64,896]{2,1,0:T(8,128)(2,1)S(1)}, u32[]{:S(2)}, u32[]{:S(2)}) %collective-permute-start.21) | collective-permute-done | bytes 229408 | tf_op jit(solution)/shard_map/ppermute | solution.py:434
  122.2 10.7 %collective-permute-done.20 = bf16[2,64,896]{2,1,0:T(8,128)(2,1)S(1)} collective-permute-done((bf16[2,64,896]{2,1,0:T(8,128)(2,1)S(1)}, bf16[2,64,896]{2,1,0:T(8,128)(2,1)S(1)}, u32[]{:S(2)}, u32[]{:S(2)}) %collective-permute-start.20) | collective-permute-done | bytes 229408 | tf_op jit(solution)/shard_map/ppermute | solution.py:434
  136.1 1.6 collective-permute-done.23
  139.0 10.3 %collective-permute-done.24.b_ref = bf16[8,32,640]{2,1,0:T(8,128)(2,1)S(1)} collective-permute-done((bf16[8,32,640]{2,1,0:T(8,128)(2,1)S(1)}, bf16[8,32,640]{2,1,0:T(8,128)(2,1)S(1)}, u32[]{:S(2)}, u32[]{:S(2)}) %collective-permute-start.24) | collective-permute-done | bytes 327712 | tf_op jit(solution)/shard_map/ppermute | solution.py:419
  150.0 13.1 %all_to_all.11.grad_ref = bf16[8,32,640]{2,1,0:T(8,128)(2,1)S(1)} all-to-all(bf16[8,32,640]{2,1,0:T(8,128)(2,1)S(1)} %arrange_out.1), channel_id=1, replica_groups=mesh['grp'=2,'dp'=8,'tp'=2] {'dp'}, dimensions={0} | all-to-all | bytes 655360 | tf_op jit(solution)/shard_map/all_to_all | solution.py:550
  163.2 8.9 %encoder_backward.1 = bf16[128,1280]{1,0:T(8,128)(2,1)} custom-call(s32[1]{0:T(128)} %bitcast.flag_ref.refs_0_.refs_1_, bf16[8,32,640]{2,1,0:T(8,128)(2,1)S(1)} %all_to_all.11.grad_ref, bf16[1,1280]{1,0:T(2,128)(2,1)S(1)} %copy-done.9, bf16[6,128,640]{2,1,0:T(8,128)(2,1)S(1)} %copy-done.2, f32[16,128,128]{2,1,0:T(8,128)S(1)} %copy-done.1, ...), custom_call_target="tpu_custom_call" | custom-call | flops 1000 | bytes 1000 | tf_op jit(solution)/shard_map/encoder_backward/pallas_call | solution.py:251
  (102 shorter events, 24.2 us)
Async XLA Ops:
  0.0 38.0 %collective-permute-start.3 = (bf16[640,1152]{1,0:T(8,128)(2,1)S(1)}, bf16[640,1152]{1,0:T(8,128)(2,1)}, u32[]{:S(2)}, u32[]{:S(2)}) collective-permute-start(bf16[640,1152]{1,0:T(8,128)(2,1)S(1)} %give_columns.2.refs_1_), channel_id=1, source_target_pairs={{16,0},{17,1},{18,2},{19,3},{20,4},{21,5},{22,6},{23,7},{24,8},{25... | collective-permute-start | bytes 4423688 | tf_op jit(solution)/shard_map/ppermute | solution.py:419
  27.2 6.4 %collective-permute-start.1 = (bf16[8,32,640]{2,1,0:T(8,128)(2,1)S(1)}, bf16[8,32,640]{2,1,0:T(8,128)(2,1)}, u32[]{:S(2)}, u32[]{:S(2)}) collective-permute-start(bf16[8,32,640]{2,1,0:T(8,128)(2,1)S(1)} %all_to_all.10.a_ref), channel_id=1, source_target_pairs={{0,16},{1,17},{2,18},{3,19},{4,20},{5,21},{6,22},{7,23},{8,24},{9,... | collective-permute-start | bytes 983048 | tf_op jit(solution)/shard_map/ppermute | solution.py:419
  29.4 6.7 %copy-start.13 = (s32[2]{0:T(128)S(1)}, s32[2]{0:T(128)}, u32[]{:S(2)}) copy-start(s32[2]{0:T(128)} %param.8) | copy-start | bytes 28
  34.7 2.0 %collective-permute-start.2 = (bf16[8,32,640]{2,1,0:T(8,128)(2,1)S(1)}, bf16[8,32,640]{2,1,0:T(8,128)(2,1)}, u32[]{:S(2)}, u32[]{:S(2)}) collective-permute-start(bf16[8,32,640]{2,1,0:T(8,128)(2,1)S(1)} %arrange_in.1), channel_id=1, source_target_pairs={{0,1},{1,0},{2,3},{3,2},{4,5},{5,4},{6,7},{7,6},{8,9},{9,8},{10,11... | collective-permute-start | bytes 983048 | tf_op jit(solution)/shard_map/ppermute | solution.py:443
  34.8 29.9 %collective-permute-start.9 = (bf16[640,896]{1,0:T(8,128)(2,1)S(1)}, bf16[640,896]{1,0:T(8,128)(2,1)}, u32[]{:S(2)}, u32[]{:S(2)}) collective-permute-start(bf16[640,896]{1,0:T(8,128)(2,1)S(1)} %give_columns.3.after_ref), channel_id=1, source_target_pairs={{16,0},{17,1},{18,2},{19,3},{20,4},{21,5},{22,6},{23,7},{24,8},{25... | collective-permute-start | bytes 3440648 | tf_op jit(solution)/shard_map/ppermute | solution.py:419
  40.6 10.7 %copy-start.6 = (f32[64,1152]{1,0:T(8,128)}, f32[64,1152]{1,0:T(8,128)S(1)}, u32[]{:S(2)}) copy-start(f32[64,1152]{1,0:T(8,128)S(1)} %get-tuple-element.37) | copy-start | bytes 884740
  40.6 9.9 %collective-permute-start.4 = (bf16[2,64,1152]{2,1,0:T(8,128)(2,1)S(1)}, bf16[2,64,1152]{2,1,0:T(8,128)(2,1)S(1)}, u32[]{:S(2)}, u32[]{:S(2)}) collective-permute-start(bf16[2,64,1152]{2,1,0:T(8,128)(2,1)S(1)} %get-tuple-element.38), channel_id=1, source_target_pairs={{0,2},{2,0},{4,6},{6,4},{8,10},{10,8},{12,14},{14,12},{1,3},{3,1},... | collective-permute-start | bytes 884744 | tf_op jit(solution)/shard_map/ppermute | solution.py:438
  43.5 12.7 %collective-permute-start.5 = (bf16[2,64,1152]{2,1,0:T(8,128)(2,1)S(1)}, bf16[2,64,1152]{2,1,0:T(8,128)(2,1)S(1)}, u32[]{:S(2)}, u32[]{:S(2)}) collective-permute-start(bf16[2,64,1152]{2,1,0:T(8,128)(2,1)S(1)} %get-tuple-element.40), channel_id=1, source_target_pairs={{0,2},{2,0},{4,6},{6,4},{8,10},{10,8},{12,14},{14,12},{1,3},{3,1},... | collective-permute-start | bytes 884744 | tf_op jit(solution)/shard_map/ppermute | solution.py:438
  57.0 10.8 %collective-permute-start.6 = (bf16[64,1152]{1,0:T(8,128)(2,1)}, bf16[64,1152]{1,0:T(8,128)(2,1)S(1)}, u32[]{:S(2)}, u32[]{:S(2)}) collective-permute-start(bf16[64,1152]{1,0:T(8,128)(2,1)} %get-tuple-element.43), channel_id=1, source_target_pairs={{0,4},{2,6},{4,0},{6,2},{8,12},{10,14},{12,8},{14,10},{1,5},{3,7},... | collective-permute-start | bytes 442376 | tf_op jit(solution)/shard_map/ppermute | solution.py:434
  58.0 14.2 %collective-permute-start.7 = (bf16[64,1152]{1,0:T(8,128)(2,1)}, bf16[64,1152]{1,0:T(8,128)(2,1)}, u32[]{:S(2)}, u32[]{:S(2)}) collective-permute-start(bf16[64,1152]{1,0:T(8,128)(2,1)} %get-tuple-element.44), channel_id=1, source_target_pairs={{0,8},{2,10},{4,12},{6,14},{8,0},{10,2},{12,4},{14,6},{1,9},{3,11}... | collective-permute-start | bytes 442376 | tf_op jit(solution)/shard_map/ppermute | solution.py:434
  60.6 11.6 %collective-permute-start.8 = (bf16[64,1152]{1,0:T(8,128)(2,1)}, bf16[64,1152]{1,0:T(8,128)(2,1)}, u32[]{:S(2)}, u32[]{:S(2)}) collective-permute-start(bf16[64,1152]{1,0:T(8,128)(2,1)} %fusion.17), channel_id=1, source_target_pairs={{0,12},{2,14},{4,8},{6,10},{8,4},{10,6},{12,0},{14,2},{1,13},{3,15... | collective-permute-start | bytes 442376 | tf_op jit(solution)/shard_map/ppermute | solution.py:434
  61.6 10.6 %copy-start.7 = (f32[64,1152]{1,0:T(8,128)S(1)}, f32[64,1152]{1,0:T(8,128)}, u32[]{:S(2)}) copy-start(f32[64,1152]{1,0:T(8,128)} %copy-done.6) | copy-start | bytes 884740
  61.6 10.6 %copy-start.12 = (bf16[2,64,1152]{2,1,0:T(8,128)(2,1)S(1)}, bf16[2,64,1152]{2,1,0:T(8,128)(2,1)}, u32[]{:S(2)}) copy-start(bf16[2,64,1152]{2,1,0:T(8,128)(2,1)} %copy-done.11) | copy-start | bytes 884740
  61.6 11.9 %collective-permute-start = (bf16[80,2048]{1,0:T(8,128)(2,1)}, bf16[80,2048]{1,0:T(8,128)(2,1)S(1)}, u32[]{:S(2)}, u32[]{:S(2)}) collective-permute-start(bf16[80,2048]{1,0:T(8,128)(2,1)} %copy-done.5), channel_id=1, source_target_pairs={{16,0},{17,1},{18,2},{19,3},{20,4},{21,5},{22,6},{23,7},{24,8},{25... | collective-permute-start | bytes 983048 | tf_op jit(solution)/shard_map/ppermute | solution.py:419
  66.9 8.6 %collective-permute-start.10 = (bf16[2,64,896]{2,1,0:T(8,128)(2,1)S(1)}, bf16[2,64,896]{2,1,0:T(8,128)(2,1)S(1)}, u32[]{:S(2)}, u32[]{:S(2)}) collective-permute-start(bf16[2,64,896]{2,1,0:T(8,128)(2,1)S(1)} %get-tuple-element.49), channel_id=1, source_target_pairs={{0,2},{2,0},{4,6},{6,4},{8,10},{10,8},{12,14},{14,12},{1,3},{3,1},... | collective-permute-start | bytes 688136 | tf_op jit(solution)/shard_map/ppermute | solution.py:438
  67.8 11.4 %collective-permute-start.11 = (bf16[2,64,896]{2,1,0:T(8,128)(2,1)S(1)}, bf16[2,64,896]{2,1,0:T(8,128)(2,1)S(1)}, u32[]{:S(2)}, u32[]{:S(2)}) collective-permute-start(bf16[2,64,896]{2,1,0:T(8,128)(2,1)S(1)} %get-tuple-element.51), channel_id=1, source_target_pairs={{0,2},{2,0},{4,6},{6,4},{8,10},{10,8},{12,14},{14,12},{1,3},{3,1},... | collective-permute-start | bytes 688136 | tf_op jit(solution)/shard_map/ppermute | solution.py:438
  75.5 7.6 %collective-permute-start.14 = (bf16[64,896]{1,0:T(8,128)(2,1)S(1)}, bf16[64,896]{1,0:T(8,128)(2,1)S(1)}, u32[]{:S(2)}, u32[]{:S(2)}) collective-permute-start(bf16[64,896]{1,0:T(8,128)(2,1)S(1)} %fusion.23), channel_id=1, source_target_pairs={{0,12},{2,14},{4,8},{6,10},{8,4},{10,6},{12,0},{14,2},{1,13},{3,15... | collective-permute-start | bytes 344072 | tf_op jit(solution)/shard_map/ppermute | solution.py:434
  79.3 7.8 %collective-permute-start.12 = (bf16[64,896]{1,0:T(8,128)(2,1)S(1)}, bf16[64,896]{1,0:T(8,128)(2,1)S(1)}, u32[]{:S(2)}, u32[]{:S(2)}) collective-permute-start(bf16[64,896]{1,0:T(8,128)(2,1)S(1)} %get-tuple-element.72), channel_id=1, source_target_pairs={{0,4},{2,6},{4,0},{6,2},{8,12},{10,14},{12,8},{14,10},{1,5},{3,7},... | collective-permute-start | bytes 344072 | tf_op jit(solution)/shard_map/ppermute | solution.py:434
  80.3 6.7 %collective-permute-start.13 = (bf16[64,896]{1,0:T(8,128)(2,1)S(1)}, bf16[64,896]{1,0:T(8,128)(2,1)S(1)}, u32[]{:S(2)}, u32[]{:S(2)}) collective-permute-start(bf16[64,896]{1,0:T(8,128)(2,1)S(1)} %get-tuple-element.73), channel_id=1, source_target_pairs={{0,8},{2,10},{4,12},{6,14},{8,0},{10,2},{12,4},{14,6},{1,9},{3,11}... | collective-permute-start | bytes 344072 | tf_op jit(solution)/shard_map/ppermute | solution.py:434
  97.0 5.4 %collective-permute-start.18 = (bf16[64,896]{1,0:T(8,128)(2,1)S(1)}, bf16[64,896]{1,0:T(8,128)(2,1)S(1)}, u32[]{:S(2)}, u32[]{:S(2)}) collective-permute-start(bf16[64,896]{1,0:T(8,128)(2,1)S(1)} %subtract_convert_fusion.1), channel_id=1, source_target_pairs={{0,2},{2,0},{4,6},{6,4},{8,10},{10,8},{12,14},{14,12},{1,3},{3,1},... | collective-permute-start | bytes 344072 | tf_op jit(solution)/shard_map/ppermute | solution.py:438
  97.9 8.6 %collective-permute-start.17 = (bf16[64,1152]{1,0:T(8,128)(2,1)S(1)}, bf16[64,1152]{1,0:T(8,128)(2,1)S(1)}, u32[]{:S(2)}, u32[]{:S(2)}) collective-permute-start(bf16[64,1152]{1,0:T(8,128)(2,1)S(1)} %subtract_convert_fusion), channel_id=1, source_target_pairs={{0,12},{2,14},{4,8},{6,10},{8,4},{10,6},{12,0},{14,2},{1,13},{3,15... | collective-permute-start | bytes 442376 | tf_op jit(solution)/shard_map/ppermute | solution.py:434
  99.9 11.7 %collective-permute-start.16 = (bf16[64,1152]{1,0:T(8,128)(2,1)S(1)}, bf16[64,1152]{1,0:T(8,128)(2,1)S(1)}, u32[]{:S(2)}, u32[]{:S(2)}) collective-permute-start(bf16[64,1152]{1,0:T(8,128)(2,1)S(1)} %subtract_convert_fusion), channel_id=1, source_target_pairs={{0,8},{2,10},{4,12},{6,14},{8,0},{10,2},{12,4},{14,6},{1,9},{3,11}... | collective-permute-start | bytes 442376 | tf_op jit(solution)/shard_map/ppermute | solution.py:434
  99.9 11.7 %collective-permute-start.15 = (bf16[64,1152]{1,0:T(8,128)(2,1)S(1)}, bf16[64,1152]{1,0:T(8,128)(2,1)S(1)}, u32[]{:S(2)}, u32[]{:S(2)}) collective-permute-start(bf16[64,1152]{1,0:T(8,128)(2,1)S(1)} %subtract_convert_fusion), channel_id=1, source_target_pairs={{0,4},{2,6},{4,0},{6,2},{8,12},{10,14},{12,8},{14,10},{1,5},{3,7},... | collective-permute-start | bytes 442376 | tf_op jit(solution)/shard_map/ppermute | solution.py:434
  111.7 10.5 %collective-permute-start.21 = (bf16[2,64,896]{2,1,0:T(8,128)(2,1)S(1)}, bf16[2,64,896]{2,1,0:T(8,128)(2,1)S(1)}, u32[]{:S(2)}, u32[]{:S(2)}) collective-permute-start(bf16[2,64,896]{2,1,0:T(8,128)(2,1)S(1)} %pad_maximum_fusion.5), channel_id=1, source_target_pairs={{0,12},{2,14},{4,8},{6,10},{8,4},{10,6},{12,0},{14,2},{1,13},{3,15... | collective-permute-start | bytes 688136 | tf_op jit(solution)/shard_map/ppermute | solution.py:434
  114.1 18.8 %collective-permute-start.20 = (bf16[2,64,896]{2,1,0:T(8,128)(2,1)S(1)}, bf16[2,64,896]{2,1,0:T(8,128)(2,1)S(1)}, u32[]{:S(2)}, u32[]{:S(2)}) collective-permute-start(bf16[2,64,896]{2,1,0:T(8,128)(2,1)S(1)} %pad_maximum_fusion.5), channel_id=1, source_target_pairs={{0,8},{2,10},{4,12},{6,14},{8,0},{10,2},{12,4},{14,6},{1,9},{3,11}... | collective-permute-start | bytes 688136 | tf_op jit(solution)/shard_map/ppermute | solution.py:434
  114.1 18.8 %collective-permute-start.19 = (bf16[2,64,896]{2,1,0:T(8,128)(2,1)S(1)}, bf16[2,64,896]{2,1,0:T(8,128)(2,1)S(1)}, u32[]{:S(2)}, u32[]{:S(2)}) collective-permute-start(bf16[2,64,896]{2,1,0:T(8,128)(2,1)S(1)} %pad_maximum_fusion.5), channel_id=1, source_target_pairs={{0,4},{2,6},{4,0},{6,2},{8,12},{10,14},{12,8},{14,10},{1,5},{3,7},... | collective-permute-start | bytes 688136 | tf_op jit(solution)/shard_map/ppermute | solution.py:434
  116.2 18.7 %collective-permute-start.22 = (bf16[4,64,1152]{2,1,0:T(8,128)(2,1)S(1)}, bf16[4,64,1152]{2,1,0:T(8,128)(2,1)S(1)}, u32[]{:S(2)}, u32[]{:S(2)}) collective-permute-start(bf16[4,64,1152]{2,1,0:T(8,128)(2,1)S(1)} %pad_maximum_fusion.3), channel_id=1, source_target_pairs={{0,2},{2,0},{4,6},{6,4},{8,10},{10,8},{12,14},{14,12},{1,3},{3,1},... | collective-permute-start | bytes 1769480 | tf_op jit(solution)/shard_map/ppermute | solution.py:438
  135.9 27.2 %copy-start.1 = (f32[16,128,128]{2,1,0:T(8,128)S(1)}, f32[16,128,128]{2,1,0:T(8,128)}, u32[]{:S(2)}) copy-start(f32[16,128,128]{2,1,0:T(8,128)} %get-tuple-element.60.probs_ref) | copy-start | bytes 3145732
  136.0 27.2 %copy-start.2 = (bf16[6,128,640]{2,1,0:T(8,128)(2,1)S(1)}, bf16[6,128,640]{2,1,0:T(8,128)(2,1)}, u32[]{:S(2)}) copy-start(bf16[6,128,640]{2,1,0:T(8,128)(2,1)} %get-tuple-element.59.qkv_ref) | copy-start | bytes 2949124
  136.0 27.2 %copy-start.3 = (f32[2,128,640]{2,1,0:T(8,128)S(1)}, f32[2,128,640]{2,1,0:T(8,128)}, u32[]{:S(2)}) copy-start(f32[2,128,640]{2,1,0:T(8,128)} %get-tuple-element.61.norm_ref) | copy-start | bytes 1966084
  136.0 1.7 collective-permute-start.23
  137.7 11.6 %collective-permute-start.24 = (bf16[8,32,640]{2,1,0:T(8,128)(2,1)S(1)}, bf16[8,32,640]{2,1,0:T(8,128)(2,1)S(1)}, u32[]{:S(2)}, u32[]{:S(2)}) collective-permute-start(bf16[8,32,640]{2,1,0:T(8,128)(2,1)S(1)} %fusion.15.a_ref), channel_id=1, source_target_pairs={{16,0},{17,1},{18,2},{19,3},{20,4},{21,5},{22,6},{23,7},{24,8},{25... | collective-permute-start | bytes 983048 | tf_op jit(solution)/shard_map/ppermute | solution.py:419
  (7 other events, 20.2 us)

commit v6 on v5

--- a/solution.py
+++ b/solution.py
@@ -395,17 +395,17 @@
         out_ref[r] = jnp.where(keep, a_ref[place], b_ref[place])
 
 
-def arrange_out_kernel(order_ref, a_ref, b_ref, out_ref):
-    for r in range(out_ref.shape[0]):
-        value = a_ref[r].astype(jnp.float32) + b_ref[r].astype(jnp.float32)
-        out_ref[order_ref[r]] = value.astype(out_ref.dtype)
+def arrange_last_kernel(order_ref, near_ref, far_ref, out_ref):
+    for s in range(near_ref.shape[0]):
+        out_ref[order_ref[2 * s]] = near_ref[s]
+        out_ref[order_ref[2 * s + 1]] = far_ref[s]
 
 
 def arrange(kernel, name, scalars, a, b):
     vmem = pl.BlockSpec(memory_space=pltpu.VMEM)
     return pl.pallas_call(
         kernel,
-        out_shape=jax.ShapeDtypeStruct(b.shape, b.dtype),
+        out_shape=jax.ShapeDtypeStruct((scalars[-1].shape[0],) + b.shape[1:], b.dtype),
         in_specs=[pl.BlockSpec(memory_space=pltpu.SMEM)] * len(scalars) + [vmem, vmem],
         out_specs=vmem,
         compiler_params=pltpu.CompilerParams(vmem_limit_bytes=32 << 20),
@@ -545,9 +545,18 @@
     for s in range(1, tp_count):
         total = total + sent_tp(terms[:, s].astype(bf16), s).astype(f32)
     total = total.astype(bf16)
-    returned = passed_along(total, "grp", -1)
-    whole = arrange(arrange_out_kernel, "arrange_out", (order,), total, returned)
-    whole = lax.all_to_all(whole, "dp", 0, 0)
+    total = total.reshape(pair_count, 2, tokens_here, depth)
+    middle = pair_count // 2
+    summed = [None] * pair_count
+    for start, stop in ((middle, pair_count), (0, middle)):
+        part = total[start:stop]
+        part = part.astype(f32) + passed_along(part, "grp", -1).astype(f32)
+        for s in range(start, stop):
+            summed[s] = part[s - start].astype(bf16)
+    blocks = [summed[0]] + [sent_round(summed[s], s) for s in range(1, pair_count)]
+    near = jnp.stack([block[0] for block in blocks])
+    far = sent_across(jnp.stack([block[1] for block in blocks]))
+    whole = arrange(arrange_last_kernel, "arrange_last", (order,), near, far)
     if depth != CHUNK:
         whole = whole.reshape(-1, CHUNK // depth, tokens_here, depth)
         whole = whole.transpose(0, 2, 1, 3).reshape(-1, tokens_here, CHUNK)

time: 173 us -> 172 us (level)
  blocking collectives: 38.8 us -> 25.7 us
  waiting for transfers between devices: 63.3 us -> 71.5 us
  starting transfers between devices: 33.8 us -> 37.6 us
    all_to_all x1 -> x0, blocking collectives: 13.1 us -> none  [per_device(): whole = lax.all_to_all(whole, 'dp', 0, 0)]
    ppermute x12 -> x15, waiting for transfers between devices: 31.9 us -> 37.4 us  [sent_round(): return lax.ppermute(block, 'dp', [(i, i ^ 2 * move) for i in range(count)])]
    ppermute x6 -> x7, waiting for transfers between devices: 13.9 us -> 18.5 us  [sent_across(): lax.ppermute(block, 'dp', [(i, i ^ 1) for i in range(lax.axis_size('dp'))])]
    ppermute x5 -> x6, waiting for transfers between devices: 15.8 us -> 14 us  [passed_along(): return lax.ppermute(block, axis, route)]
    ppermute x12 -> x15, starting transfers between devices: 19.9 us -> 21.6 us  [sent_round(): return lax.ppermute(block, 'dp', [(i, i ^ 2 * move) for i in range(count)])]
    ppermute x5 -> x6, starting transfers between devices: 7.6 us -> 9.03 us  [passed_along(): return lax.ppermute(block, axis, route)]
    ppermute x6 -> x7, starting transfers between devices: 6.11 us -> 6.9 us  [sent_across(): lax.ppermute(block, 'dp', [(i, i ^ 1) for i in range(lax.axis_size('dp'))])]
  transfers between devices with their start and end apart: 25 -> 30, of which waited for: 16 -> 21; matrix products, arithmetic and copies ran while one was open for 5% -> 5% of each run, Pallas kernels for 8% -> 8%
where the time goes in v6:
time: 172 us; the launch traced here: 171 us
  waiting for transfers between devices  71.5 us (42%)
  starting transfers between devices  37.6 us (22%)
  blocking collectives  25.7 us (15%)
  Pallas kernels  22.9 us (13%)
  other arithmetic  8.22 us (5%)
  matrix products  2.62 us (2%)
  local copies, waits for them, and re-layouts  2.07 us (1%)
    ppermute x15, waiting for transfers between devices, sent_round(): return lax.ppermute(block, 'dp', [(i, i ^ 2 * move) for i in range(count)])  37.4 us
    ppermute x15, starting transfers between devices, sent_round(): return lax.ppermute(block, 'dp', [(i, i ^ 2 * move) for i in range(count)])  21.6 us
    ppermute x7, waiting for transfers between devices, sent_across(): lax.ppermute(block, 'dp', [(i, i ^ 1) for i in range(lax.axis_size('dp'))])  18.5 us
    all_to_all x1, blocking collectives, per_device(): swapped = lax.all_to_all(pieces, 'dp', 0, 0)  18 us
    ppermute x6, waiting for transfers between devices, passed_along(): return lax.ppermute(block, axis, route)  14 us
    ppermute x6, starting transfers between devices, passed_along(): return lax.ppermute(block, axis, route)  9.03 us
    pallas_call x1, Pallas kernels, encoder_backward(): pl.pallas_call(encoder_backward_kernel, out_shape=jax.ShapeDtypeStruct((l...  8.73 us
    pallas_call x1, Pallas kernels, encoder_forward(): pl.pallas_call(encoder_forward_kernel, out_shape=(jax.ShapeDtypeStruct((8...  7.78 us
  transfers between devices with their start and end apart: 30, of which 21 were waited for; matrix products, arithmetic and copies ran while one was open for 5% of the time, Pallas kernels for 8%

profile of v6, /device:TPU:0, one launch (start us, length us, event | category | flops | bytes accessed | tf_op | source)
XLA Modules:
  0.0 171.3 jit_solution(5127078207664470102)
XLA Ops:
  1.5 7.8 %encoder_forward.1 = (bf16[8,32,640]{2,1,0:T(8,128)(2,1)S(1)}, bf16[6,128,640]{2,1,0:T(8,128)(2,1)}, f32[16,128,128]{2,1,0:T(8,128)}, f32[2,128,640]{2,1,0:T(8,128)}, f32[128,1]{1,0:T(8,128)S(1)}) custom-call(s32[1]{0:T(128)} %bitcast.flag_ref.refs_0_.refs_1_, bf16[128,1280]{1,0:T(8,128)(2,1)S(1)} %bitcast.128, bf16[1,1280]{1,0:T(2,128)(2,1)S(1)} %copy-done.9, ...), custom_call_target="tpu_custom_call" | custom-call | flops 1000 | bytes 1000 | tf_op jit(solution)/shard_map/encoder_forward/pallas_call | solution.py:151
  9.3 18.0 %all_to_all.5.a_ref = bf16[8,32,640]{2,1,0:T(8,128)(2,1)S(1)} all-to-all(bf16[8,32,640]{2,1,0:T(8,128)(2,1)S(1)} %get-tuple-element.34), channel_id=1, replica_groups=mesh['grp'=2,'dp'=8,'tp'=2] {'dp'}, dimensions={0} | all-to-all | bytes 655360 | tf_op jit(solution)/shard_map/all_to_all | solution.py:475
  27.3 2.1 %collective-permute-start.1 = (bf16[8,32,640]{2,1,0:T(8,128)(2,1)S(1)}, bf16[8,32,640]{2,1,0:T(8,128)(2,1)}, u32[]{:S(2)}, u32[]{:S(2)}) collective-permute-start(bf16[8,32,640]{2,1,0:T(8,128)(2,1)S(1)} %all_to_all.5.a_ref), channel_id=1, source_target_pairs={{0,16},{1,17},{2,18},{3,19},{4,20},{5,21},{6,22},{7,23},{8,24},{9,... | collective-permute-start | bytes 983048 | tf_op jit(solution)/shard_map/ppermute | solution.py:419
  30.2 3.5 %collective-permute-done.1.b_ref = bf16[8,32,640]{2,1,0:T(8,128)(2,1)} collective-permute-done((bf16[8,32,640]{2,1,0:T(8,128)(2,1)S(1)}, bf16[8,32,640]{2,1,0:T(8,128)(2,1)}, u32[]{:S(2)}, u32[]{:S(2)}) %collective-permute-start.1) | collective-permute-done | bytes 327712 | tf_op jit(solution)/shard_map/ppermute | solution.py:419
  38.0 2.5 %partial_products.2 = (bf16[2,64,1152]{2,1,0:T(8,128)(2,1)S(1)}, bf16[2,64,1152]{2,1,0:T(8,128)(2,1)S(1)}, f32[64,1152]{1,0:T(8,128)S(1)}, f32[64,1152]{1,0:T(8,...) custom-call(s32[1]{0:T(128)} %bitcast.flag_ref.refs_0_.refs_1_, ...), custom_call_target="tpu_custom_call" | custom-call | flops 1000 | bytes 1000 | tf_op jit(solution)/shard_map/partial_products/pallas_call | solution.py:371
  40.6 1.6 collective-permute-start.4
  44.1 6.4 %collective-permute-done.4 = bf16[2,64,1152]{2,1,0:T(8,128)(2,1)S(1)} collective-permute-done((bf16[2,64,1152]{2,1,0:T(8,128)(2,1)S(1)}, bf16[2,64,1152]{2,1,0:T(8,128)(2,1)S(1)}, u32[]{:S(2)}, u32[]{:S(2)}) %collective-permute-start.4) | collective-permute-done | bytes 294944 | tf_op jit(solution)/shard_map/ppermute | solution.py:438
  51.3 5.0 %collective-permute-done.5 = bf16[2,64,1152]{2,1,0:T(8,128)(2,1)S(1)} collective-permute-done((bf16[2,64,1152]{2,1,0:T(8,128)(2,1)S(1)}, bf16[2,64,1152]{2,1,0:T(8,128)(2,1)S(1)}, u32[]{:S(2)}, u32[]{:S(2)}) %collective-permute-start.5) | collective-permute-done | bytes 294944 | tf_op jit(solution)/shard_map/ppermute | solution.py:438
  58.0 2.6 %collective-permute-start.7 = (bf16[64,1152]{1,0:T(8,128)(2,1)}, bf16[64,1152]{1,0:T(8,128)(2,1)}, u32[]{:S(2)}, u32[]{:S(2)}) collective-permute-start(bf16[64,1152]{1,0:T(8,128)(2,1)} %get-tuple-element.44), channel_id=1, source_target_pairs={{0,8},{2,10},{4,12},{6,14},{8,0},{10,2},{12,4},{14,6},{1,9},{3,11}... | collective-permute-start | bytes 442376 | tf_op jit(solution)/shard_map/ppermute | solution.py:434
  63.0 1.6 collective-permute-done.9.refs_2_
  64.7 2.2 %partial_products.3 = (bf16[2,64,896]{2,1,0:T(8,128)(2,1)S(1)}, bf16[2,64,896]{2,1,0:T(8,128)(2,1)S(1)}, f32[64,896]{1,0:T(8,128)S(1)}, f32[64,896]{1,0:T(8,128)...) custom-call(s32[1]{0:T(128)} %bitcast.flag_ref.refs_0_.refs_1_, ...), custom_call_target="tpu_custom_call" | custom-call | flops 1000 | bytes 1000 | tf_op jit(solution)/shard_map/partial_products/pallas_call | solution.py:371
  69.0 3.3 %collective-permute-done.7 = bf16[64,1152]{1,0:T(8,128)(2,1)} collective-permute-done((bf16[64,1152]{1,0:T(8,128)(2,1)}, bf16[64,1152]{1,0:T(8,128)(2,1)}, u32[]{:S(2)}, u32[]{:S(2)}) %collective-permute-start.7) | collective-permute-done | bytes 147488 | tf_op jit(solution)/shard_map/ppermute | solution.py:434
  73.7 1.7 %collective-permute-done.10 = bf16[2,64,896]{2,1,0:T(8,128)(2,1)S(1)} collective-permute-done((bf16[2,64,896]{2,1,0:T(8,128)(2,1)S(1)}, bf16[2,64,896]{2,1,0:T(8,128)(2,1)S(1)}, u32[]{:S(2)}, u32[]{:S(2)}) %collective-permute-start.10) | collective-permute-done | bytes 229408 | tf_op jit(solution)/shard_map/ppermute | solution.py:438
  75.5 3.0 %collective-permute-start.14 = (bf16[64,896]{1,0:T(8,128)(2,1)S(1)}, bf16[64,896]{1,0:T(8,128)(2,1)S(1)}, u32[]{:S(2)}, u32[]{:S(2)}) collective-permute-start(bf16[64,896]{1,0:T(8,128)(2,1)S(1)} %fusion.23), channel_id=1, source_target_pairs={{0,12},{2,14},{4,8},{6,10},{8,4},{10,6},{12,0},{14,2},{1,13},{3,15... | collective-permute-start | bytes 344072 | tf_op jit(solution)/shard_map/ppermute | solution.py:434
  80.3 2.6 %collective-permute-start.13 = (bf16[64,896]{1,0:T(8,128)(2,1)S(1)}, bf16[64,896]{1,0:T(8,128)(2,1)S(1)}, u32[]{:S(2)}, u32[]{:S(2)}) collective-permute-start(bf16[64,896]{1,0:T(8,128)(2,1)S(1)} %get-tuple-element.75), channel_id=1, source_target_pairs={{0,8},{2,10},{4,12},{6,14},{8,0},{10,2},{12,4},{14,6},{1,9},{3,11}... | collective-permute-start | bytes 344072 | tf_op jit(solution)/shard_map/ppermute | solution.py:434
  83.1 4.0 %collective-permute-done.12 = bf16[64,896]{1,0:T(8,128)(2,1)S(1)} collective-permute-done((bf16[64,896]{1,0:T(8,128)(2,1)S(1)}, bf16[64,896]{1,0:T(8,128)(2,1)S(1)}, u32[]{:S(2)}, u32[]{:S(2)}) %collective-permute-start.12) | collective-permute-done | bytes 114720 | tf_op jit(solution)/shard_map/ppermute | solution.py:434
  88.2 7.7 %psum.7 = f32[2,32,2]{1,2,0:T(2,128)S(1)} all-reduce(f32[2,32,2]{1,2,0:T(2,128)S(1)} %maximum_select_fusion), channel_id=1, replica_groups=mesh['grp'=2,'dp'=8,'tp'=2] {'grp','tp'}, use_global_device_ids=true, to_apply=%region_4.5 | all-reduce | flops 128 | bytes 1024 | tf_op jit(solution)/shard_map/psum | solution.py:513
  98.0 2.0 %collective-permute-start.17 = (bf16[64,1152]{1,0:T(8,128)(2,1)S(1)}, bf16[64,1152]{1,0:T(8,128)(2,1)S(1)}, u32[]{:S(2)}, u32[]{:S(2)}) collective-permute-start(bf16[64,1152]{1,0:T(8,128)(2,1)S(1)} %subtract_convert_fusion), channel_id=1, source_target_pairs={{0,12},{2,14},{4,8},{6,10},{8,4},{10,6},{12,0},{14,2},{1,13},{3,15... | collective-permute-start | bytes 442376 | tf_op jit(solution)/shard_map/ppermute | solution.py:434
  99.9 2.5 %collective-permute-start.15 = (bf16[64,1152]{1,0:T(8,128)(2,1)S(1)}, bf16[64,1152]{1,0:T(8,128)(2,1)S(1)}, u32[]{:S(2)}, u32[]{:S(2)}) collective-permute-start(bf16[64,1152]{1,0:T(8,128)(2,1)S(1)} %subtract_convert_fusion), channel_id=1, source_target_pairs={{0,4},{2,6},{4,0},{6,2},{8,12},{10,14},{12,8},{14,10},{1,5},{3,7},... | collective-permute-start | bytes 442376 | tf_op jit(solution)/shard_map/ppermute | solution.py:434
  102.5 4.2 %collective-permute-done.17 = bf16[64,1152]{1,0:T(8,128)(2,1)S(1)} collective-permute-done((bf16[64,1152]{1,0:T(8,128)(2,1)S(1)}, bf16[64,1152]{1,0:T(8,128)(2,1)S(1)}, u32[]{:S(2)}, u32[]{:S(2)}) %collective-permute-start.17) | collective-permute-done | bytes 147488 | tf_op jit(solution)/shard_map/ppermute | solution.py:434
  106.6 5.0 %collective-permute-done.16 = bf16[64,1152]{1,0:T(8,128)(2,1)S(1)} collective-permute-done((bf16[64,1152]{1,0:T(8,128)(2,1)S(1)}, bf16[64,1152]{1,0:T(8,128)(2,1)S(1)}, u32[]{:S(2)}, u32[]{:S(2)}) %collective-permute-start.16) | collective-permute-done | bytes 147488 | tf_op jit(solution)/shard_map/ppermute | solution.py:434
  111.8 2.4 %collective-permute-start.21 = (bf16[2,64,896]{2,1,0:T(8,128)(2,1)S(1)}, bf16[2,64,896]{2,1,0:T(8,128)(2,1)S(1)}, u32[]{:S(2)}, u32[]{:S(2)}) collective-permute-start(bf16[2,64,896]{2,1,0:T(8,128)(2,1)S(1)} %pad_maximum_fusion.5), channel_id=1, source_target_pairs={{0,12},{2,14},{4,8},{6,10},{8,4},{10,6},{12,0},{14,2},{1,13},{3,15... | collective-permute-start | bytes 688136 | tf_op jit(solution)/shard_map/ppermute | solution.py:434
  114.1 2.1 %collective-permute-start.19 = (bf16[2,64,896]{2,1,0:T(8,128)(2,1)S(1)}, bf16[2,64,896]{2,1,0:T(8,128)(2,1)S(1)}, u32[]{:S(2)}, u32[]{:S(2)}) collective-permute-start(bf16[2,64,896]{2,1,0:T(8,128)(2,1)S(1)} %pad_maximum_fusion.5), channel_id=1, source_target_pairs={{0,4},{2,6},{4,0},{6,2},{8,12},{10,14},{12,8},{14,10},{1,5},{3,7},... | collective-permute-start | bytes 688136 | tf_op jit(solution)/shard_map/ppermute | solution.py:434
  117.3 4.9 %collective-permute-done.21 = bf16[2,64,896]{2,1,0:T(8,128)(2,1)S(1)} collective-permute-done((bf16[2,64,896]{2,1,0:T(8,128)(2,1)S(1)}, bf16[2,64,896]{2,1,0:T(8,128)(2,1)S(1)}, u32[]{:S(2)}, u32[]{:S(2)}) %collective-permute-start.21) | collective-permute-done | bytes 229408 | tf_op jit(solution)/shard_map/ppermute | solution.py:434
  122.2 10.7 %collective-permute-done.20 = bf16[2,64,896]{2,1,0:T(8,128)(2,1)S(1)} collective-permute-done((bf16[2,64,896]{2,1,0:T(8,128)(2,1)S(1)}, bf16[2,64,896]{2,1,0:T(8,128)(2,1)S(1)}, u32[]{:S(2)}, u32[]{:S(2)}) %collective-permute-start.20) | collective-permute-done | bytes 229408 | tf_op jit(solution)/shard_map/ppermute | solution.py:434
  136.0 1.6 collective-permute-done.23
  140.5 6.2 %collective-permute-done.26 = bf16[2,2,32,640]{3,2,1,0:T(8,128)(2,1)S(1)} collective-permute-done((bf16[2,2,32,640]{3,2,1,0:T(8,128)(2,1)S(1)}, bf16[2,2,32,640]{3,2,1,0:T(8,128)(2,1)S(1)}, u32[]{:S(2)}, u32[]{:S(2)}) %collective-permute-start.26) | collective-permute-done | bytes 163872 | tf_op jit(solution)/shard_map/ppermute | solution.py:419
  146.8 2.5 %collective-permute-done.24 = bf16[2,2,32,640]{3,2,1,0:T(8,128)(2,1)S(1)} collective-permute-done((bf16[2,2,32,640]{3,2,1,0:T(8,128)(2,1)S(1)}, bf16[2,2,32,640]{3,2,1,0:T(8,128)(2,1)S(1)}, u32[]{:S(2)}, u32[]{:S(2)}) %collective-permute-start.24) | collective-permute-done | bytes 163872 | tf_op jit(solution)/shard_map/ppermute | solution.py:419
  149.5 1.6 collective-permute-start.28
  152.4 3.6 %collective-permute-done.28 = bf16[2,32,640]{2,1,0:T(8,128)(2,1)S(1)} collective-permute-done((bf16[2,32,640]{2,1,0:T(8,128)(2,1)S(1)}, bf16[2,32,640]{2,1,0:T(8,128)(2,1)S(1)}, u32[]{:S(2)}, u32[]{:S(2)}) %collective-permute-start.28) | collective-permute-done | bytes 81952 | tf_op jit(solution)/shard_map/ppermute | solution.py:434
  157.2 4.6 %collective-permute-done.29.far_ref = bf16[4,32,640]{2,1,0:T(8,128)(2,1)S(1)} collective-permute-done((bf16[4,32,640]{2,1,0:T(8,128)(2,1)S(1)}, bf16[4,32,640]{2,1,0:T(8,128)(2,1)S(1)}, u32[]{:S(2)}, u32[]{:S(2)}) %collective-permute-start.29) | collective-permute-done | bytes 163872 | tf_op jit(solution)/shard_map/ppermute | solution.py:438
  162.4 8.7 %encoder_backward.1 = bf16[128,1280]{1,0:T(8,128)(2,1)} custom-call(s32[1]{0:T(128)} %bitcast.flag_ref.refs_0_.refs_1_, bf16[8,32,640]{2,1,0:T(8,128)(2,1)S(1)} %arrange_last.1.grad_ref, bf16[1,1280]{1,0:T(2,128)(2,1)S(1)} %copy-done.9, bf16[6,128,640]{2,1,0:T(8,128)(2,1)S(1)} %copy-done.2, f32[16,128,128]{2,1,0:T(8,128)S(1)} %copy-done.1, ...), custom_call_target="tpu_custom_call" | custom-call | flops 1000 | bytes 1000 | tf_op jit(solution)/shard_map/encoder_backward/pallas_call | solution.py:251
  (122 shorter events, 32.5 us)
Async XLA Ops:
  0.0 38.0 %collective-permute-start.3 = (bf16[640,1152]{1,0:T(8,128)(2,1)S(1)}, bf16[640,1152]{1,0:T(8,128)(2,1)}, u32[]{:S(2)}, u32[]{:S(2)}) collective-permute-start(bf16[640,1152]{1,0:T(8,128)(2,1)S(1)} %give_columns.2.refs_1_), channel_id=1, source_target_pairs={{16,0},{17,1},{18,2},{19,3},{20,4},{21,5},{22,6},{23,7},{24,8},{25... | collective-permute-start | bytes 4423688 | tf_op jit(solution)/shard_map/ppermute | solution.py:419
  27.3 6.4 %collective-permute-start.1 = (bf16[8,32,640]{2,1,0:T(8,128)(2,1)S(1)}, bf16[8,32,640]{2,1,0:T(8,128)(2,1)}, u32[]{:S(2)}, u32[]{:S(2)}) collective-permute-start(bf16[8,32,640]{2,1,0:T(8,128)(2,1)S(1)} %all_to_all.5.a_ref), channel_id=1, source_target_pairs={{0,16},{1,17},{2,18},{3,19},{4,20},{5,21},{6,22},{7,23},{8,24},{9,... | collective-permute-start | bytes 983048 | tf_op jit(solution)/shard_map/ppermute | solution.py:419
  34.7 2.1 %collective-permute-start.2 = (bf16[8,32,640]{2,1,0:T(8,128)(2,1)S(1)}, bf16[8,32,640]{2,1,0:T(8,128)(2,1)}, u32[]{:S(2)}, u32[]{:S(2)}) collective-permute-start(bf16[8,32,640]{2,1,0:T(8,128)(2,1)S(1)} %arrange_in.1), channel_id=1, source_target_pairs={{0,1},{1,0},{2,3},{3,2},{4,5},{5,4},{6,7},{7,6},{8,9},{9,8},{10,11... | collective-permute-start | bytes 983048 | tf_op jit(solution)/shard_map/ppermute | solution.py:443
  34.8 29.9 %collective-permute-start.9 = (bf16[640,896]{1,0:T(8,128)(2,1)S(1)}, bf16[640,896]{1,0:T(8,128)(2,1)}, u32[]{:S(2)}, u32[]{:S(2)}) collective-permute-start(bf16[640,896]{1,0:T(8,128)(2,1)S(1)} %give_columns.3.after_ref), channel_id=1, source_target_pairs={{16,0},{17,1},{18,2},{19,3},{20,4},{21,5},{22,6},{23,7},{24,8},{25... | collective-permute-start | bytes 3440648 | tf_op jit(solution)/shard_map/ppermute | solution.py:419
  40.6 9.9 %collective-permute-start.4 = (bf16[2,64,1152]{2,1,0:T(8,128)(2,1)S(1)}, bf16[2,64,1152]{2,1,0:T(8,128)(2,1)S(1)}, u32[]{:S(2)}, u32[]{:S(2)}) collective-permute-start(bf16[2,64,1152]{2,1,0:T(8,128)(2,1)S(1)} %get-tuple-element.38), channel_id=1, source_target_pairs={{0,2},{2,0},{4,6},{6,4},{8,10},{10,8},{12,14},{14,12},{1,3},{3,1},... | collective-permute-start | bytes 884744 | tf_op jit(solution)/shard_map/ppermute | solution.py:438
  43.6 12.7 %collective-permute-start.5 = (bf16[2,64,1152]{2,1,0:T(8,128)(2,1)S(1)}, bf16[2,64,1152]{2,1,0:T(8,128)(2,1)S(1)}, u32[]{:S(2)}, u32[]{:S(2)}) collective-permute-start(bf16[2,64,1152]{2,1,0:T(8,128)(2,1)S(1)} %get-tuple-element.40), channel_id=1, source_target_pairs={{0,2},{2,0},{4,6},{6,4},{8,10},{10,8},{12,14},{14,12},{1,3},{3,1},... | collective-permute-start | bytes 884744 | tf_op jit(solution)/shard_map/ppermute | solution.py:438
  57.1 10.8 %collective-permute-start.6 = (bf16[64,1152]{1,0:T(8,128)(2,1)}, bf16[64,1152]{1,0:T(8,128)(2,1)S(1)}, u32[]{:S(2)}, u32[]{:S(2)}) collective-permute-start(bf16[64,1152]{1,0:T(8,128)(2,1)} %get-tuple-element.43), channel_id=1, source_target_pairs={{0,4},{2,6},{4,0},{6,2},{8,12},{10,14},{12,8},{14,10},{1,5},{3,7},... | collective-permute-start | bytes 442376 | tf_op jit(solution)/shard_map/ppermute | solution.py:434
  58.0 14.3 %collective-permute-start.7 = (bf16[64,1152]{1,0:T(8,128)(2,1)}, bf16[64,1152]{1,0:T(8,128)(2,1)}, u32[]{:S(2)}, u32[]{:S(2)}) collective-permute-start(bf16[64,1152]{1,0:T(8,128)(2,1)} %get-tuple-element.44), channel_id=1, source_target_pairs={{0,8},{2,10},{4,12},{6,14},{8,0},{10,2},{12,4},{14,6},{1,9},{3,11}... | collective-permute-start | bytes 442376 | tf_op jit(solution)/shard_map/ppermute | solution.py:434
  60.6 11.7 %collective-permute-start.8 = (bf16[64,1152]{1,0:T(8,128)(2,1)}, bf16[64,1152]{1,0:T(8,128)(2,1)}, u32[]{:S(2)}, u32[]{:S(2)}) collective-permute-start(bf16[64,1152]{1,0:T(8,128)(2,1)} %fusion.17), channel_id=1, source_target_pairs={{0,12},{2,14},{4,8},{6,10},{8,4},{10,6},{12,0},{14,2},{1,13},{3,15... | collective-permute-start | bytes 442376 | tf_op jit(solution)/shard_map/ppermute | solution.py:434
  61.6 11.9 %collective-permute-start = (bf16[80,2048]{1,0:T(8,128)(2,1)}, bf16[80,2048]{1,0:T(8,128)(2,1)S(1)}, u32[]{:S(2)}, u32[]{:S(2)}) collective-permute-start(bf16[80,2048]{1,0:T(8,128)(2,1)} %copy-done.5), channel_id=1, source_target_pairs={{16,0},{17,1},{18,2},{19,3},{20,4},{21,5},{22,6},{23,7},{24,8},{25... | collective-permute-start | bytes 983048 | tf_op jit(solution)/shard_map/ppermute | solution.py:419
  66.9 8.6 %collective-permute-start.10 = (bf16[2,64,896]{2,1,0:T(8,128)(2,1)S(1)}, bf16[2,64,896]{2,1,0:T(8,128)(2,1)S(1)}, u32[]{:S(2)}, u32[]{:S(2)}) collective-permute-start(bf16[2,64,896]{2,1,0:T(8,128)(2,1)S(1)} %get-tuple-element.49), channel_id=1, source_target_pairs={{0,2},{2,0},{4,6},{6,4},{8,10},{10,8},{12,14},{14,12},{1,3},{3,1},... | collective-permute-start | bytes 688136 | tf_op jit(solution)/shard_map/ppermute | solution.py:438
  67.9 11.4 %collective-permute-start.11 = (bf16[2,64,896]{2,1,0:T(8,128)(2,1)S(1)}, bf16[2,64,896]{2,1,0:T(8,128)(2,1)S(1)}, u32[]{:S(2)}, u32[]{:S(2)}) collective-permute-start(bf16[2,64,896]{2,1,0:T(8,128)(2,1)S(1)} %get-tuple-element.51), channel_id=1, source_target_pairs={{0,2},{2,0},{4,6},{6,4},{8,10},{10,8},{12,14},{14,12},{1,3},{3,1},... | collective-permute-start | bytes 688136 | tf_op jit(solution)/shard_map/ppermute | solution.py:438
  75.5 7.6 %collective-permute-start.14 = (bf16[64,896]{1,0:T(8,128)(2,1)S(1)}, bf16[64,896]{1,0:T(8,128)(2,1)S(1)}, u32[]{:S(2)}, u32[]{:S(2)}) collective-permute-start(bf16[64,896]{1,0:T(8,128)(2,1)S(1)} %fusion.23), channel_id=1, source_target_pairs={{0,12},{2,14},{4,8},{6,10},{8,4},{10,6},{12,0},{14,2},{1,13},{3,15... | collective-permute-start | bytes 344072 | tf_op jit(solution)/shard_map/ppermute | solution.py:434
  79.3 7.8 %collective-permute-start.12 = (bf16[64,896]{1,0:T(8,128)(2,1)S(1)}, bf16[64,896]{1,0:T(8,128)(2,1)S(1)}, u32[]{:S(2)}, u32[]{:S(2)}) collective-permute-start(bf16[64,896]{1,0:T(8,128)(2,1)S(1)} %get-tuple-element.74), channel_id=1, source_target_pairs={{0,4},{2,6},{4,0},{6,2},{8,12},{10,14},{12,8},{14,10},{1,5},{3,7},... | collective-permute-start | bytes 344072 | tf_op jit(solution)/shard_map/ppermute | solution.py:434
  80.3 6.7 %collective-permute-start.13 = (bf16[64,896]{1,0:T(8,128)(2,1)S(1)}, bf16[64,896]{1,0:T(8,128)(2,1)S(1)}, u32[]{:S(2)}, u32[]{:S(2)}) collective-permute-start(bf16[64,896]{1,0:T(8,128)(2,1)S(1)} %get-tuple-element.75), channel_id=1, source_target_pairs={{0,8},{2,10},{4,12},{6,14},{8,0},{10,2},{12,4},{14,6},{1,9},{3,11}... | collective-permute-start | bytes 344072 | tf_op jit(solution)/shard_map/ppermute | solution.py:434
  97.1 5.4 %collective-permute-start.18 = (bf16[64,896]{1,0:T(8,128)(2,1)S(1)}, bf16[64,896]{1,0:T(8,128)(2,1)S(1)}, u32[]{:S(2)}, u32[]{:S(2)}) collective-permute-start(bf16[64,896]{1,0:T(8,128)(2,1)S(1)} %subtract_convert_fusion.1), channel_id=1, source_target_pairs={{0,2},{2,0},{4,6},{6,4},{8,10},{10,8},{12,14},{14,12},{1,3},{3,1},... | collective-permute-start | bytes 344072 | tf_op jit(solution)/shard_map/ppermute | solution.py:438
  98.0 8.7 %collective-permute-start.17 = (bf16[64,1152]{1,0:T(8,128)(2,1)S(1)}, bf16[64,1152]{1,0:T(8,128)(2,1)S(1)}, u32[]{:S(2)}, u32[]{:S(2)}) collective-permute-start(bf16[64,1152]{1,0:T(8,128)(2,1)S(1)} %subtract_convert_fusion), channel_id=1, source_target_pairs={{0,12},{2,14},{4,8},{6,10},{8,4},{10,6},{12,0},{14,2},{1,13},{3,15... | collective-permute-start | bytes 442376 | tf_op jit(solution)/shard_map/ppermute | solution.py:434
  99.9 11.7 %collective-permute-start.16 = (bf16[64,1152]{1,0:T(8,128)(2,1)S(1)}, bf16[64,1152]{1,0:T(8,128)(2,1)S(1)}, u32[]{:S(2)}, u32[]{:S(2)}) collective-permute-start(bf16[64,1152]{1,0:T(8,128)(2,1)S(1)} %subtract_convert_fusion), channel_id=1, source_target_pairs={{0,8},{2,10},{4,12},{6,14},{8,0},{10,2},{12,4},{14,6},{1,9},{3,11}... | collective-permute-start | bytes 442376 | tf_op jit(solution)/shard_map/ppermute | solution.py:434
  99.9 11.7 %collective-permute-start.15 = (bf16[64,1152]{1,0:T(8,128)(2,1)S(1)}, bf16[64,1152]{1,0:T(8,128)(2,1)S(1)}, u32[]{:S(2)}, u32[]{:S(2)}) collective-permute-start(bf16[64,1152]{1,0:T(8,128)(2,1)S(1)} %subtract_convert_fusion), channel_id=1, source_target_pairs={{0,4},{2,6},{4,0},{6,2},{8,12},{10,14},{12,8},{14,10},{1,5},{3,7},... | collective-permute-start | bytes 442376 | tf_op jit(solution)/shard_map/ppermute | solution.py:434
  111.8 10.4 %collective-permute-start.21 = (bf16[2,64,896]{2,1,0:T(8,128)(2,1)S(1)}, bf16[2,64,896]{2,1,0:T(8,128)(2,1)S(1)}, u32[]{:S(2)}, u32[]{:S(2)}) collective-permute-start(bf16[2,64,896]{2,1,0:T(8,128)(2,1)S(1)} %pad_maximum_fusion.5), channel_id=1, source_target_pairs={{0,12},{2,14},{4,8},{6,10},{8,4},{10,6},{12,0},{14,2},{1,13},{3,15... | collective-permute-start | bytes 688136 | tf_op jit(solution)/shard_map/ppermute | solution.py:434
  114.1 18.8 %collective-permute-start.20 = (bf16[2,64,896]{2,1,0:T(8,128)(2,1)S(1)}, bf16[2,64,896]{2,1,0:T(8,128)(2,1)S(1)}, u32[]{:S(2)}, u32[]{:S(2)}) collective-permute-start(bf16[2,64,896]{2,1,0:T(8,128)(2,1)S(1)} %pad_maximum_fusion.5), channel_id=1, source_target_pairs={{0,8},{2,10},{4,12},{6,14},{8,0},{10,2},{12,4},{14,6},{1,9},{3,11}... | collective-permute-start | bytes 688136 | tf_op jit(solution)/shard_map/ppermute | solution.py:434
  114.1 18.8 %collective-permute-start.19 = (bf16[2,64,896]{2,1,0:T(8,128)(2,1)S(1)}, bf16[2,64,896]{2,1,0:T(8,128)(2,1)S(1)}, u32[]{:S(2)}, u32[]{:S(2)}) collective-permute-start(bf16[2,64,896]{2,1,0:T(8,128)(2,1)S(1)} %pad_maximum_fusion.5), channel_id=1, source_target_pairs={{0,4},{2,6},{4,0},{6,2},{8,12},{10,14},{12,8},{14,10},{1,5},{3,7},... | collective-permute-start | bytes 688136 | tf_op jit(solution)/shard_map/ppermute | solution.py:434
  116.2 18.8 %collective-permute-start.22 = (bf16[4,64,1152]{2,1,0:T(8,128)(2,1)S(1)}, bf16[4,64,1152]{2,1,0:T(8,128)(2,1)S(1)}, u32[]{:S(2)}, u32[]{:S(2)}) collective-permute-start(bf16[4,64,1152]{2,1,0:T(8,128)(2,1)S(1)} %pad_maximum_fusion.3), channel_id=1, source_target_pairs={{0,2},{2,0},{4,6},{6,4},{8,10},{10,8},{12,14},{14,12},{1,3},{3,1},... | collective-permute-start | bytes 1769480 | tf_op jit(solution)/shard_map/ppermute | solution.py:438
  135.9 1.7 collective-permute-start.23
  137.7 8.9 %collective-permute-start.26 = (bf16[2,2,32,640]{3,2,1,0:T(8,128)(2,1)S(1)}, bf16[2,2,32,640]{3,2,1,0:T(8,128)(2,1)S(1)}, u32[]{:S(2)}, u32[]{:S(2)}) collective-permute-start(bf16[2,2,32,640]{3,2,1,0:T(8,128)(2,1)S(1)} %bitcast.144), channel_id=1, source_target_pairs={{16,0},{17,1},{18,2},{19,3},{20,4},{21,5},{22,6},{23,7},{24,8},{25... | collective-permute-start | bytes 491528 | tf_op jit(solution)/shard_map/ppermute | solution.py:419
  139.0 10.3 %collective-permute-start.24 = (bf16[2,2,32,640]{3,2,1,0:T(8,128)(2,1)S(1)}, bf16[2,2,32,640]{3,2,1,0:T(8,128)(2,1)S(1)}, u32[]{:S(2)}, u32[]{:S(2)}) collective-permute-start(bf16[2,2,32,640]{3,2,1,0:T(8,128)(2,1)S(1)} %bitcast.142), channel_id=1, source_target_pairs={{16,0},{17,1},{18,2},{19,3},{20,4},{21,5},{22,6},{23,7},{24,8},{25... | collective-permute-start | bytes 491528 | tf_op jit(solution)/shard_map/ppermute | solution.py:419
  146.7 15.6 %copy-start.3 = (f32[2,128,640]{2,1,0:T(8,128)S(1)}, f32[2,128,640]{2,1,0:T(8,128)}, u32[]{:S(2)}) copy-start(f32[2,128,640]{2,1,0:T(8,128)} %get-tuple-element.61.norm_ref) | copy-start | bytes 1966084
  146.7 15.6 %copy-start.1 = (f32[16,128,128]{2,1,0:T(8,128)S(1)}, f32[16,128,128]{2,1,0:T(8,128)}, u32[]{:S(2)}) copy-start(f32[16,128,128]{2,1,0:T(8,128)} %get-tuple-element.60.probs_ref) | copy-start | bytes 3145732
  146.8 5.6 %collective-permute-start.27 = (bf16[2,32,640]{2,1,0:T(8,128)(2,1)S(1)}, bf16[2,32,640]{2,1,0:T(8,128)(2,1)S(1)}, u32[]{:S(2)}, u32[]{:S(2)}) collective-permute-start(bf16[2,32,640]{2,1,0:T(8,128)(2,1)S(1)} %get-tuple-element.78), channel_id=1, source_target_pairs={{0,8},{2,10},{4,12},{6,14},{8,0},{10,2},{12,4},{14,6},{1,9},{3,11}... | collective-permute-start | bytes 245768 | tf_op jit(solution)/shard_map/ppermute | solution.py:434
  149.5 6.5 %collective-permute-start.28 = (bf16[2,32,640]{2,1,0:T(8,128)(2,1)S(1)}, bf16[2,32,640]{2,1,0:T(8,128)(2,1)S(1)}, u32[]{:S(2)}, u32[]{:S(2)}) collective-permute-start(bf16[2,32,640]{2,1,0:T(8,128)(2,1)S(1)} %get-tuple-element.79), channel_id=1, source_target_pairs={{0,12},{2,14},{4,8},{6,10},{8,4},{10,6},{12,0},{14,2},{1,13},{3,15... | collective-permute-start | bytes 245768 | tf_op jit(solution)/shard_map/ppermute | solution.py:434
  151.0 5.3 %collective-permute-start.25 = (bf16[2,32,640]{2,1,0:T(8,128)(2,1)S(1)}, bf16[2,32,640]{2,1,0:T(8,128)(2,1)S(1)}, u32[]{:S(2)}, u32[]{:S(2)}) collective-permute-start(bf16[2,32,640]{2,1,0:T(8,128)(2,1)S(1)} %slice_bitcast_fusion.17), channel_id=1, source_target_pairs={{0,4},{2,6},{4,0},{6,2},{8,12},{10,14},{12,8},{14,10},{1,5},{3,7},... | collective-permute-start | bytes 245768 | tf_op jit(solution)/shard_map/ppermute | solution.py:434
  156.4 5.4 %collective-permute-start.29 = (bf16[4,32,640]{2,1,0:T(8,128)(2,1)S(1)}, bf16[4,32,640]{2,1,0:T(8,128)(2,1)S(1)}, u32[]{:S(2)}, u32[]{:S(2)}) collective-permute-start(bf16[4,32,640]{2,1,0:T(8,128)(2,1)S(1)} %pad_maximum_fusion.7), channel_id=1, source_target_pairs={{0,2},{2,0},{4,6},{6,4},{8,10},{10,8},{12,14},{14,12},{1,3},{3,1},... | collective-permute-start | bytes 491528 | tf_op jit(solution)/shard_map/ppermute | solution.py:438
  (12 other events, 74.6 us)

commit v7 on v6

--- a/solution.py
+++ b/solution.py
@@ -168,7 +168,7 @@
             pltpu.SemaphoreType.DMA((6,)),
             pltpu.SemaphoreType.DMA((5,)),
         ],
-        compiler_params=pltpu.CompilerParams(vmem_limit_bytes=40 << 20),
+        compiler_params=pltpu.CompilerParams(vmem_limit_bytes=24 << 20),
         cost_estimate=pl.CostEstimate(flops=1000, transcendentals=0, bytes_accessed=1000),
         name="encoder_forward",
     )(flag, frame, ln_gain, in_hbm(w_qkv))
@@ -261,7 +261,7 @@
             pltpu.VMEM((3, length, CHUNK), bf16),
             pltpu.SemaphoreType.DMA((6,)),
         ],
-        compiler_params=pltpu.CompilerParams(vmem_limit_bytes=40 << 20),
+        compiler_params=pltpu.CompilerParams(vmem_limit_bytes=26 << 20),
         cost_estimate=pl.CostEstimate(flops=1000, transcendentals=0, bytes_accessed=1000),
         name="encoder_backward",
     )(flag, grad, ln_gain, qkv, probs, norm, inverse, in_hbm(w_qkv))
@@ -381,7 +381,7 @@
         ],
         out_specs=(vmem,) * (3 + pairs),
         scratch_shapes=[pltpu.SemaphoreType.DMA],
-        compiler_params=pltpu.CompilerParams(vmem_limit_bytes=32 << 20),
+        compiler_params=pltpu.CompilerParams(vmem_limit_bytes=20 << 20),
         cost_estimate=pl.CostEstimate(flops=1000, transcendentals=0, bytes_accessed=1000),
         name="partial_products",
     )(flag, features, in_hbm(got), in_hbm(matrix))

time: 172 us -> 172 us (level)
  no operation moved by 1% of the time
where the time goes in v7:
time: 172 us; the launch traced here: 171 us
  waiting for transfers between devices  71.5 us (42%)
  starting transfers between devices  37.6 us (22%)
  blocking collectives  25.7 us (15%)
  Pallas kernels  22.9 us (13%)
  other arithmetic  8.22 us (5%)
  matrix products  2.62 us (2%)
  local copies, waits for them, and re-layouts  2.07 us (1%)
    ppermute x15, waiting for transfers between devices, sent_round(): return lax.ppermute(block, 'dp', [(i, i ^ 2 * move) for i in range(count)])  37.4 us
    ppermute x15, starting transfers between devices, sent_round(): return lax.ppermute(block, 'dp', [(i, i ^ 2 * move) for i in range(count)])  21.6 us
    ppermute x7, waiting for transfers between devices, sent_across(): lax.ppermute(block, 'dp', [(i, i ^ 1) for i in range(lax.axis_size('dp'))])  18.5 us
    all_to_all x1, blocking collectives, per_device(): swapped = lax.all_to_all(pieces, 'dp', 0, 0)  18 us
    ppermute x6, waiting for transfers between devices, passed_along(): return lax.ppermute(block, axis, route)  14 us
    ppermute x6, starting transfers between devices, passed_along(): return lax.ppermute(block, axis, route)  9.03 us
    pallas_call x1, Pallas kernels, encoder_backward(): pl.pallas_call(encoder_backward_kernel, out_shape=jax.ShapeDtypeStruct((l...  8.73 us
    pallas_call x1, Pallas kernels, encoder_forward(): pl.pallas_call(encoder_forward_kernel, out_shape=(jax.ShapeDtypeStruct((8...  7.78 us
  transfers between devices with their start and end apart: 30, of which 21 were waited for; matrix products, arithmetic and copies ran while one was open for 5% of the time, Pallas kernels for 8%

profile of v7, /device:TPU:0, one launch (start us, length us, event | category | flops | bytes accessed | tf_op | source)
XLA Modules:
  0.0 171.3 jit_solution(67628784641182844)
XLA Ops:
  1.5 7.8 %encoder_forward.1 = (bf16[8,32,640]{2,1,0:T(8,128)(2,1)S(1)}, bf16[6,128,640]{2,1,0:T(8,128)(2,1)}, f32[16,128,128]{2,1,0:T(8,128)}, f32[2,128,640]{2,1,0:T(8,128)}, f32[128,1]{1,0:T(8,128)S(1)}) custom-call(s32[1]{0:T(128)} %bitcast.flag_ref.refs_0_.refs_1_, bf16[128,1280]{1,0:T(8,128)(2,1)S(1)} %bitcast.128, bf16[1,1280]{1,0:T(2,128)(2,1)S(1)} %copy-done.9, ...), custom_call_target="tpu_custom_call" | custom-call | flops 1000 | bytes 1000 | tf_op jit(solution)/shard_map/encoder_forward/pallas_call | solution.py:151
  9.3 18.0 %all_to_all.5.a_ref = bf16[8,32,640]{2,1,0:T(8,128)(2,1)S(1)} all-to-all(bf16[8,32,640]{2,1,0:T(8,128)(2,1)S(1)} %get-tuple-element.34), channel_id=1, replica_groups=mesh['grp'=2,'dp'=8,'tp'=2] {'dp'}, dimensions={0} | all-to-all | bytes 655360 | tf_op jit(solution)/shard_map/all_to_all | solution.py:475
  27.3 2.1 %collective-permute-start.1 = (bf16[8,32,640]{2,1,0:T(8,128)(2,1)S(1)}, bf16[8,32,640]{2,1,0:T(8,128)(2,1)}, u32[]{:S(2)}, u32[]{:S(2)}) collective-permute-start(bf16[8,32,640]{2,1,0:T(8,128)(2,1)S(1)} %all_to_all.5.a_ref), channel_id=1, source_target_pairs={{0,16},{1,17},{2,18},{3,19},{4,20},{5,21},{6,22},{7,23},{8,24},{9,... | collective-permute-start | bytes 983048 | tf_op jit(solution)/shard_map/ppermute | solution.py:419
  30.2 3.5 %collective-permute-done.1.b_ref = bf16[8,32,640]{2,1,0:T(8,128)(2,1)} collective-permute-done((bf16[8,32,640]{2,1,0:T(8,128)(2,1)S(1)}, bf16[8,32,640]{2,1,0:T(8,128)(2,1)}, u32[]{:S(2)}, u32[]{:S(2)}) %collective-permute-start.1) | collective-permute-done | bytes 327712 | tf_op jit(solution)/shard_map/ppermute | solution.py:419
  38.0 2.5 %partial_products.2 = (bf16[2,64,1152]{2,1,0:T(8,128)(2,1)S(1)}, bf16[2,64,1152]{2,1,0:T(8,128)(2,1)S(1)}, f32[64,1152]{1,0:T(8,128)S(1)}, f32[64,1152]{1,0:T(8,...) custom-call(s32[1]{0:T(128)} %bitcast.flag_ref.refs_0_.refs_1_, ...), custom_call_target="tpu_custom_call" | custom-call | flops 1000 | bytes 1000 | tf_op jit(solution)/shard_map/partial_products/pallas_call | solution.py:371
  40.6 1.6 collective-permute-start.4
  44.1 6.4 %collective-permute-done.4 = bf16[2,64,1152]{2,1,0:T(8,128)(2,1)S(1)} collective-permute-done((bf16[2,64,1152]{2,1,0:T(8,128)(2,1)S(1)}, bf16[2,64,1152]{2,1,0:T(8,128)(2,1)S(1)}, u32[]{:S(2)}, u32[]{:S(2)}) %collective-permute-start.4) | collective-permute-done | bytes 294944 | tf_op jit(solution)/shard_map/ppermute | solution.py:438
  51.3 5.0 %collective-permute-done.5 = bf16[2,64,1152]{2,1,0:T(8,128)(2,1)S(1)} collective-permute-done((bf16[2,64,1152]{2,1,0:T(8,128)(2,1)S(1)}, bf16[2,64,1152]{2,1,0:T(8,128)(2,1)S(1)}, u32[]{:S(2)}, u32[]{:S(2)}) %collective-permute-start.5) | collective-permute-done | bytes 294944 | tf_op jit(solution)/shard_map/ppermute | solution.py:438
  58.0 2.6 %collective-permute-start.7 = (bf16[64,1152]{1,0:T(8,128)(2,1)}, bf16[64,1152]{1,0:T(8,128)(2,1)}, u32[]{:S(2)}, u32[]{:S(2)}) collective-permute-start(bf16[64,1152]{1,0:T(8,128)(2,1)} %get-tuple-element.44), channel_id=1, source_target_pairs={{0,8},{2,10},{4,12},{6,14},{8,0},{10,2},{12,4},{14,6},{1,9},{3,11}... | collective-permute-start | bytes 442376 | tf_op jit(solution)/shard_map/ppermute | solution.py:434
  63.0 1.6 collective-permute-done.9.refs_2_
  64.7 2.2 %partial_products.3 = (bf16[2,64,896]{2,1,0:T(8,128)(2,1)S(1)}, bf16[2,64,896]{2,1,0:T(8,128)(2,1)S(1)}, f32[64,896]{1,0:T(8,128)S(1)}, f32[64,896]{1,0:T(8,128)...) custom-call(s32[1]{0:T(128)} %bitcast.flag_ref.refs_0_.refs_1_, ...), custom_call_target="tpu_custom_call" | custom-call | flops 1000 | bytes 1000 | tf_op jit(solution)/shard_map/partial_products/pallas_call | solution.py:371
  69.0 3.3 %collective-permute-done.7 = bf16[64,1152]{1,0:T(8,128)(2,1)} collective-permute-done((bf16[64,1152]{1,0:T(8,128)(2,1)}, bf16[64,1152]{1,0:T(8,128)(2,1)}, u32[]{:S(2)}, u32[]{:S(2)}) %collective-permute-start.7) | collective-permute-done | bytes 147488 | tf_op jit(solution)/shard_map/ppermute | solution.py:434
  73.7 1.7 %collective-permute-done.10 = bf16[2,64,896]{2,1,0:T(8,128)(2,1)S(1)} collective-permute-done((bf16[2,64,896]{2,1,0:T(8,128)(2,1)S(1)}, bf16[2,64,896]{2,1,0:T(8,128)(2,1)S(1)}, u32[]{:S(2)}, u32[]{:S(2)}) %collective-permute-start.10) | collective-permute-done | bytes 229408 | tf_op jit(solution)/shard_map/ppermute | solution.py:438
  75.5 3.0 %collective-permute-start.14 = (bf16[64,896]{1,0:T(8,128)(2,1)S(1)}, bf16[64,896]{1,0:T(8,128)(2,1)S(1)}, u32[]{:S(2)}, u32[]{:S(2)}) collective-permute-start(bf16[64,896]{1,0:T(8,128)(2,1)S(1)} %fusion.23), channel_id=1, source_target_pairs={{0,12},{2,14},{4,8},{6,10},{8,4},{10,6},{12,0},{14,2},{1,13},{3,15... | collective-permute-start | bytes 344072 | tf_op jit(solution)/shard_map/ppermute | solution.py:434
  80.3 2.6 %collective-permute-start.13 = (bf16[64,896]{1,0:T(8,128)(2,1)S(1)}, bf16[64,896]{1,0:T(8,128)(2,1)S(1)}, u32[]{:S(2)}, u32[]{:S(2)}) collective-permute-start(bf16[64,896]{1,0:T(8,128)(2,1)S(1)} %get-tuple-element.75), channel_id=1, source_target_pairs={{0,8},{2,10},{4,12},{6,14},{8,0},{10,2},{12,4},{14,6},{1,9},{3,11}... | collective-permute-start | bytes 344072 | tf_op jit(solution)/shard_map/ppermute | solution.py:434
  83.1 4.0 %collective-permute-done.12 = bf16[64,896]{1,0:T(8,128)(2,1)S(1)} collective-permute-done((bf16[64,896]{1,0:T(8,128)(2,1)S(1)}, bf16[64,896]{1,0:T(8,128)(2,1)S(1)}, u32[]{:S(2)}, u32[]{:S(2)}) %collective-permute-start.12) | collective-permute-done | bytes 114720 | tf_op jit(solution)/shard_map/ppermute | solution.py:434
  88.2 7.7 %psum.7 = f32[2,32,2]{1,2,0:T(2,128)S(1)} all-reduce(f32[2,32,2]{1,2,0:T(2,128)S(1)} %maximum_select_fusion), channel_id=1, replica_groups=mesh['grp'=2,'dp'=8,'tp'=2] {'grp','tp'}, use_global_device_ids=true, to_apply=%region_4.5 | all-reduce | flops 128 | bytes 1024 | tf_op jit(solution)/shard_map/psum | solution.py:513
  98.0 2.0 %collective-permute-start.17 = (bf16[64,1152]{1,0:T(8,128)(2,1)S(1)}, bf16[64,1152]{1,0:T(8,128)(2,1)S(1)}, u32[]{:S(2)}, u32[]{:S(2)}) collective-permute-start(bf16[64,1152]{1,0:T(8,128)(2,1)S(1)} %subtract_convert_fusion), channel_id=1, source_target_pairs={{0,12},{2,14},{4,8},{6,10},{8,4},{10,6},{12,0},{14,2},{1,13},{3,15... | collective-permute-start | bytes 442376 | tf_op jit(solution)/shard_map/ppermute | solution.py:434
  99.9 2.5 %collective-permute-start.15 = (bf16[64,1152]{1,0:T(8,128)(2,1)S(1)}, bf16[64,1152]{1,0:T(8,128)(2,1)S(1)}, u32[]{:S(2)}, u32[]{:S(2)}) collective-permute-start(bf16[64,1152]{1,0:T(8,128)(2,1)S(1)} %subtract_convert_fusion), channel_id=1, source_target_pairs={{0,4},{2,6},{4,0},{6,2},{8,12},{10,14},{12,8},{14,10},{1,5},{3,7},... | collective-permute-start | bytes 442376 | tf_op jit(solution)/shard_map/ppermute | solution.py:434
  102.5 4.2 %collective-permute-done.17 = bf16[64,1152]{1,0:T(8,128)(2,1)S(1)} collective-permute-done((bf16[64,1152]{1,0:T(8,128)(2,1)S(1)}, bf16[64,1152]{1,0:T(8,128)(2,1)S(1)}, u32[]{:S(2)}, u32[]{:S(2)}) %collective-permute-start.17) | collective-permute-done | bytes 147488 | tf_op jit(solution)/shard_map/ppermute | solution.py:434
  106.6 5.0 %collective-permute-done.16 = bf16[64,1152]{1,0:T(8,128)(2,1)S(1)} collective-permute-done((bf16[64,1152]{1,0:T(8,128)(2,1)S(1)}, bf16[64,1152]{1,0:T(8,128)(2,1)S(1)}, u32[]{:S(2)}, u32[]{:S(2)}) %collective-permute-start.16) | collective-permute-done | bytes 147488 | tf_op jit(solution)/shard_map/ppermute | solution.py:434
  111.8 2.4 %collective-permute-start.21 = (bf16[2,64,896]{2,1,0:T(8,128)(2,1)S(1)}, bf16[2,64,896]{2,1,0:T(8,128)(2,1)S(1)}, u32[]{:S(2)}, u32[]{:S(2)}) collective-permute-start(bf16[2,64,896]{2,1,0:T(8,128)(2,1)S(1)} %pad_maximum_fusion.5), channel_id=1, source_target_pairs={{0,12},{2,14},{4,8},{6,10},{8,4},{10,6},{12,0},{14,2},{1,13},{3,15... | collective-permute-start | bytes 688136 | tf_op jit(solution)/shard_map/ppermute | solution.py:434
  114.1 2.1 %collective-permute-start.19 = (bf16[2,64,896]{2,1,0:T(8,128)(2,1)S(1)}, bf16[2,64,896]{2,1,0:T(8,128)(2,1)S(1)}, u32[]{:S(2)}, u32[]{:S(2)}) collective-permute-start(bf16[2,64,896]{2,1,0:T(8,128)(2,1)S(1)} %pad_maximum_fusion.5), channel_id=1, source_target_pairs={{0,4},{2,6},{4,0},{6,2},{8,12},{10,14},{12,8},{14,10},{1,5},{3,7},... | collective-permute-start | bytes 688136 | tf_op jit(solution)/shard_map/ppermute | solution.py:434
  117.3 4.9 %collective-permute-done.21 = bf16[2,64,896]{2,1,0:T(8,128)(2,1)S(1)} collective-permute-done((bf16[2,64,896]{2,1,0:T(8,128)(2,1)S(1)}, bf16[2,64,896]{2,1,0:T(8,128)(2,1)S(1)}, u32[]{:S(2)}, u32[]{:S(2)}) %collective-permute-start.21) | collective-permute-done | bytes 229408 | tf_op jit(solution)/shard_map/ppermute | solution.py:434
  122.2 10.7 %collective-permute-done.20 = bf16[2,64,896]{2,1,0:T(8,128)(2,1)S(1)} collective-permute-done((bf16[2,64,896]{2,1,0:T(8,128)(2,1)S(1)}, bf16[2,64,896]{2,1,0:T(8,128)(2,1)S(1)}, u32[]{:S(2)}, u32[]{:S(2)}) %collective-permute-start.20) | collective-permute-done | bytes 229408 | tf_op jit(solution)/shard_map/ppermute | solution.py:434
  136.0 1.6 collective-permute-done.23
  140.5 6.2 %collective-permute-done.26 = bf16[2,2,32,640]{3,2,1,0:T(8,128)(2,1)S(1)} collective-permute-done((bf16[2,2,32,640]{3,2,1,0:T(8,128)(2,1)S(1)}, bf16[2,2,32,640]{3,2,1,0:T(8,128)(2,1)S(1)}, u32[]{:S(2)}, u32[]{:S(2)}) %collective-permute-start.26) | collective-permute-done | bytes 163872 | tf_op jit(solution)/shard_map/ppermute | solution.py:419
  146.8 2.5 %collective-permute-done.24 = bf16[2,2,32,640]{3,2,1,0:T(8,128)(2,1)S(1)} collective-permute-done((bf16[2,2,32,640]{3,2,1,0:T(8,128)(2,1)S(1)}, bf16[2,2,32,640]{3,2,1,0:T(8,128)(2,1)S(1)}, u32[]{:S(2)}, u32[]{:S(2)}) %collective-permute-start.24) | collective-permute-done | bytes 163872 | tf_op jit(solution)/shard_map/ppermute | solution.py:419
  149.5 1.6 collective-permute-start.28
  152.4 3.6 %collective-permute-done.28 = bf16[2,32,640]{2,1,0:T(8,128)(2,1)S(1)} collective-permute-done((bf16[2,32,640]{2,1,0:T(8,128)(2,1)S(1)}, bf16[2,32,640]{2,1,0:T(8,128)(2,1)S(1)}, u32[]{:S(2)}, u32[]{:S(2)}) %collective-permute-start.28) | collective-permute-done | bytes 81952 | tf_op jit(solution)/shard_map/ppermute | solution.py:434
  157.2 4.6 %collective-permute-done.29.far_ref = bf16[4,32,640]{2,1,0:T(8,128)(2,1)S(1)} collective-permute-done((bf16[4,32,640]{2,1,0:T(8,128)(2,1)S(1)}, bf16[4,32,640]{2,1,0:T(8,128)(2,1)S(1)}, u32[]{:S(2)}, u32[]{:S(2)}) %collective-permute-start.29) | collective-permute-done | bytes 163872 | tf_op jit(solution)/shard_map/ppermute | solution.py:438
  162.4 8.7 %encoder_backward.1 = bf16[128,1280]{1,0:T(8,128)(2,1)} custom-call(s32[1]{0:T(128)} %bitcast.flag_ref.refs_0_.refs_1_, bf16[8,32,640]{2,1,0:T(8,128)(2,1)S(1)} %arrange_last.1.grad_ref, bf16[1,1280]{1,0:T(2,128)(2,1)S(1)} %copy-done.9, bf16[6,128,640]{2,1,0:T(8,128)(2,1)S(1)} %copy-done.2, f32[16,128,128]{2,1,0:T(8,128)S(1)} %copy-done.1, ...), custom_call_target="tpu_custom_call" | custom-call | flops 1000 | bytes 1000 | tf_op jit(solution)/shard_map/encoder_backward/pallas_call | solution.py:251
  (122 shorter events, 32.5 us)
Async XLA Ops:
  0.0 38.0 %collective-permute-start.3 = (bf16[640,1152]{1,0:T(8,128)(2,1)S(1)}, bf16[640,1152]{1,0:T(8,128)(2,1)}, u32[]{:S(2)}, u32[]{:S(2)}) collective-permute-start(bf16[640,1152]{1,0:T(8,128)(2,1)S(1)} %give_columns.2.refs_1_), channel_id=1, source_target_pairs={{16,0},{17,1},{18,2},{19,3},{20,4},{21,5},{22,6},{23,7},{24,8},{25... | collective-permute-start | bytes 4423688 | tf_op jit(solution)/shard_map/ppermute | solution.py:419
  27.3 6.4 %collective-permute-start.1 = (bf16[8,32,640]{2,1,0:T(8,128)(2,1)S(1)}, bf16[8,32,640]{2,1,0:T(8,128)(2,1)}, u32[]{:S(2)}, u32[]{:S(2)}) collective-permute-start(bf16[8,32,640]{2,1,0:T(8,128)(2,1)S(1)} %all_to_all.5.a_ref), channel_id=1, source_target_pairs={{0,16},{1,17},{2,18},{3,19},{4,20},{5,21},{6,22},{7,23},{8,24},{9,... | collective-permute-start | bytes 983048 | tf_op jit(solution)/shard_map/ppermute | solution.py:419
  34.7 2.1 %collective-permute-start.2 = (bf16[8,32,640]{2,1,0:T(8,128)(2,1)S(1)}, bf16[8,32,640]{2,1,0:T(8,128)(2,1)}, u32[]{:S(2)}, u32[]{:S(2)}) collective-permute-start(bf16[8,32,640]{2,1,0:T(8,128)(2,1)S(1)} %arrange_in.1), channel_id=1, source_target_pairs={{0,1},{1,0},{2,3},{3,2},{4,5},{5,4},{6,7},{7,6},{8,9},{9,8},{10,11... | collective-permute-start | bytes 983048 | tf_op jit(solution)/shard_map/ppermute | solution.py:443
  34.8 29.9 %collective-permute-start.9 = (bf16[640,896]{1,0:T(8,128)(2,1)S(1)}, bf16[640,896]{1,0:T(8,128)(2,1)}, u32[]{:S(2)}, u32[]{:S(2)}) collective-permute-start(bf16[640,896]{1,0:T(8,128)(2,1)S(1)} %give_columns.3.after_ref), channel_id=1, source_target_pairs={{16,0},{17,1},{18,2},{19,3},{20,4},{21,5},{22,6},{23,7},{24,8},{25... | collective-permute-start | bytes 3440648 | tf_op jit(solution)/shard_map/ppermute | solution.py:419
  40.6 9.9 %collective-permute-start.4 = (bf16[2,64,1152]{2,1,0:T(8,128)(2,1)S(1)}, bf16[2,64,1152]{2,1,0:T(8,128)(2,1)S(1)}, u32[]{:S(2)}, u32[]{:S(2)}) collective-permute-start(bf16[2,64,1152]{2,1,0:T(8,128)(2,1)S(1)} %get-tuple-element.38), channel_id=1, source_target_pairs={{0,2},{2,0},{4,6},{6,4},{8,10},{10,8},{12,14},{14,12},{1,3},{3,1},... | collective-permute-start | bytes 884744 | tf_op jit(solution)/shard_map/ppermute | solution.py:438
  43.6 12.7 %collective-permute-start.5 = (bf16[2,64,1152]{2,1,0:T(8,128)(2,1)S(1)}, bf16[2,64,1152]{2,1,0:T(8,128)(2,1)S(1)}, u32[]{:S(2)}, u32[]{:S(2)}) collective-permute-start(bf16[2,64,1152]{2,1,0:T(8,128)(2,1)S(1)} %get-tuple-element.40), channel_id=1, source_target_pairs={{0,2},{2,0},{4,6},{6,4},{8,10},{10,8},{12,14},{14,12},{1,3},{3,1},... | collective-permute-start | bytes 884744 | tf_op jit(solution)/shard_map/ppermute | solution.py:438
  57.1 10.8 %collective-permute-start.6 = (bf16[64,1152]{1,0:T(8,128)(2,1)}, bf16[64,1152]{1,0:T(8,128)(2,1)S(1)}, u32[]{:S(2)}, u32[]{:S(2)}) collective-permute-start(bf16[64,1152]{1,0:T(8,128)(2,1)} %get-tuple-element.43), channel_id=1, source_target_pairs={{0,4},{2,6},{4,0},{6,2},{8,12},{10,14},{12,8},{14,10},{1,5},{3,7},... | collective-permute-start | bytes 442376 | tf_op jit(solution)/shard_map/ppermute | solution.py:434
  58.0 14.3 %collective-permute-start.7 = (bf16[64,1152]{1,0:T(8,128)(2,1)}, bf16[64,1152]{1,0:T(8,128)(2,1)}, u32[]{:S(2)}, u32[]{:S(2)}) collective-permute-start(bf16[64,1152]{1,0:T(8,128)(2,1)} %get-tuple-element.44), channel_id=1, source_target_pairs={{0,8},{2,10},{4,12},{6,14},{8,0},{10,2},{12,4},{14,6},{1,9},{3,11}... | collective-permute-start | bytes 442376 | tf_op jit(solution)/shard_map/ppermute | solution.py:434
  60.6 11.7 %collective-permute-start.8 = (bf16[64,1152]{1,0:T(8,128)(2,1)}, bf16[64,1152]{1,0:T(8,128)(2,1)}, u32[]{:S(2)}, u32[]{:S(2)}) collective-permute-start(bf16[64,1152]{1,0:T(8,128)(2,1)} %fusion.17), channel_id=1, source_target_pairs={{0,12},{2,14},{4,8},{6,10},{8,4},{10,6},{12,0},{14,2},{1,13},{3,15... | collective-permute-start | bytes 442376 | tf_op jit(solution)/shard_map/ppermute | solution.py:434
  61.6 11.9 %collective-permute-start = (bf16[80,2048]{1,0:T(8,128)(2,1)}, bf16[80,2048]{1,0:T(8,128)(2,1)S(1)}, u32[]{:S(2)}, u32[]{:S(2)}) collective-permute-start(bf16[80,2048]{1,0:T(8,128)(2,1)} %copy-done.5), channel_id=1, source_target_pairs={{16,0},{17,1},{18,2},{19,3},{20,4},{21,5},{22,6},{23,7},{24,8},{25... | collective-permute-start | bytes 983048 | tf_op jit(solution)/shard_map/ppermute | solution.py:419
  66.9 8.6 %collective-permute-start.10 = (bf16[2,64,896]{2,1,0:T(8,128)(2,1)S(1)}, bf16[2,64,896]{2,1,0:T(8,128)(2,1)S(1)}, u32[]{:S(2)}, u32[]{:S(2)}) collective-permute-start(bf16[2,64,896]{2,1,0:T(8,128)(2,1)S(1)} %get-tuple-element.49), channel_id=1, source_target_pairs={{0,2},{2,0},{4,6},{6,4},{8,10},{10,8},{12,14},{14,12},{1,3},{3,1},... | collective-permute-start | bytes 688136 | tf_op jit(solution)/shard_map/ppermute | solution.py:438
  67.9 11.4 %collective-permute-start.11 = (bf16[2,64,896]{2,1,0:T(8,128)(2,1)S(1)}, bf16[2,64,896]{2,1,0:T(8,128)(2,1)S(1)}, u32[]{:S(2)}, u32[]{:S(2)}) collective-permute-start(bf16[2,64,896]{2,1,0:T(8,128)(2,1)S(1)} %get-tuple-element.51), channel_id=1, source_target_pairs={{0,2},{2,0},{4,6},{6,4},{8,10},{10,8},{12,14},{14,12},{1,3},{3,1},... | collective-permute-start | bytes 688136 | tf_op jit(solution)/shard_map/ppermute | solution.py:438
  75.5 7.6 %collective-permute-start.14 = (bf16[64,896]{1,0:T(8,128)(2,1)S(1)}, bf16[64,896]{1,0:T(8,128)(2,1)S(1)}, u32[]{:S(2)}, u32[]{:S(2)}) collective-permute-start(bf16[64,896]{1,0:T(8,128)(2,1)S(1)} %fusion.23), channel_id=1, source_target_pairs={{0,12},{2,14},{4,8},{6,10},{8,4},{10,6},{12,0},{14,2},{1,13},{3,15... | collective-permute-start | bytes 344072 | tf_op jit(solution)/shard_map/ppermute | solution.py:434
  79.3 7.8 %collective-permute-start.12 = (bf16[64,896]{1,0:T(8,128)(2,1)S(1)}, bf16[64,896]{1,0:T(8,128)(2,1)S(1)}, u32[]{:S(2)}, u32[]{:S(2)}) collective-permute-start(bf16[64,896]{1,0:T(8,128)(2,1)S(1)} %get-tuple-element.74), channel_id=1, source_target_pairs={{0,4},{2,6},{4,0},{6,2},{8,12},{10,14},{12,8},{14,10},{1,5},{3,7},... | collective-permute-start | bytes 344072 | tf_op jit(solution)/shard_map/ppermute | solution.py:434
  80.3 6.7 %collective-permute-start.13 = (bf16[64,896]{1,0:T(8,128)(2,1)S(1)}, bf16[64,896]{1,0:T(8,128)(2,1)S(1)}, u32[]{:S(2)}, u32[]{:S(2)}) collective-permute-start(bf16[64,896]{1,0:T(8,128)(2,1)S(1)} %get-tuple-element.75), channel_id=1, source_target_pairs={{0,8},{2,10},{4,12},{6,14},{8,0},{10,2},{12,4},{14,6},{1,9},{3,11}... | collective-permute-start | bytes 344072 | tf_op jit(solution)/shard_map/ppermute | solution.py:434
  97.1 5.4 %collective-permute-start.18 = (bf16[64,896]{1,0:T(8,128)(2,1)S(1)}, bf16[64,896]{1,0:T(8,128)(2,1)S(1)}, u32[]{:S(2)}, u32[]{:S(2)}) collective-permute-start(bf16[64,896]{1,0:T(8,128)(2,1)S(1)} %subtract_convert_fusion.1), channel_id=1, source_target_pairs={{0,2},{2,0},{4,6},{6,4},{8,10},{10,8},{12,14},{14,12},{1,3},{3,1},... | collective-permute-start | bytes 344072 | tf_op jit(solution)/shard_map/ppermute | solution.py:438
  98.0 8.7 %collective-permute-start.17 = (bf16[64,1152]{1,0:T(8,128)(2,1)S(1)}, bf16[64,1152]{1,0:T(8,128)(2,1)S(1)}, u32[]{:S(2)}, u32[]{:S(2)}) collective-permute-start(bf16[64,1152]{1,0:T(8,128)(2,1)S(1)} %subtract_convert_fusion), channel_id=1, source_target_pairs={{0,12},{2,14},{4,8},{6,10},{8,4},{10,6},{12,0},{14,2},{1,13},{3,15... | collective-permute-start | bytes 442376 | tf_op jit(solution)/shard_map/ppermute | solution.py:434
  99.9 11.7 %collective-permute-start.16 = (bf16[64,1152]{1,0:T(8,128)(2,1)S(1)}, bf16[64,1152]{1,0:T(8,128)(2,1)S(1)}, u32[]{:S(2)}, u32[]{:S(2)}) collective-permute-start(bf16[64,1152]{1,0:T(8,128)(2,1)S(1)} %subtract_convert_fusion), channel_id=1, source_target_pairs={{0,8},{2,10},{4,12},{6,14},{8,0},{10,2},{12,4},{14,6},{1,9},{3,11}... | collective-permute-start | bytes 442376 | tf_op jit(solution)/shard_map/ppermute | solution.py:434
  99.9 11.7 %collective-permute-start.15 = (bf16[64,1152]{1,0:T(8,128)(2,1)S(1)}, bf16[64,1152]{1,0:T(8,128)(2,1)S(1)}, u32[]{:S(2)}, u32[]{:S(2)}) collective-permute-start(bf16[64,1152]{1,0:T(8,128)(2,1)S(1)} %subtract_convert_fusion), channel_id=1, source_target_pairs={{0,4},{2,6},{4,0},{6,2},{8,12},{10,14},{12,8},{14,10},{1,5},{3,7},... | collective-permute-start | bytes 442376 | tf_op jit(solution)/shard_map/ppermute | solution.py:434
  111.8 10.4 %collective-permute-start.21 = (bf16[2,64,896]{2,1,0:T(8,128)(2,1)S(1)}, bf16[2,64,896]{2,1,0:T(8,128)(2,1)S(1)}, u32[]{:S(2)}, u32[]{:S(2)}) collective-permute-start(bf16[2,64,896]{2,1,0:T(8,128)(2,1)S(1)} %pad_maximum_fusion.5), channel_id=1, source_target_pairs={{0,12},{2,14},{4,8},{6,10},{8,4},{10,6},{12,0},{14,2},{1,13},{3,15... | collective-permute-start | bytes 688136 | tf_op jit(solution)/shard_map/ppermute | solution.py:434
  114.1 18.8 %collective-permute-start.20 = (bf16[2,64,896]{2,1,0:T(8,128)(2,1)S(1)}, bf16[2,64,896]{2,1,0:T(8,128)(2,1)S(1)}, u32[]{:S(2)}, u32[]{:S(2)}) collective-permute-start(bf16[2,64,896]{2,1,0:T(8,128)(2,1)S(1)} %pad_maximum_fusion.5), channel_id=1, source_target_pairs={{0,8},{2,10},{4,12},{6,14},{8,0},{10,2},{12,4},{14,6},{1,9},{3,11}... | collective-permute-start | bytes 688136 | tf_op jit(solution)/shard_map/ppermute | solution.py:434
  114.1 18.8 %collective-permute-start.19 = (bf16[2,64,896]{2,1,0:T(8,128)(2,1)S(1)}, bf16[2,64,896]{2,1,0:T(8,128)(2,1)S(1)}, u32[]{:S(2)}, u32[]{:S(2)}) collective-permute-start(bf16[2,64,896]{2,1,0:T(8,128)(2,1)S(1)} %pad_maximum_fusion.5), channel_id=1, source_target_pairs={{0,4},{2,6},{4,0},{6,2},{8,12},{10,14},{12,8},{14,10},{1,5},{3,7},... | collective-permute-start | bytes 688136 | tf_op jit(solution)/shard_map/ppermute | solution.py:434
  116.2 18.8 %collective-permute-start.22 = (bf16[4,64,1152]{2,1,0:T(8,128)(2,1)S(1)}, bf16[4,64,1152]{2,1,0:T(8,128)(2,1)S(1)}, u32[]{:S(2)}, u32[]{:S(2)}) collective-permute-start(bf16[4,64,1152]{2,1,0:T(8,128)(2,1)S(1)} %pad_maximum_fusion.3), channel_id=1, source_target_pairs={{0,2},{2,0},{4,6},{6,4},{8,10},{10,8},{12,14},{14,12},{1,3},{3,1},... | collective-permute-start | bytes 1769480 | tf_op jit(solution)/shard_map/ppermute | solution.py:438
  135.9 1.7 collective-permute-start.23
  137.7 8.9 %collective-permute-start.26 = (bf16[2,2,32,640]{3,2,1,0:T(8,128)(2,1)S(1)}, bf16[2,2,32,640]{3,2,1,0:T(8,128)(2,1)S(1)}, u32[]{:S(2)}, u32[]{:S(2)}) collective-permute-start(bf16[2,2,32,640]{3,2,1,0:T(8,128)(2,1)S(1)} %bitcast.144), channel_id=1, source_target_pairs={{16,0},{17,1},{18,2},{19,3},{20,4},{21,5},{22,6},{23,7},{24,8},{25... | collective-permute-start | bytes 491528 | tf_op jit(solution)/shard_map/ppermute | solution.py:419
  139.0 10.3 %collective-permute-start.24 = (bf16[2,2,32,640]{3,2,1,0:T(8,128)(2,1)S(1)}, bf16[2,2,32,640]{3,2,1,0:T(8,128)(2,1)S(1)}, u32[]{:S(2)}, u32[]{:S(2)}) collective-permute-start(bf16[2,2,32,640]{3,2,1,0:T(8,128)(2,1)S(1)} %bitcast.142), channel_id=1, source_target_pairs={{16,0},{17,1},{18,2},{19,3},{20,4},{21,5},{22,6},{23,7},{24,8},{25... | collective-permute-start | bytes 491528 | tf_op jit(solution)/shard_map/ppermute | solution.py:419
  146.7 15.6 %copy-start.3 = (f32[2,128,640]{2,1,0:T(8,128)S(1)}, f32[2,128,640]{2,1,0:T(8,128)}, u32[]{:S(2)}) copy-start(f32[2,128,640]{2,1,0:T(8,128)} %get-tuple-element.61.norm_ref) | copy-start | bytes 1966084
  146.7 15.6 %copy-start.1 = (f32[16,128,128]{2,1,0:T(8,128)S(1)}, f32[16,128,128]{2,1,0:T(8,128)}, u32[]{:S(2)}) copy-start(f32[16,128,128]{2,1,0:T(8,128)} %get-tuple-element.60.probs_ref) | copy-start | bytes 3145732
  146.8 5.6 %collective-permute-start.27 = (bf16[2,32,640]{2,1,0:T(8,128)(2,1)S(1)}, bf16[2,32,640]{2,1,0:T(8,128)(2,1)S(1)}, u32[]{:S(2)}, u32[]{:S(2)}) collective-permute-start(bf16[2,32,640]{2,1,0:T(8,128)(2,1)S(1)} %get-tuple-element.78), channel_id=1, source_target_pairs={{0,8},{2,10},{4,12},{6,14},{8,0},{10,2},{12,4},{14,6},{1,9},{3,11}... | collective-permute-start | bytes 245768 | tf_op jit(solution)/shard_map/ppermute | solution.py:434
  149.5 6.5 %collective-permute-start.28 = (bf16[2,32,640]{2,1,0:T(8,128)(2,1)S(1)}, bf16[2,32,640]{2,1,0:T(8,128)(2,1)S(1)}, u32[]{:S(2)}, u32[]{:S(2)}) collective-permute-start(bf16[2,32,640]{2,1,0:T(8,128)(2,1)S(1)} %get-tuple-element.79), channel_id=1, source_target_pairs={{0,12},{2,14},{4,8},{6,10},{8,4},{10,6},{12,0},{14,2},{1,13},{3,15... | collective-permute-start | bytes 245768 | tf_op jit(solution)/shard_map/ppermute | solution.py:434
  151.0 5.3 %collective-permute-start.25 = (bf16[2,32,640]{2,1,0:T(8,128)(2,1)S(1)}, bf16[2,32,640]{2,1,0:T(8,128)(2,1)S(1)}, u32[]{:S(2)}, u32[]{:S(2)}) collective-permute-start(bf16[2,32,640]{2,1,0:T(8,128)(2,1)S(1)} %slice_bitcast_fusion.17), channel_id=1, source_target_pairs={{0,4},{2,6},{4,0},{6,2},{8,12},{10,14},{12,8},{14,10},{1,5},{3,7},... | collective-permute-start | bytes 245768 | tf_op jit(solution)/shard_map/ppermute | solution.py:434
  156.4 5.4 %collective-permute-start.29 = (bf16[4,32,640]{2,1,0:T(8,128)(2,1)S(1)}, bf16[4,32,640]{2,1,0:T(8,128)(2,1)S(1)}, u32[]{:S(2)}, u32[]{:S(2)}) collective-permute-start(bf16[4,32,640]{2,1,0:T(8,128)(2,1)S(1)} %pad_maximum_fusion.7), channel_id=1, source_target_pairs={{0,2},{2,0},{4,6},{6,4},{8,10},{10,8},{12,14},{14,12},{1,3},{3,1},... | collective-permute-start | bytes 491528 | tf_op jit(solution)/shard_map/ppermute | solution.py:438
  (12 other events, 74.6 us)

commit v8 on v7

--- a/solution.py
+++ b/solution.py
@@ -548,7 +548,7 @@
     total = total.reshape(pair_count, 2, tokens_here, depth)
     middle = pair_count // 2
     summed = [None] * pair_count
-    for start, stop in ((middle, pair_count), (0, middle)):
+    for start, stop in ((0, middle), (middle, pair_count)):
         part = total[start:stop]
         part = part.astype(f32) + passed_along(part, "grp", -1).astype(f32)
         for s in range(start, stop):

time: 172 us -> 172 us (level)
  no operation moved by 1% of the time
where the time goes in v8:
time: 172 us; the launch traced here: 171 us
  waiting for transfers between devices  71.5 us (42%)
  starting transfers between devices  37.6 us (22%)
  blocking collectives  25.7 us (15%)
  Pallas kernels  22.9 us (13%)
  other arithmetic  8.22 us (5%)
  matrix products  2.62 us (2%)
  local copies, waits for them, and re-layouts  2.07 us (1%)
    ppermute x15, waiting for transfers between devices, sent_round(): return lax.ppermute(block, 'dp', [(i, i ^ 2 * move) for i in range(count)])  37.4 us
    ppermute x15, starting transfers between devices, sent_round(): return lax.ppermute(block, 'dp', [(i, i ^ 2 * move) for i in range(count)])  21.6 us
    ppermute x7, waiting for transfers between devices, sent_across(): lax.ppermute(block, 'dp', [(i, i ^ 1) for i in range(lax.axis_size('dp'))])  18.5 us
    all_to_all x1, blocking collectives, per_device(): swapped = lax.all_to_all(pieces, 'dp', 0, 0)  18 us
    ppermute x6, waiting for transfers between devices, passed_along(): return lax.ppermute(block, axis, route)  14 us
    ppermute x6, starting transfers between devices, passed_along(): return lax.ppermute(block, axis, route)  9.03 us
    pallas_call x1, Pallas kernels, encoder_backward(): pl.pallas_call(encoder_backward_kernel, out_shape=jax.ShapeDtypeStruct((l...  8.73 us
    pallas_call x1, Pallas kernels, encoder_forward(): pl.pallas_call(encoder_forward_kernel, out_shape=(jax.ShapeDtypeStruct((8...  7.78 us
  transfers between devices with their start and end apart: 30, of which 21 were waited for; matrix products, arithmetic and copies ran while one was open for 5% of the time, Pallas kernels for 8%

profile of v8, /device:TPU:0, one launch (start us, length us, event | category | flops | bytes accessed | tf_op | source)
XLA Modules:
  0.0 171.3 jit_solution(67628784641182844)
XLA Ops:
  1.5 7.8 %encoder_forward.1 = (bf16[8,32,640]{2,1,0:T(8,128)(2,1)S(1)}, bf16[6,128,640]{2,1,0:T(8,128)(2,1)}, f32[16,128,128]{2,1,0:T(8,128)}, f32[2,128,640]{2,1,0:T(8,128)}, f32[128,1]{1,0:T(8,128)S(1)}) custom-call(s32[1]{0:T(128)} %bitcast.flag_ref.refs_0_.refs_1_, bf16[128,1280]{1,0:T(8,128)(2,1)S(1)} %bitcast.128, bf16[1,1280]{1,0:T(2,128)(2,1)S(1)} %copy-done.9, ...), custom_call_target="tpu_custom_call" | custom-call | flops 1000 | bytes 1000 | tf_op jit(solution)/shard_map/encoder_forward/pallas_call | solution.py:151
  9.3 18.0 %all_to_all.5.a_ref = bf16[8,32,640]{2,1,0:T(8,128)(2,1)S(1)} all-to-all(bf16[8,32,640]{2,1,0:T(8,128)(2,1)S(1)} %get-tuple-element.34), channel_id=1, replica_groups=mesh['grp'=2,'dp'=8,'tp'=2] {'dp'}, dimensions={0} | all-to-all | bytes 655360 | tf_op jit(solution)/shard_map/all_to_all | solution.py:475
  27.3 2.1 %collective-permute-start.1 = (bf16[8,32,640]{2,1,0:T(8,128)(2,1)S(1)}, bf16[8,32,640]{2,1,0:T(8,128)(2,1)}, u32[]{:S(2)}, u32[]{:S(2)}) collective-permute-start(bf16[8,32,640]{2,1,0:T(8,128)(2,1)S(1)} %all_to_all.5.a_ref), channel_id=1, source_target_pairs={{0,16},{1,17},{2,18},{3,19},{4,20},{5,21},{6,22},{7,23},{8,24},{9,... | collective-permute-start | bytes 983048 | tf_op jit(solution)/shard_map/ppermute | solution.py:419
  30.2 3.5 %collective-permute-done.1.b_ref = bf16[8,32,640]{2,1,0:T(8,128)(2,1)} collective-permute-done((bf16[8,32,640]{2,1,0:T(8,128)(2,1)S(1)}, bf16[8,32,640]{2,1,0:T(8,128)(2,1)}, u32[]{:S(2)}, u32[]{:S(2)}) %collective-permute-start.1) | collective-permute-done | bytes 327712 | tf_op jit(solution)/shard_map/ppermute | solution.py:419
  38.0 2.5 %partial_products.2 = (bf16[2,64,1152]{2,1,0:T(8,128)(2,1)S(1)}, bf16[2,64,1152]{2,1,0:T(8,128)(2,1)S(1)}, f32[64,1152]{1,0:T(8,128)S(1)}, f32[64,1152]{1,0:T(8,...) custom-call(s32[1]{0:T(128)} %bitcast.flag_ref.refs_0_.refs_1_, ...), custom_call_target="tpu_custom_call" | custom-call | flops 1000 | bytes 1000 | tf_op jit(solution)/shard_map/partial_products/pallas_call | solution.py:371
  40.6 1.6 collective-permute-start.4
  44.1 6.4 %collective-permute-done.4 = bf16[2,64,1152]{2,1,0:T(8,128)(2,1)S(1)} collective-permute-done((bf16[2,64,1152]{2,1,0:T(8,128)(2,1)S(1)}, bf16[2,64,1152]{2,1,0:T(8,128)(2,1)S(1)}, u32[]{:S(2)}, u32[]{:S(2)}) %collective-permute-start.4) | collective-permute-done | bytes 294944 | tf_op jit(solution)/shard_map/ppermute | solution.py:438
  51.3 5.0 %collective-permute-done.5 = bf16[2,64,1152]{2,1,0:T(8,128)(2,1)S(1)} collective-permute-done((bf16[2,64,1152]{2,1,0:T(8,128)(2,1)S(1)}, bf16[2,64,1152]{2,1,0:T(8,128)(2,1)S(1)}, u32[]{:S(2)}, u32[]{:S(2)}) %collective-permute-start.5) | collective-permute-done | bytes 294944 | tf_op jit(solution)/shard_map/ppermute | solution.py:438
  58.0 2.6 %collective-permute-start.7 = (bf16[64,1152]{1,0:T(8,128)(2,1)}, bf16[64,1152]{1,0:T(8,128)(2,1)}, u32[]{:S(2)}, u32[]{:S(2)}) collective-permute-start(bf16[64,1152]{1,0:T(8,128)(2,1)} %get-tuple-element.44), channel_id=1, source_target_pairs={{0,8},{2,10},{4,12},{6,14},{8,0},{10,2},{12,4},{14,6},{1,9},{3,11}... | collective-permute-start | bytes 442376 | tf_op jit(solution)/shard_map/ppermute | solution.py:434
  63.0 1.6 collective-permute-done.9.refs_2_
  64.7 2.2 %partial_products.3 = (bf16[2,64,896]{2,1,0:T(8,128)(2,1)S(1)}, bf16[2,64,896]{2,1,0:T(8,128)(2,1)S(1)}, f32[64,896]{1,0:T(8,128)S(1)}, f32[64,896]{1,0:T(8,128)...) custom-call(s32[1]{0:T(128)} %bitcast.flag_ref.refs_0_.refs_1_, ...), custom_call_target="tpu_custom_call" | custom-call | flops 1000 | bytes 1000 | tf_op jit(solution)/shard_map/partial_products/pallas_call | solution.py:371
  69.0 3.3 %collective-permute-done.7 = bf16[64,1152]{1,0:T(8,128)(2,1)} collective-permute-done((bf16[64,1152]{1,0:T(8,128)(2,1)}, bf16[64,1152]{1,0:T(8,128)(2,1)}, u32[]{:S(2)}, u32[]{:S(2)}) %collective-permute-start.7) | collective-permute-done | bytes 147488 | tf_op jit(solution)/shard_map/ppermute | solution.py:434
  73.7 1.7 %collective-permute-done.10 = bf16[2,64,896]{2,1,0:T(8,128)(2,1)S(1)} collective-permute-done((bf16[2,64,896]{2,1,0:T(8,128)(2,1)S(1)}, bf16[2,64,896]{2,1,0:T(8,128)(2,1)S(1)}, u32[]{:S(2)}, u32[]{:S(2)}) %collective-permute-start.10) | collective-permute-done | bytes 229408 | tf_op jit(solution)/shard_map/ppermute | solution.py:438
  75.5 3.0 %collective-permute-start.14 = (bf16[64,896]{1,0:T(8,128)(2,1)S(1)}, bf16[64,896]{1,0:T(8,128)(2,1)S(1)}, u32[]{:S(2)}, u32[]{:S(2)}) collective-permute-start(bf16[64,896]{1,0:T(8,128)(2,1)S(1)} %fusion.23), channel_id=1, source_target_pairs={{0,12},{2,14},{4,8},{6,10},{8,4},{10,6},{12,0},{14,2},{1,13},{3,15... | collective-permute-start | bytes 344072 | tf_op jit(solution)/shard_map/ppermute | solution.py:434
  80.3 2.6 %collective-permute-start.13 = (bf16[64,896]{1,0:T(8,128)(2,1)S(1)}, bf16[64,896]{1,0:T(8,128)(2,1)S(1)}, u32[]{:S(2)}, u32[]{:S(2)}) collective-permute-start(bf16[64,896]{1,0:T(8,128)(2,1)S(1)} %get-tuple-element.75), channel_id=1, source_target_pairs={{0,8},{2,10},{4,12},{6,14},{8,0},{10,2},{12,4},{14,6},{1,9},{3,11}... | collective-permute-start | bytes 344072 | tf_op jit(solution)/shard_map/ppermute | solution.py:434
  83.1 4.0 %collective-permute-done.12 = bf16[64,896]{1,0:T(8,128)(2,1)S(1)} collective-permute-done((bf16[64,896]{1,0:T(8,128)(2,1)S(1)}, bf16[64,896]{1,0:T(8,128)(2,1)S(1)}, u32[]{:S(2)}, u32[]{:S(2)}) %collective-permute-start.12) | collective-permute-done | bytes 114720 | tf_op jit(solution)/shard_map/ppermute | solution.py:434
  88.2 7.7 %psum.7 = f32[2,32,2]{1,2,0:T(2,128)S(1)} all-reduce(f32[2,32,2]{1,2,0:T(2,128)S(1)} %maximum_select_fusion), channel_id=1, replica_groups=mesh['grp'=2,'dp'=8,'tp'=2] {'grp','tp'}, use_global_device_ids=true, to_apply=%region_4.5 | all-reduce | flops 128 | bytes 1024 | tf_op jit(solution)/shard_map/psum | solution.py:513
  98.0 2.0 %collective-permute-start.17 = (bf16[64,1152]{1,0:T(8,128)(2,1)S(1)}, bf16[64,1152]{1,0:T(8,128)(2,1)S(1)}, u32[]{:S(2)}, u32[]{:S(2)}) collective-permute-start(bf16[64,1152]{1,0:T(8,128)(2,1)S(1)} %subtract_convert_fusion), channel_id=1, source_target_pairs={{0,12},{2,14},{4,8},{6,10},{8,4},{10,6},{12,0},{14,2},{1,13},{3,15... | collective-permute-start | bytes 442376 | tf_op jit(solution)/shard_map/ppermute | solution.py:434
  99.9 2.5 %collective-permute-start.15 = (bf16[64,1152]{1,0:T(8,128)(2,1)S(1)}, bf16[64,1152]{1,0:T(8,128)(2,1)S(1)}, u32[]{:S(2)}, u32[]{:S(2)}) collective-permute-start(bf16[64,1152]{1,0:T(8,128)(2,1)S(1)} %subtract_convert_fusion), channel_id=1, source_target_pairs={{0,4},{2,6},{4,0},{6,2},{8,12},{10,14},{12,8},{14,10},{1,5},{3,7},... | collective-permute-start | bytes 442376 | tf_op jit(solution)/shard_map/ppermute | solution.py:434
  102.5 4.2 %collective-permute-done.17 = bf16[64,1152]{1,0:T(8,128)(2,1)S(1)} collective-permute-done((bf16[64,1152]{1,0:T(8,128)(2,1)S(1)}, bf16[64,1152]{1,0:T(8,128)(2,1)S(1)}, u32[]{:S(2)}, u32[]{:S(2)}) %collective-permute-start.17) | collective-permute-done | bytes 147488 | tf_op jit(solution)/shard_map/ppermute | solution.py:434
  106.6 5.0 %collective-permute-done.16 = bf16[64,1152]{1,0:T(8,128)(2,1)S(1)} collective-permute-done((bf16[64,1152]{1,0:T(8,128)(2,1)S(1)}, bf16[64,1152]{1,0:T(8,128)(2,1)S(1)}, u32[]{:S(2)}, u32[]{:S(2)}) %collective-permute-start.16) | collective-permute-done | bytes 147488 | tf_op jit(solution)/shard_map/ppermute | solution.py:434
  111.8 2.4 %collective-permute-start.21 = (bf16[2,64,896]{2,1,0:T(8,128)(2,1)S(1)}, bf16[2,64,896]{2,1,0:T(8,128)(2,1)S(1)}, u32[]{:S(2)}, u32[]{:S(2)}) collective-permute-start(bf16[2,64,896]{2,1,0:T(8,128)(2,1)S(1)} %pad_maximum_fusion.5), channel_id=1, source_target_pairs={{0,12},{2,14},{4,8},{6,10},{8,4},{10,6},{12,0},{14,2},{1,13},{3,15... | collective-permute-start | bytes 688136 | tf_op jit(solution)/shard_map/ppermute | solution.py:434
  114.1 2.1 %collective-permute-start.19 = (bf16[2,64,896]{2,1,0:T(8,128)(2,1)S(1)}, bf16[2,64,896]{2,1,0:T(8,128)(2,1)S(1)}, u32[]{:S(2)}, u32[]{:S(2)}) collective-permute-start(bf16[2,64,896]{2,1,0:T(8,128)(2,1)S(1)} %pad_maximum_fusion.5), channel_id=1, source_target_pairs={{0,4},{2,6},{4,0},{6,2},{8,12},{10,14},{12,8},{14,10},{1,5},{3,7},... | collective-permute-start | bytes 688136 | tf_op jit(solution)/shard_map/ppermute | solution.py:434
  117.3 4.9 %collective-permute-done.21 = bf16[2,64,896]{2,1,0:T(8,128)(2,1)S(1)} collective-permute-done((bf16[2,64,896]{2,1,0:T(8,128)(2,1)S(1)}, bf16[2,64,896]{2,1,0:T(8,128)(2,1)S(1)}, u32[]{:S(2)}, u32[]{:S(2)}) %collective-permute-start.21) | collective-permute-done | bytes 229408 | tf_op jit(solution)/shard_map/ppermute | solution.py:434
  122.2 10.7 %collective-permute-done.20 = bf16[2,64,896]{2,1,0:T(8,128)(2,1)S(1)} collective-permute-done((bf16[2,64,896]{2,1,0:T(8,128)(2,1)S(1)}, bf16[2,64,896]{2,1,0:T(8,128)(2,1)S(1)}, u32[]{:S(2)}, u32[]{:S(2)}) %collective-permute-start.20) | collective-permute-done | bytes 229408 | tf_op jit(solution)/shard_map/ppermute | solution.py:434
  136.0 1.6 collective-permute-done.23
  140.5 6.2 %collective-permute-done.26 = bf16[2,2,32,640]{3,2,1,0:T(8,128)(2,1)S(1)} collective-permute-done((bf16[2,2,32,640]{3,2,1,0:T(8,128)(2,1)S(1)}, bf16[2,2,32,640]{3,2,1,0:T(8,128)(2,1)S(1)}, u32[]{:S(2)}, u32[]{:S(2)}) %collective-permute-start.26) | collective-permute-done | bytes 163872 | tf_op jit(solution)/shard_map/ppermute | solution.py:419
  146.8 2.5 %collective-permute-done.24 = bf16[2,2,32,640]{3,2,1,0:T(8,128)(2,1)S(1)} collective-permute-done((bf16[2,2,32,640]{3,2,1,0:T(8,128)(2,1)S(1)}, bf16[2,2,32,640]{3,2,1,0:T(8,128)(2,1)S(1)}, u32[]{:S(2)}, u32[]{:S(2)}) %collective-permute-start.24) | collective-permute-done | bytes 163872 | tf_op jit(solution)/shard_map/ppermute | solution.py:419
  149.5 1.6 collective-permute-start.28
  152.4 3.6 %collective-permute-done.28 = bf16[2,32,640]{2,1,0:T(8,128)(2,1)S(1)} collective-permute-done((bf16[2,32,640]{2,1,0:T(8,128)(2,1)S(1)}, bf16[2,32,640]{2,1,0:T(8,128)(2,1)S(1)}, u32[]{:S(2)}, u32[]{:S(2)}) %collective-permute-start.28) | collective-permute-done | bytes 81952 | tf_op jit(solution)/shard_map/ppermute | solution.py:434
  157.2 4.6 %collective-permute-done.29.far_ref = bf16[4,32,640]{2,1,0:T(8,128)(2,1)S(1)} collective-permute-done((bf16[4,32,640]{2,1,0:T(8,128)(2,1)S(1)}, bf16[4,32,640]{2,1,0:T(8,128)(2,1)S(1)}, u32[]{:S(2)}, u32[]{:S(2)}) %collective-permute-start.29) | collective-permute-done | bytes 163872 | tf_op jit(solution)/shard_map/ppermute | solution.py:438
  162.4 8.7 %encoder_backward.1 = bf16[128,1280]{1,0:T(8,128)(2,1)} custom-call(s32[1]{0:T(128)} %bitcast.flag_ref.refs_0_.refs_1_, bf16[8,32,640]{2,1,0:T(8,128)(2,1)S(1)} %arrange_last.1.grad_ref, bf16[1,1280]{1,0:T(2,128)(2,1)S(1)} %copy-done.9, bf16[6,128,640]{2,1,0:T(8,128)(2,1)S(1)} %copy-done.2, f32[16,128,128]{2,1,0:T(8,128)S(1)} %copy-done.1, ...), custom_call_target="tpu_custom_call" | custom-call | flops 1000 | bytes 1000 | tf_op jit(solution)/shard_map/encoder_backward/pallas_call | solution.py:251
  (122 shorter events, 32.5 us)
Async XLA Ops:
  0.0 38.0 %collective-permute-start.3 = (bf16[640,1152]{1,0:T(8,128)(2,1)S(1)}, bf16[640,1152]{1,0:T(8,128)(2,1)}, u32[]{:S(2)}, u32[]{:S(2)}) collective-permute-start(bf16[640,1152]{1,0:T(8,128)(2,1)S(1)} %give_columns.2.refs_1_), channel_id=1, source_target_pairs={{16,0},{17,1},{18,2},{19,3},{20,4},{21,5},{22,6},{23,7},{24,8},{25... | collective-permute-start | bytes 4423688 | tf_op jit(solution)/shard_map/ppermute | solution.py:419
  27.3 6.4 %collective-permute-start.1 = (bf16[8,32,640]{2,1,0:T(8,128)(2,1)S(1)}, bf16[8,32,640]{2,1,0:T(8,128)(2,1)}, u32[]{:S(2)}, u32[]{:S(2)}) collective-permute-start(bf16[8,32,640]{2,1,0:T(8,128)(2,1)S(1)} %all_to_all.5.a_ref), channel_id=1, source_target_pairs={{0,16},{1,17},{2,18},{3,19},{4,20},{5,21},{6,22},{7,23},{8,24},{9,... | collective-permute-start | bytes 983048 | tf_op jit(solution)/shard_map/ppermute | solution.py:419
  34.7 2.1 %collective-permute-start.2 = (bf16[8,32,640]{2,1,0:T(8,128)(2,1)S(1)}, bf16[8,32,640]{2,1,0:T(8,128)(2,1)}, u32[]{:S(2)}, u32[]{:S(2)}) collective-permute-start(bf16[8,32,640]{2,1,0:T(8,128)(2,1)S(1)} %arrange_in.1), channel_id=1, source_target_pairs={{0,1},{1,0},{2,3},{3,2},{4,5},{5,4},{6,7},{7,6},{8,9},{9,8},{10,11... | collective-permute-start | bytes 983048 | tf_op jit(solution)/shard_map/ppermute | solution.py:443
  34.8 29.9 %collective-permute-start.9 = (bf16[640,896]{1,0:T(8,128)(2,1)S(1)}, bf16[640,896]{1,0:T(8,128)(2,1)}, u32[]{:S(2)}, u32[]{:S(2)}) collective-permute-start(bf16[640,896]{1,0:T(8,128)(2,1)S(1)} %give_columns.3.after_ref), channel_id=1, source_target_pairs={{16,0},{17,1},{18,2},{19,3},{20,4},{21,5},{22,6},{23,7},{24,8},{25... | collective-permute-start | bytes 3440648 | tf_op jit(solution)/shard_map/ppermute | solution.py:419
  40.6 9.9 %collective-permute-start.4 = (bf16[2,64,1152]{2,1,0:T(8,128)(2,1)S(1)}, bf16[2,64,1152]{2,1,0:T(8,128)(2,1)S(1)}, u32[]{:S(2)}, u32[]{:S(2)}) collective-permute-start(bf16[2,64,1152]{2,1,0:T(8,128)(2,1)S(1)} %get-tuple-element.38), channel_id=1, source_target_pairs={{0,2},{2,0},{4,6},{6,4},{8,10},{10,8},{12,14},{14,12},{1,3},{3,1},... | collective-permute-start | bytes 884744 | tf_op jit(solution)/shard_map/ppermute | solution.py:438
  43.6 12.7 %collective-permute-start.5 = (bf16[2,64,1152]{2,1,0:T(8,128)(2,1)S(1)}, bf16[2,64,1152]{2,1,0:T(8,128)(2,1)S(1)}, u32[]{:S(2)}, u32[]{:S(2)}) collective-permute-start(bf16[2,64,1152]{2,1,0:T(8,128)(2,1)S(1)} %get-tuple-element.40), channel_id=1, source_target_pairs={{0,2},{2,0},{4,6},{6,4},{8,10},{10,8},{12,14},{14,12},{1,3},{3,1},... | collective-permute-start | bytes 884744 | tf_op jit(solution)/shard_map/ppermute | solution.py:438
  57.1 10.8 %collective-permute-start.6 = (bf16[64,1152]{1,0:T(8,128)(2,1)}, bf16[64,1152]{1,0:T(8,128)(2,1)S(1)}, u32[]{:S(2)}, u32[]{:S(2)}) collective-permute-start(bf16[64,1152]{1,0:T(8,128)(2,1)} %get-tuple-element.43), channel_id=1, source_target_pairs={{0,4},{2,6},{4,0},{6,2},{8,12},{10,14},{12,8},{14,10},{1,5},{3,7},... | collective-permute-start | bytes 442376 | tf_op jit(solution)/shard_map/ppermute | solution.py:434
  58.0 14.3 %collective-permute-start.7 = (bf16[64,1152]{1,0:T(8,128)(2,1)}, bf16[64,1152]{1,0:T(8,128)(2,1)}, u32[]{:S(2)}, u32[]{:S(2)}) collective-permute-start(bf16[64,1152]{1,0:T(8,128)(2,1)} %get-tuple-element.44), channel_id=1, source_target_pairs={{0,8},{2,10},{4,12},{6,14},{8,0},{10,2},{12,4},{14,6},{1,9},{3,11}... | collective-permute-start | bytes 442376 | tf_op jit(solution)/shard_map/ppermute | solution.py:434
  60.6 11.7 %collective-permute-start.8 = (bf16[64,1152]{1,0:T(8,128)(2,1)}, bf16[64,1152]{1,0:T(8,128)(2,1)}, u32[]{:S(2)}, u32[]{:S(2)}) collective-permute-start(bf16[64,1152]{1,0:T(8,128)(2,1)} %fusion.17), channel_id=1, source_target_pairs={{0,12},{2,14},{4,8},{6,10},{8,4},{10,6},{12,0},{14,2},{1,13},{3,15... | collective-permute-start | bytes 442376 | tf_op jit(solution)/shard_map/ppermute | solution.py:434
  61.6 11.9 %collective-permute-start = (bf16[80,2048]{1,0:T(8,128)(2,1)}, bf16[80,2048]{1,0:T(8,128)(2,1)S(1)}, u32[]{:S(2)}, u32[]{:S(2)}) collective-permute-start(bf16[80,2048]{1,0:T(8,128)(2,1)} %copy-done.5), channel_id=1, source_target_pairs={{16,0},{17,1},{18,2},{19,3},{20,4},{21,5},{22,6},{23,7},{24,8},{25... | collective-permute-start | bytes 983048 | tf_op jit(solution)/shard_map/ppermute | solution.py:419
  66.9 8.6 %collective-permute-start.10 = (bf16[2,64,896]{2,1,0:T(8,128)(2,1)S(1)}, bf16[2,64,896]{2,1,0:T(8,128)(2,1)S(1)}, u32[]{:S(2)}, u32[]{:S(2)}) collective-permute-start(bf16[2,64,896]{2,1,0:T(8,128)(2,1)S(1)} %get-tuple-element.49), channel_id=1, source_target_pairs={{0,2},{2,0},{4,6},{6,4},{8,10},{10,8},{12,14},{14,12},{1,3},{3,1},... | collective-permute-start | bytes 688136 | tf_op jit(solution)/shard_map/ppermute | solution.py:438
  67.9 11.4 %collective-permute-start.11 = (bf16[2,64,896]{2,1,0:T(8,128)(2,1)S(1)}, bf16[2,64,896]{2,1,0:T(8,128)(2,1)S(1)}, u32[]{:S(2)}, u32[]{:S(2)}) collective-permute-start(bf16[2,64,896]{2,1,0:T(8,128)(2,1)S(1)} %get-tuple-element.51), channel_id=1, source_target_pairs={{0,2},{2,0},{4,6},{6,4},{8,10},{10,8},{12,14},{14,12},{1,3},{3,1},... | collective-permute-start | bytes 688136 | tf_op jit(solution)/shard_map/ppermute | solution.py:438
  75.5 7.6 %collective-permute-start.14 = (bf16[64,896]{1,0:T(8,128)(2,1)S(1)}, bf16[64,896]{1,0:T(8,128)(2,1)S(1)}, u32[]{:S(2)}, u32[]{:S(2)}) collective-permute-start(bf16[64,896]{1,0:T(8,128)(2,1)S(1)} %fusion.23), channel_id=1, source_target_pairs={{0,12},{2,14},{4,8},{6,10},{8,4},{10,6},{12,0},{14,2},{1,13},{3,15... | collective-permute-start | bytes 344072 | tf_op jit(solution)/shard_map/ppermute | solution.py:434
  79.3 7.8 %collective-permute-start.12 = (bf16[64,896]{1,0:T(8,128)(2,1)S(1)}, bf16[64,896]{1,0:T(8,128)(2,1)S(1)}, u32[]{:S(2)}, u32[]{:S(2)}) collective-permute-start(bf16[64,896]{1,0:T(8,128)(2,1)S(1)} %get-tuple-element.74), channel_id=1, source_target_pairs={{0,4},{2,6},{4,0},{6,2},{8,12},{10,14},{12,8},{14,10},{1,5},{3,7},... | collective-permute-start | bytes 344072 | tf_op jit(solution)/shard_map/ppermute | solution.py:434
  80.3 6.7 %collective-permute-start.13 = (bf16[64,896]{1,0:T(8,128)(2,1)S(1)}, bf16[64,896]{1,0:T(8,128)(2,1)S(1)}, u32[]{:S(2)}, u32[]{:S(2)}) collective-permute-start(bf16[64,896]{1,0:T(8,128)(2,1)S(1)} %get-tuple-element.75), channel_id=1, source_target_pairs={{0,8},{2,10},{4,12},{6,14},{8,0},{10,2},{12,4},{14,6},{1,9},{3,11}... | collective-permute-start | bytes 344072 | tf_op jit(solution)/shard_map/ppermute | solution.py:434
  97.1 5.4 %collective-permute-start.18 = (bf16[64,896]{1,0:T(8,128)(2,1)S(1)}, bf16[64,896]{1,0:T(8,128)(2,1)S(1)}, u32[]{:S(2)}, u32[]{:S(2)}) collective-permute-start(bf16[64,896]{1,0:T(8,128)(2,1)S(1)} %subtract_convert_fusion.1), channel_id=1, source_target_pairs={{0,2},{2,0},{4,6},{6,4},{8,10},{10,8},{12,14},{14,12},{1,3},{3,1},... | collective-permute-start | bytes 344072 | tf_op jit(solution)/shard_map/ppermute | solution.py:438
  98.0 8.7 %collective-permute-start.17 = (bf16[64,1152]{1,0:T(8,128)(2,1)S(1)}, bf16[64,1152]{1,0:T(8,128)(2,1)S(1)}, u32[]{:S(2)}, u32[]{:S(2)}) collective-permute-start(bf16[64,1152]{1,0:T(8,128)(2,1)S(1)} %subtract_convert_fusion), channel_id=1, source_target_pairs={{0,12},{2,14},{4,8},{6,10},{8,4},{10,6},{12,0},{14,2},{1,13},{3,15... | collective-permute-start | bytes 442376 | tf_op jit(solution)/shard_map/ppermute | solution.py:434
  99.9 11.7 %collective-permute-start.16 = (bf16[64,1152]{1,0:T(8,128)(2,1)S(1)}, bf16[64,1152]{1,0:T(8,128)(2,1)S(1)}, u32[]{:S(2)}, u32[]{:S(2)}) collective-permute-start(bf16[64,1152]{1,0:T(8,128)(2,1)S(1)} %subtract_convert_fusion), channel_id=1, source_target_pairs={{0,8},{2,10},{4,12},{6,14},{8,0},{10,2},{12,4},{14,6},{1,9},{3,11}... | collective-permute-start | bytes 442376 | tf_op jit(solution)/shard_map/ppermute | solution.py:434
  99.9 11.7 %collective-permute-start.15 = (bf16[64,1152]{1,0:T(8,128)(2,1)S(1)}, bf16[64,1152]{1,0:T(8,128)(2,1)S(1)}, u32[]{:S(2)}, u32[]{:S(2)}) collective-permute-start(bf16[64,1152]{1,0:T(8,128)(2,1)S(1)} %subtract_convert_fusion), channel_id=1, source_target_pairs={{0,4},{2,6},{4,0},{6,2},{8,12},{10,14},{12,8},{14,10},{1,5},{3,7},... | collective-permute-start | bytes 442376 | tf_op jit(solution)/shard_map/ppermute | solution.py:434
  111.8 10.4 %collective-permute-start.21 = (bf16[2,64,896]{2,1,0:T(8,128)(2,1)S(1)}, bf16[2,64,896]{2,1,0:T(8,128)(2,1)S(1)}, u32[]{:S(2)}, u32[]{:S(2)}) collective-permute-start(bf16[2,64,896]{2,1,0:T(8,128)(2,1)S(1)} %pad_maximum_fusion.5), channel_id=1, source_target_pairs={{0,12},{2,14},{4,8},{6,10},{8,4},{10,6},{12,0},{14,2},{1,13},{3,15... | collective-permute-start | bytes 688136 | tf_op jit(solution)/shard_map/ppermute | solution.py:434
  114.1 18.8 %collective-permute-start.20 = (bf16[2,64,896]{2,1,0:T(8,128)(2,1)S(1)}, bf16[2,64,896]{2,1,0:T(8,128)(2,1)S(1)}, u32[]{:S(2)}, u32[]{:S(2)}) collective-permute-start(bf16[2,64,896]{2,1,0:T(8,128)(2,1)S(1)} %pad_maximum_fusion.5), channel_id=1, source_target_pairs={{0,8},{2,10},{4,12},{6,14},{8,0},{10,2},{12,4},{14,6},{1,9},{3,11}... | collective-permute-start | bytes 688136 | tf_op jit(solution)/shard_map/ppermute | solution.py:434
  114.1 18.8 %collective-permute-start.19 = (bf16[2,64,896]{2,1,0:T(8,128)(2,1)S(1)}, bf16[2,64,896]{2,1,0:T(8,128)(2,1)S(1)}, u32[]{:S(2)}, u32[]{:S(2)}) collective-permute-start(bf16[2,64,896]{2,1,0:T(8,128)(2,1)S(1)} %pad_maximum_fusion.5), channel_id=1, source_target_pairs={{0,4},{2,6},{4,0},{6,2},{8,12},{10,14},{12,8},{14,10},{1,5},{3,7},... | collective-permute-start | bytes 688136 | tf_op jit(solution)/shard_map/ppermute | solution.py:434
  116.2 18.8 %collective-permute-start.22 = (bf16[4,64,1152]{2,1,0:T(8,128)(2,1)S(1)}, bf16[4,64,1152]{2,1,0:T(8,128)(2,1)S(1)}, u32[]{:S(2)}, u32[]{:S(2)}) collective-permute-start(bf16[4,64,1152]{2,1,0:T(8,128)(2,1)S(1)} %pad_maximum_fusion.3), channel_id=1, source_target_pairs={{0,2},{2,0},{4,6},{6,4},{8,10},{10,8},{12,14},{14,12},{1,3},{3,1},... | collective-permute-start | bytes 1769480 | tf_op jit(solution)/shard_map/ppermute | solution.py:438
  135.9 1.7 collective-permute-start.23
  137.7 8.9 %collective-permute-start.26 = (bf16[2,2,32,640]{3,2,1,0:T(8,128)(2,1)S(1)}, bf16[2,2,32,640]{3,2,1,0:T(8,128)(2,1)S(1)}, u32[]{:S(2)}, u32[]{:S(2)}) collective-permute-start(bf16[2,2,32,640]{3,2,1,0:T(8,128)(2,1)S(1)} %bitcast.144), channel_id=1, source_target_pairs={{16,0},{17,1},{18,2},{19,3},{20,4},{21,5},{22,6},{23,7},{24,8},{25... | collective-permute-start | bytes 491528 | tf_op jit(solution)/shard_map/ppermute | solution.py:419
  139.0 10.3 %collective-permute-start.24 = (bf16[2,2,32,640]{3,2,1,0:T(8,128)(2,1)S(1)}, bf16[2,2,32,640]{3,2,1,0:T(8,128)(2,1)S(1)}, u32[]{:S(2)}, u32[]{:S(2)}) collective-permute-start(bf16[2,2,32,640]{3,2,1,0:T(8,128)(2,1)S(1)} %bitcast.142), channel_id=1, source_target_pairs={{16,0},{17,1},{18,2},{19,3},{20,4},{21,5},{22,6},{23,7},{24,8},{25... | collective-permute-start | bytes 491528 | tf_op jit(solution)/shard_map/ppermute | solution.py:419
  146.7 15.6 %copy-start.3 = (f32[2,128,640]{2,1,0:T(8,128)S(1)}, f32[2,128,640]{2,1,0:T(8,128)}, u32[]{:S(2)}) copy-start(f32[2,128,640]{2,1,0:T(8,128)} %get-tuple-element.61.norm_ref) | copy-start | bytes 1966084
  146.7 15.6 %copy-start.1 = (f32[16,128,128]{2,1,0:T(8,128)S(1)}, f32[16,128,128]{2,1,0:T(8,128)}, u32[]{:S(2)}) copy-start(f32[16,128,128]{2,1,0:T(8,128)} %get-tuple-element.60.probs_ref) | copy-start | bytes 3145732
  146.8 5.6 %collective-permute-start.27 = (bf16[2,32,640]{2,1,0:T(8,128)(2,1)S(1)}, bf16[2,32,640]{2,1,0:T(8,128)(2,1)S(1)}, u32[]{:S(2)}, u32[]{:S(2)}) collective-permute-start(bf16[2,32,640]{2,1,0:T(8,128)(2,1)S(1)} %get-tuple-element.78), channel_id=1, source_target_pairs={{0,8},{2,10},{4,12},{6,14},{8,0},{10,2},{12,4},{14,6},{1,9},{3,11}... | collective-permute-start | bytes 245768 | tf_op jit(solution)/shard_map/ppermute | solution.py:434
  149.5 6.5 %collective-permute-start.28 = (bf16[2,32,640]{2,1,0:T(8,128)(2,1)S(1)}, bf16[2,32,640]{2,1,0:T(8,128)(2,1)S(1)}, u32[]{:S(2)}, u32[]{:S(2)}) collective-permute-start(bf16[2,32,640]{2,1,0:T(8,128)(2,1)S(1)} %get-tuple-element.79), channel_id=1, source_target_pairs={{0,12},{2,14},{4,8},{6,10},{8,4},{10,6},{12,0},{14,2},{1,13},{3,15... | collective-permute-start | bytes 245768 | tf_op jit(solution)/shard_map/ppermute | solution.py:434
  151.0 5.3 %collective-permute-start.25 = (bf16[2,32,640]{2,1,0:T(8,128)(2,1)S(1)}, bf16[2,32,640]{2,1,0:T(8,128)(2,1)S(1)}, u32[]{:S(2)}, u32[]{:S(2)}) collective-permute-start(bf16[2,32,640]{2,1,0:T(8,128)(2,1)S(1)} %slice_bitcast_fusion.17), channel_id=1, source_target_pairs={{0,4},{2,6},{4,0},{6,2},{8,12},{10,14},{12,8},{14,10},{1,5},{3,7},... | collective-permute-start | bytes 245768 | tf_op jit(solution)/shard_map/ppermute | solution.py:434
  156.4 5.4 %collective-permute-start.29 = (bf16[4,32,640]{2,1,0:T(8,128)(2,1)S(1)}, bf16[4,32,640]{2,1,0:T(8,128)(2,1)S(1)}, u32[]{:S(2)}, u32[]{:S(2)}) collective-permute-start(bf16[4,32,640]{2,1,0:T(8,128)(2,1)S(1)} %pad_maximum_fusion.7), channel_id=1, source_target_pairs={{0,2},{2,0},{4,6},{6,4},{8,10},{10,8},{12,14},{14,12},{1,3},{3,1},... | collective-permute-start | bytes 491528 | tf_op jit(solution)/shard_map/ppermute | solution.py:438
  (12 other events, 74.6 us)
